TPU v7x, 512 devices: a whole 4x8x8 slice. The times are simulated.
512 devices in a mesh: prefix: 16 (over z, core), resp: 32 (over y, x).
Axes of the slice: x: 4, y: 8, z: 8, core: 2. Of those that a mesh axis runs over, the one named last changes fastest.
Arguments:
- prompt_kv: bfloat16 [2, 512, 512], P(None, 'prefix'), may hold values from -6 to 6
- response_queries: bfloat16 [1024, 128, 1792], P(('prefix', 'resp')), may hold values from -300 to 300
- resp_kv: bfloat16 [1024, 128, 512], P(('prefix', 'resp')), may hold values from -6 to 6
- readout: bfloat16 [1024, 128, 1792], P(('prefix', 'resp')), may hold values from -3 to 3
- slot_response: int32 [1024], P(('prefix', 'resp')), may hold values from 0 to 1023, each once
- lengths: int32 [1024], replicated, may hold values from 32 to 128
- pair_prompt: int32 [512], replicated, may hold values from 0 to 1
- ref_margin: float32 [512], replicated, may hold values from -60 to 60
Outputs:
- margins: float32 [512], replicated
- grad_q: bfloat16 [1024, 128, 1792], P(('prefix', 'resp'))
- grad_resp_kv: bfloat16 [1024, 128, 512], P(('prefix', 'resp'))
- grad_prompt_kv: bfloat16 [2, 512, 512], P(None, 'prefix')
Inputs may be any that keep to these rules, and one draw needn't show every extreme that they name: `slot_response`: each response appears in exactly one slot; response 2 k is the chosen and 2 k + 1 the rejected response of pair k.
All inputs are finite; a program needn't handle non-finite values.
Results may differ from a plain program's by a relative error of at most 0.015.
Values may be sent and summed in bfloat16 or wider, within the bound.
No kernel may reach another device: no remote copies, remote signals or barrier semaphores. Data moves between devices by JAX's collectives and lax.ppermute only.
A program may use at most 64 MiB of HBM per device.

v0:
```python
import jax
import jax.numpy as jnp
from jax import lax
from jax.sharding import Mesh
from jax.sharding import PartitionSpec as P

QUERY_HEADS = 14
KEY_VALUE_HEADS = 2
HEAD_SIZE = 128
PREFIX = ("prefix_0", "prefix_1")
PREFIX_RESP = ("prefix_0", "prefix_1", "resp_0", "resp_1")
RESP = ("resp_0", "resp_1")


margin_beta = 0.1
loss_scale = 256.0


def in_order(pieces, dim):
    dims = list(pieces.shape[1:])
    dims[dim] *= pieces.shape[0]
    return jnp.moveaxis(pieces, 0, dim).reshape(dims)


def copy_for_each(shard, axis):
    size = lax.axis_size(axis)
    return lax.all_to_all(
        jnp.broadcast_to(shard[None], (size, *shard.shape)), axis, 0, 0, tiled=True
    )


def gather_directly(shard, axis, dim):
    return in_order(copy_for_each(shard, axis), dim)


def taken_together(shard, axis):
    everything = copy_for_each(shard, axis)
    return jnp.sum(everything, axis=0)


def over_axes(shard, axes):
    far, near = axes
    return taken_together(taken_together(shard, near), far)


def split_up(shard, dim, size):
    dims = shard.shape
    pieces = shard.reshape(*dims[:dim], size, dims[dim] // size, *dims[dim + 1 :])
    return jnp.moveaxis(pieces, dim, 0)


def summed_on_arrival(shard, axis, dim):
    size = lax.axis_size(axis)
    pieces = lax.all_to_all(split_up(shard, dim, size), axis, 0, 0, tiled=True)
    return jnp.sum(pieces.astype(jnp.float32), axis=0)


def sum_in_two_steps(shard, axes, dim):
    far, near = axes
    own = summed_on_arrival(split_up(shard, dim, lax.axis_size(far)), near, dim + 1)
    return jnp.sum(
        lax.all_to_all(own.astype(jnp.bfloat16), far, 0, 0, tiled=True).astype(jnp.float32), axis=0
    )


def unpack(packed_rows):
    row_block = packed_rows.shape[0]
    head_width = packed_rows.shape[1] // 2
    key_rows = packed_rows[:, :head_width].reshape(row_block, KEY_VALUE_HEADS, HEAD_SIZE)
    value_rows = packed_rows[:, head_width:].reshape(row_block, KEY_VALUE_HEADS, HEAD_SIZE)
    return (key_rows, value_rows)


def forward_pieces(query_rows, prompt_packed, own_packed, causal):
    prompt_keys, prompt_values = unpack(prompt_packed)
    own_keys, own_values = unpack(own_packed)
    scale_factor = HEAD_SIZE ** (-0.5)
    prompt_scores = (
        jnp.einsum("tgjd,kgd->gjtk", query_rows, prompt_keys, preferred_element_type=jnp.float32)
        * scale_factor
    )
    own_scores = (
        jnp.einsum("tgjd,kgd->gjtk", query_rows, own_keys, preferred_element_type=jnp.float32)
        * scale_factor
    )
    own_scores = jnp.where(causal, own_scores, -jnp.inf)
    row_max = jnp.maximum(
        jnp.max(prompt_scores, -1, keepdims=True), jnp.max(own_scores, -1, keepdims=True)
    )
    prompt_exp = jnp.exp(prompt_scores - row_max)
    own_exp = jnp.exp(own_scores - row_max)
    total = jnp.sum(prompt_exp, -1, keepdims=True) + jnp.sum(own_exp, -1, keepdims=True)
    prefix_probabilities = (prompt_exp / total).astype(jnp.bfloat16)
    self_probabilities = (own_exp / total).astype(jnp.bfloat16)
    attended = jnp.einsum(
        "gjtk,kgd->tgjd", prefix_probabilities, prompt_values, preferred_element_type=jnp.float32
    )
    attended = attended + jnp.einsum(
        "gjtk,kgd->tgjd", self_probabilities, own_values, preferred_element_type=jnp.float32
    )
    return (
        prompt_keys,
        prompt_values,
        own_keys,
        own_values,
        prefix_probabilities,
        self_probabilities,
        attended,
    )


def on_device(
    prompt_kv, response_queries, resp_kv, readout, slot_response, lengths, pair_prompt, ref_margin
):
    prompts = prompt_kv.shape[0]
    slots, slot_capacity, query_width = response_queries.shape
    query_groups = QUERY_HEADS // KEY_VALUE_HEADS
    pairs = ref_margin.shape[0]
    scale_factor = HEAD_SIZE ** (-0.5)
    full_kv = gather_directly(prompt_kv, PREFIX, 1)
    prefix_length = full_kv.shape[1]
    positions = jnp.arange(slot_capacity)
    causal = positions[None, :] <= positions[:, None]
    pair_ids = jnp.arange(pairs)
    prompt_ids = jnp.arange(prompts)
    contrib = jnp.zeros((pairs,), jnp.float32)
    saved = []
    for position_index in range(slots):
        response = slot_response[position_index]
        pair_index = response // 2
        sign = 1.0 - 2.0 * (response % 2).astype(jnp.float32)
        valid = (positions < lengths[response]).astype(jnp.float32)
        prompt_index = pair_prompt[pair_index]
        prompt_packed = lax.dynamic_index_in_dim(full_kv, prompt_index, 0, keepdims=False)
        query_rows = response_queries[position_index].reshape(
            slot_capacity, KEY_VALUE_HEADS, query_groups, HEAD_SIZE
        )
        output_rows = readout[position_index].reshape(
            slot_capacity, KEY_VALUE_HEADS, query_groups, HEAD_SIZE
        )
        pieces = forward_pieces(query_rows, prompt_packed, resp_kv[position_index], causal)
        token_logp = jnp.sum(pieces[-1] * output_rows.astype(jnp.float32), axis=(1, 2, 3)) * valid
        contrib = contrib + jnp.where(pair_ids == pair_index, sign * jnp.sum(token_logp), 0.0)
        saved.append((pair_index, sign, valid, prompt_index, query_rows, output_rows, pieces))
    pair_sums = over_axes(contrib, ("prefix_0", ("prefix_1", "resp_0", "resp_1")))
    margins = margin_beta * (pair_sums - ref_margin)
    weights = -loss_scale * margin_beta * jax.nn.sigmoid(-margins)
    partial_value = jnp.zeros((prompts, prefix_length, full_kv.shape[2]), jnp.float32)
    grad_rows = []
    grad_own = []
    for pair_index, sign, valid, prompt_index, query_rows, output_rows, pieces in saved:
        (
            prompt_keys,
            prompt_values,
            own_keys,
            own_values,
            prefix_probabilities,
            self_probabilities,
            attended,
        ) = pieces
        coefficient = weights[pair_index] * sign
        output_gradient = (
            coefficient * output_rows.astype(jnp.float32) * valid[:, None, None, None]
        ).astype(jnp.bfloat16)
        prompt_dprobs = jnp.einsum(
            "tgjd,kgd->gjtk", output_gradient, prompt_values, preferred_element_type=jnp.float32
        )
        own_dprobs = jnp.einsum(
            "tgjd,kgd->gjtk", output_gradient, own_values, preferred_element_type=jnp.float32
        )
        delta = jnp.transpose(
            jnp.sum(output_gradient.astype(jnp.float32) * attended, -1), (1, 2, 0)
        )[..., None]
        prefix_score_gradient = (
            prefix_probabilities.astype(jnp.float32) * (prompt_dprobs - delta) * scale_factor
        ).astype(jnp.bfloat16)
        self_score_gradient = (
            self_probabilities.astype(jnp.float32) * (own_dprobs - delta) * scale_factor
        ).astype(jnp.bfloat16)
        grad_queries = jnp.einsum(
            "gjtk,kgd->tgjd", prefix_score_gradient, prompt_keys, preferred_element_type=jnp.float32
        )
        grad_queries = grad_queries + jnp.einsum(
            "gjtk,kgd->tgjd", self_score_gradient, own_keys, preferred_element_type=jnp.float32
        )
        prompt_grad = jnp.concatenate(
            [
                jnp.einsum(
                    "hybi,bhyu->ihu",
                    prefix_score_gradient,
                    query_rows,
                    preferred_element_type=jnp.float32,
                ).reshape(prefix_length, KEY_VALUE_HEADS * HEAD_SIZE),
                jnp.einsum(
                    "hybi,bhyu->ihu",
                    prefix_probabilities,
                    output_gradient,
                    preferred_element_type=jnp.float32,
                ).reshape(prefix_length, KEY_VALUE_HEADS * HEAD_SIZE),
            ],
            axis=-1,
        )
        own_grad = jnp.concatenate(
            [
                jnp.einsum(
                    "hybi,bhyu->ihu",
                    self_score_gradient,
                    query_rows,
                    preferred_element_type=jnp.float32,
                ).reshape(slot_capacity, KEY_VALUE_HEADS * HEAD_SIZE),
                jnp.einsum(
                    "hybi,bhyu->ihu",
                    self_probabilities,
                    output_gradient,
                    preferred_element_type=jnp.float32,
                ).reshape(slot_capacity, KEY_VALUE_HEADS * HEAD_SIZE),
            ],
            axis=-1,
        )
        selector = (prompt_ids == prompt_index)[:, None, None]
        partial_value = partial_value + jnp.where(selector, prompt_grad[None], 0.0)
        grad_rows.append(grad_queries.reshape(slot_capacity, query_width).astype(jnp.bfloat16))
        grad_own.append(own_grad.astype(jnp.bfloat16))
    spread = sum_in_two_steps(
        partial_value.astype(jnp.bfloat16), ("prefix_0", ("prefix_1", "resp_0", "resp_1")), 1
    )
    grad_prompt = gather_directly(spread.astype(jnp.bfloat16), RESP, 1)
    return (margins, jnp.stack(grad_rows), jnp.stack(grad_own), grad_prompt)


def solution(mesh):
    split = Mesh(mesh.devices.reshape(8, 2, 8, 4), ("prefix_0", "prefix_1", "resp_0", "resp_1"))
    in_specs = (
        P(None, PREFIX, None),
        P(PREFIX_RESP, None, None),
        P(PREFIX_RESP, None, None),
        P(PREFIX_RESP, None, None),
        P(PREFIX_RESP),
        P(),
        P(),
        P(),
    )
    out_specs = (P(), P(PREFIX_RESP, None, None), P(PREFIX_RESP, None, None), P(None, PREFIX, None))
    return jax.shard_map(
        on_device, mesh=split, in_specs=in_specs, out_specs=out_specs, check_vma=False
    )
```

profile of v0, /device:TPU:8, one launch (start us, length us, event | category | flops | bytes accessed | tf_op | source)
XLA Modules:
  0.0 200.2 jit_solution(9331851848621631917)
XLA Ops:
  2.6 10.4 %all-to-all-start = ((bf16[16,2,32,512]{3,2,1,0:T(8,128)(2,1)}), bf16[16,2,32,512]{3,2,1,0:T(8,128)(2,1)S(1)}, u32[]{:S(2)}, u32[]{:S(2)}) async-start(bf16[16,2,32,512]{3,2,1,0:T(8,128)(2,1)} %broadcast_in_dim.97), calls=%async_computation | async-start | bytes 2097152 | tf_op jit(solution)/shard_map/all_to_all | solution.py:27
  29.1 2.2 %slice_convert_fusion.1 = (f32[1,128,1792]{2,1,0:T(8,128)}, f32[1,128,1792]{2,1,0:T(8,128)S(1)}) fusion(bf16[2,128,1792]{2,1,0:T(8,128)(2,1)} %param.11), kind=kLoop, calls=%fused_computation.80 | loop fusion | flops 458752 | bytes 2752512 | tf_op jit(solution)/shard_map/convert_element_type | solution.py:142
  31.3 2.4 %copy.346 = f32[1,128,1792]{1,2,0:T(8,128)} copy(f32[1,128,1792]{2,1,0:T(8,128)} %get-tuple-element.28) | data formatting | bytes 1835008 | tf_op jit(solution)/shard_map/convert_element_type | solution.py:142
  54.1 2.7 %multiply_reduce_fusion.2 = (f32[128]{0:T(128)S(1)}, f32[128,2,7,128]{0,3,2,1:T(8,128)}) fusion(f32[128,2,7,128]{0,3,2,1:T(8,128)} %bitcast.293, f32[128,2,7,128]{0,3,2,1:T(8,128)S(1)} %convolution_bitcast_fusion.2, bf16[512,2,128,1]{0,2,3,1:T(8,128)(2,1)S(1)} %bitcast.298, bf16[2,7,128,512]{2,3,1,0:T(8,128)(2,1)S(1)} %divide_convert_fusion), kind=kOutput, calls=%fused_computation.69 | convolution fusion | flops 235569024 | bytes 4850176 | tf_op jit(solution)/shard_map/gjtk,kgd->tgjd/dot_general | solution.py:95
  59.6 3.2 %multiply_reduce_fusion.3 = (f32[128]{0:T(128)S(1)}, f32[128,2,7,128]{0,3,2,1:T(8,128)}) fusion(f32[128,2,7,128]{0,3,2,1:T(8,128)} %bitcast.295, f32[128,2,7,128]{0,3,2,1:T(8,128)S(1)} %convolution_bitcast_fusion.3, bf16[512,2,128,1]{0,2,3,1:T(8,128)(2,1)} %bitcast.300, bf16[2,7,128,512]{2,3,1,0:T(8,128)(2,1)} %divide_convert_fusion.1), kind=kOutput, calls=%fused_computation.72 | convolution fusion | flops 235569024 | bytes 4850176 | tf_op jit(solution)/shard_map/gjtk,kgd->tgjd/dot_general | solution.py:95
  65.4 10.9 %all-to-all-start.1 = ((f32[64,1,512]{2,1,0:T(1,128)}), f32[64,1,512]{2,1,0:T(1,128)S(1)}, u32[]{:S(2)}, u32[]{:S(2)}) async-start(f32[64,1,512]{2,1,0:T(1,128)} %broadcast_in_dim.103), calls=%async_computation.1 | async-start | bytes 262144 | tf_op jit(solution)/shard_map/all_to_all | solution.py:27
  78.2 8.0 %all-to-all-done.1 = f32[64,1,512]{2,1,0:T(1,128)S(1)} async-done(((f32[64,1,512]{2,1,0:T(1,128)}), f32[64,1,512]{2,1,0:T(1,128)S(1)}, u32[]{:S(2)}, u32[]{:S(2)}) %all-to-all-start.1) | async-done | bytes 131104 | tf_op jit(solution)/shard_map/all_to_all | solution.py:27
  86.9 6.8 %all-to-all-start.2 = ((f32[8,1,512]{2,1,0:T(1,128)}), f32[8,1,512]{2,1,0:T(1,128)S(1)}, u32[]{:S(2)}, u32[]{:S(2)}) async-start(f32[8,1,512]{2,1,0:T(1,128)} %broadcast_in_dim.104), calls=%async_computation.2 | async-start | bytes 32768 | tf_op jit(solution)/shard_map/all_to_all | solution.py:27
  94.9 6.6 %all-to-all-done.2 = f32[8,1,512]{2,1,0:T(1,128)S(1)} async-done(((f32[8,1,512]{2,1,0:T(1,128)}), f32[8,1,512]{2,1,0:T(1,128)S(1)}, u32[]{:S(2)}, u32[]{:S(2)}) %all-to-all-start.2) | async-done | bytes 16416 | tf_op jit(solution)/shard_map/all_to_all | solution.py:27
  105.2 3.0 %convolution_bitcast_fusion.12 = f32[512,2,128]{0,2,1:T(8,128)} fusion(bf16[128,2,7,128]{0,3,2,1:T(8,128)(2,1)S(1)} %get-tuple-element.21, bf16[2,7,128,512]{2,3,1,0:T(8,128)(2,1)} %divide_convert_fusion.1), kind=kOutput, calls=%fused_computation.51 | convolution fusion | flops 234881024 | bytes 2818048 | tf_op jit(solution)/shard_map/hybi,bhyu->ihu/dot_general | solution.py:194
  108.3 2.2 %fusion.25 = bf16[2,7,128,128]{2,3,1,0:T(8,128)(2,1)} fusion(bf16[128,2,7,128]{0,3,2,1:T(8,128)(2,1)S(1)} %get-tuple-element.21, bf16[128,2,128,1]{0,2,3,1:T(8,128)(2,1)} %bitcast.315, bf16[2,7,128,128]{2,3,1,0:T(8,128)(2,1)} %divide_convert_fusion.3, f32[2,7,128]{2,1,0:T(8,128)S(1)} %bitcast.325), kind=kOutput, calls=%fused_computation.46 | convolution fusion | flops 59867136 | bytes 1448960 | tf_op jit(solution)/shard_map/tgjd,kgd->gjtk/dot_general | solution.py:168
  110.5 3.1 %fusion.5 = bf16[2,7,128,512]{2,3,1,0:T(8,128)(2,1)} fusion(bf16[2,7,128,512]{2,3,1,0:T(8,128)(2,1)S(1)} %copy-done, bf16[512,2,128,1]{0,2,3,1:T(8,128)(2,1)} %bitcast.301, bf16[128,2,7,128]{0,3,2,1:T(8,128)(2,1)S(1)} %get-tuple-element.21, f32[2,7,128]{2,1,0:T(8,128)S(1)} %bitcast.326), kind=kOutput, calls=%fused_computation.7 | convolution fusion | flops 239468544 | bytes 4398080 | tf_op jit(solution)/shard_map/tgjd,kgd->gjtk/dot_general | solution.py:165
  114.2 2.1 %convolution_bitcast_fusion.13 = f32[512,2,128]{2,0,1:T(8,128)S(1)} fusion(bf16[2,7,128,512]{2,3,1,0:T(8,128)(2,1)} %fusion.5, bf16[128,2,7,128]{0,3,2,1:T(8,128)(2,1)S(1)} %bitcast.291), kind=kOutput, calls=%fused_computation.52 | convolution fusion | flops 234881024 | bytes 2818048 | tf_op jit(solution)/shard_map/hybi,bhyu->ihu/dot_general | solution.py:188
  117.5 2.3 %concatenate.52 = f32[8,64,256]{2,1,0:T(8,128)} reshape(f32[512,2,128]{2,1,0:T(2,128)} %copy.385) | data formatting | bytes 1048576 | tf_op jit(solution)/shard_map/concatenate | solution.py:186
  121.8 2.3 %concatenate.53 = f32[8,64,256]{2,1,0:T(8,128)} reshape(f32[512,2,128]{2,1,0:T(2,128)} %copy.387) | data formatting | bytes 1048576 | tf_op jit(solution)/shard_map/concatenate | solution.py:186
  134.6 2.8 %fusion.32 = bf16[64,8,2,1,512]{4,1,3,2,0:T(8,128)(2,1)} fusion(f32[8,64,512]{2,0,1:T(8,128)S(1)} %copy.393, f32[8,64,512]{2,0,1:T(8,128)} %copy.388, pred[2]{0:T(512)(128)(4,1)S(1)} %get-tuple-element.64, pred[2]{0:T(512)(128)(4,1)S(1)} %get-tuple-element.65), kind=kLoop, calls=%fused_computation.61 | loop fusion | flops 2097152 | bytes 3145732 | tf_op jit(solution)/shard_map/transpose | solution.py:49
  137.4 5.4 %all-to-all-start.3 = ((bf16[64,8,2,1,512]{4,1,3,2,0:T(8,128)(2,1)}), bf16[64,8,2,1,512]{4,1,3,2,0:T(8,128)(2,1)}, u32[]{:S(2)}, u32[]{:S(2)}) async-start(bf16[64,8,2,1,512]{4,1,3,2,0:T(8,128)(2,1)} %fusion.32), calls=%async_computation.3 | async-start | bytes 2097152 | tf_op jit(solution)/shard_map/all_to_all | solution.py:54
  144.2 2.2 %fusion.26 = bf16[128,2,7,128]{0,3,2,1:T(8,128)(2,1)} fusion(f32[128,2,7,128]{0,3,2,1:T(8,128)S(1)} %convolution_bitcast_fusion.1, bf16[512,2,128,1]{0,2,3,1:T(8,128)(2,1)} %bitcast.305, bf16[2,7,128,512]{2,3,1,0:T(8,128)(2,1)S(1)} %copy-done.1), kind=kOutput, calls=%fused_computation.47 | convolution fusion | flops 235339776 | bytes 3473408 | tf_op jit(solution)/shard_map/gjtk,kgd->tgjd/dot_general | solution.py:180
  146.4 2.1 %copy.374 = bf16[1,128,1792]{2,1,0:T(8,128)(2,1)} copy(bf16[1,128,1792]{1,2,0:T(8,128)(2,1)} %bitcast.306) | data formatting | bytes 917504 | tf_op jit(solution)/shard_map/convert_element_type | solution.py:222
  158.4 12.3 %all-to-all-done.3 = bf16[64,8,2,1,512]{4,1,3,2,0:T(8,128)(2,1)} async-done(((bf16[64,8,2,1,512]{4,1,3,2,0:T(8,128)(2,1)}), bf16[64,8,2,1,512]{4,1,3,2,0:T(8,128)(2,1)}, u32[]{:S(2)}, u32[]{:S(2)}) %all-to-all-start.3) | async-done | bytes 1048608 | tf_op jit(solution)/shard_map/all_to_all | solution.py:54
  172.7 3.3 %all-to-all-start.4 = ((bf16[8,2,1,512]{3,1,2,0:T(2,128)(2,1)}), bf16[8,2,1,512]{3,1,2,0:T(2,128)(2,1)S(1)}, u32[]{:S(2)}, u32[]{:S(2)}) async-start(bf16[8,2,1,512]{3,1,2,0:T(2,128)(2,1)} %copy.394), calls=%async_computation.4 | async-start | bytes 32768 | tf_op jit(solution)/shard_map/all_to_all | solution.py:62
  176.4 7.4 %all-to-all-done.4 = bf16[8,2,1,512]{3,1,2,0:T(2,128)(2,1)S(1)} async-done(((bf16[8,2,1,512]{3,1,2,0:T(2,128)(2,1)}), bf16[8,2,1,512]{3,1,2,0:T(2,128)(2,1)S(1)}, u32[]{:S(2)}, u32[]{:S(2)}) %all-to-all-start.4) | async-done | bytes 16416 | tf_op jit(solution)/shard_map/all_to_all | solution.py:62
  184.5 6.0 %all-to-all-start.5 = ((bf16[32,2,1,512]{3,1,2,0:T(2,128)(2,1)}), bf16[32,2,1,512]{3,1,2,0:T(2,128)(2,1)S(1)}, u32[]{:S(2)}, u32[]{:S(2)}) async-start(bf16[32,2,1,512]{3,1,2,0:T(2,128)(2,1)} %broadcast_in_dim.110), calls=%async_computation.5 | async-start | bytes 131072 | tf_op jit(solution)/shard_map/all_to_all | solution.py:27
  192.0 7.5 %all-to-all-done.5 = bf16[32,2,1,512]{3,1,2,0:T(2,128)(2,1)S(1)} async-done(((bf16[32,2,1,512]{3,1,2,0:T(2,128)(2,1)}), bf16[32,2,1,512]{3,1,2,0:T(2,128)(2,1)S(1)}, u32[]{:S(2)}, u32[]{:S(2)}) %all-to-all-start.5) | async-done | bytes 65568 | tf_op jit(solution)/shard_map/all_to_all | solution.py:27
  (135 shorter events, 67.4 us)
Async XLA Ops:
  2.6 38.0 %all-to-all-start = ((bf16[16,2,32,512]{3,2,1,0:T(8,128)(2,1)}), bf16[16,2,32,512]{3,2,1,0:T(8,128)(2,1)S(1)}, u32[]{:S(2)}, u32[]{:S(2)}) async-start(bf16[16,2,32,512]{3,2,1,0:T(8,128)(2,1)} %broadcast_in_dim.97), calls=%async_computation | async-start | bytes 2097152 | tf_op jit(solution)/shard_map/all_to_all | solution.py:27
  38.3 2.5 %copy-start.21 = (bf16[128,256]{0,1:T(8,128)(2,1)}, bf16[128,256]{0,1:T(8,128)(2,1)S(1)}, u32[]{:S(2)}) copy-start(bf16[128,256]{0,1:T(8,128)(2,1)S(1)} %get-tuple-element.38) | copy-start | bytes 196612
  39.3 3.3 %copy-start.8 = (f32[2,7,128,128]{2,3,1,0:T(8,128)}, f32[2,7,128,128]{2,3,1,0:T(8,128)S(1)}, u32[]{:S(2)}) copy-start(f32[2,7,128,128]{2,3,1,0:T(8,128)S(1)} %get-tuple-element.53) | copy-start | bytes 2752516
  44.7 8.2 %copy-start.10 = (bf16[2,7,128,128]{2,3,1,0:T(8,128)(2,1)}, bf16[2,7,128,128]{2,3,1,0:T(8,128)(2,1)S(1)}, u32[]{:S(2)}) copy-start(bf16[2,7,128,128]{2,3,1,0:T(8,128)(2,1)S(1)} %divide_convert_fusion.2) | copy-start | bytes 1376260
  46.0 2.1 %copy-start.18 = (bf16[512,256]{0,1:T(8,128)(2,1)}, bf16[512,256]{0,1:T(8,128)(2,1)S(1)}, u32[]{:S(2)}) copy-start(bf16[512,256]{0,1:T(8,128)(2,1)S(1)} %copy.337) | copy-start | bytes 786436
  48.1 2.9 %copy-start.20 = (bf16[512,256]{1,0:T(8,128)(2,1)S(1)}, bf16[512,256]{1,0:T(8,128)(2,1)}, u32[]{:S(2)}) copy-start(bf16[512,256]{1,0:T(8,128)(2,1)} %get-tuple-element.32) | copy-start | bytes 786436
  54.1 4.4 %copy-start.12 = (bf16[2,7,128,128]{2,3,1,0:T(8,128)(2,1)S(1)}, bf16[2,7,128,128]{2,3,1,0:T(8,128)(2,1)}, u32[]{:S(2)}) copy-start(bf16[2,7,128,128]{2,3,1,0:T(8,128)(2,1)} %divide_convert_fusion.3) | copy-start | bytes 1376260
  56.7 44.8 %copy-start.23 = (f32[512]{0:T(512)S(1)}, f32[512]{0:T(512)}, u32[]{:S(2)}) copy-start(f32[512]{0:T(512)} %param.15) | copy-start | bytes 6148
  65.4 20.8 %all-to-all-start.1 = ((f32[64,1,512]{2,1,0:T(1,128)}), f32[64,1,512]{2,1,0:T(1,128)S(1)}, u32[]{:S(2)}, u32[]{:S(2)}) async-start(f32[64,1,512]{2,1,0:T(1,128)} %broadcast_in_dim.103), calls=%async_computation.1 | async-start | bytes 262144 | tf_op jit(solution)/shard_map/all_to_all | solution.py:27
  86.9 14.6 %all-to-all-start.2 = ((f32[8,1,512]{2,1,0:T(1,128)}), f32[8,1,512]{2,1,0:T(1,128)S(1)}, u32[]{:S(2)}, u32[]{:S(2)}) async-start(f32[8,1,512]{2,1,0:T(1,128)} %broadcast_in_dim.104), calls=%async_computation.2 | async-start | bytes 32768 | tf_op jit(solution)/shard_map/all_to_all | solution.py:27
  103.5 7.0 %copy-start = (bf16[2,7,128,512]{2,3,1,0:T(8,128)(2,1)S(1)}, bf16[2,7,128,512]{2,3,1,0:T(8,128)(2,1)}, u32[]{:S(2)}) copy-start(bf16[2,7,128,512]{2,3,1,0:T(8,128)(2,1)} %divide_convert_fusion.1) | copy-start | bytes 5505028
  124.1 3.1 %copy-start.6 = (f32[1,128,1792]{1,2,0:T(8,128)S(1)}, f32[1,128,1792]{1,2,0:T(8,128)}, u32[]{:S(2)}) copy-start(f32[1,128,1792]{1,2,0:T(8,128)} %copy.357) | copy-start | bytes 2752516
  124.1 3.1 %copy-start.15 = (f32[128,2,7,128]{0,3,2,1:T(8,128)S(1)}, f32[128,2,7,128]{0,3,2,1:T(8,128)}, u32[]{:S(2)}) copy-start(f32[128,2,7,128]{0,3,2,1:T(8,128)} %get-tuple-element.55) | copy-start | bytes 2752516
  128.1 4.3 %copy-start.4 = (bf16[128,2,7,128]{0,3,2,1:T(8,128)(2,1)}, bf16[128,2,7,128]{0,3,2,1:T(8,128)(2,1)S(1)}, u32[]{:S(2)}) copy-start(bf16[128,2,7,128]{0,3,2,1:T(8,128)(2,1)S(1)} %get-tuple-element.23) | copy-start | bytes 1376260
  134.0 8.9 %copy-start.22 = (bf16[128,256]{0,1:T(8,128)(2,1)S(1)}, bf16[128,256]{0,1:T(8,128)(2,1)}, u32[]{:S(2)}) copy-start(bf16[128,256]{0,1:T(8,128)(2,1)} %copy-done.21) | copy-start | bytes 196612
  134.6 9.6 %copy-start.1 = (bf16[2,7,128,512]{2,3,1,0:T(8,128)(2,1)S(1)}, bf16[2,7,128,512]{2,3,1,0:T(8,128)(2,1)}, u32[]{:S(2)}) copy-start(bf16[2,7,128,512]{2,3,1,0:T(8,128)(2,1)} %fusion.5) | copy-start | bytes 5505028
  137.4 33.3 %all-to-all-start.3 = ((bf16[64,8,2,1,512]{4,1,3,2,0:T(8,128)(2,1)}), bf16[64,8,2,1,512]{4,1,3,2,0:T(8,128)(2,1)}, u32[]{:S(2)}, u32[]{:S(2)}) async-start(bf16[64,8,2,1,512]{4,1,3,2,0:T(8,128)(2,1)} %fusion.32), calls=%async_computation.3 | async-start | bytes 2097152 | tf_op jit(solution)/shard_map/all_to_all | solution.py:54
  144.2 7.0 %copy-start.17 = (bf16[512,256]{0,1:T(8,128)(2,1)S(1)}, bf16[512,256]{0,1:T(8,128)(2,1)}, u32[]{:S(2)}) copy-start(bf16[512,256]{0,1:T(8,128)(2,1)} %copy-done.16) | copy-start | bytes 786436
  146.4 4.8 %copy-start.3 = (bf16[2,7,128,512]{2,3,1,0:T(8,128)(2,1)S(1)}, bf16[2,7,128,512]{2,3,1,0:T(8,128)(2,1)}, u32[]{:S(2)}) copy-start(bf16[2,7,128,512]{2,3,1,0:T(8,128)(2,1)} %copy-done.2) | copy-start | bytes 5505028
  152.4 23.7 %copy-start.5 = (bf16[128,2,7,128]{0,3,2,1:T(8,128)(2,1)S(1)}, bf16[128,2,7,128]{0,3,2,1:T(8,128)(2,1)}, u32[]{:S(2)}) copy-start(bf16[128,2,7,128]{0,3,2,1:T(8,128)(2,1)} %copy-done.4) | copy-start | bytes 1376260
  152.4 23.7 %copy-start.11 = (bf16[2,7,128,128]{2,3,1,0:T(8,128)(2,1)S(1)}, bf16[2,7,128,128]{2,3,1,0:T(8,128)(2,1)}, u32[]{:S(2)}) copy-start(bf16[2,7,128,128]{2,3,1,0:T(8,128)(2,1)} %copy-done.10) | copy-start | bytes 1376260
  152.4 38.1 %copy-start.14 = (bf16[2,7,128,128]{2,3,1,0:T(8,128)(2,1)S(1)}, bf16[2,7,128,128]{2,3,1,0:T(8,128)(2,1)}, u32[]{:S(2)}) copy-start(bf16[2,7,128,128]{2,3,1,0:T(8,128)(2,1)} %copy-done.13) | copy-start | bytes 1376260
  172.7 11.0 %all-to-all-start.4 = ((bf16[8,2,1,512]{3,1,2,0:T(2,128)(2,1)}), bf16[8,2,1,512]{3,1,2,0:T(2,128)(2,1)S(1)}, u32[]{:S(2)}, u32[]{:S(2)}) async-start(bf16[8,2,1,512]{3,1,2,0:T(2,128)(2,1)} %copy.394), calls=%async_computation.4 | async-start | bytes 32768 | tf_op jit(solution)/shard_map/all_to_all | solution.py:62
  184.5 15.1 %all-to-all-start.5 = ((bf16[32,2,1,512]{3,1,2,0:T(2,128)(2,1)}), bf16[32,2,1,512]{3,1,2,0:T(2,128)(2,1)S(1)}, u32[]{:S(2)}, u32[]{:S(2)}) async-start(bf16[32,2,1,512]{3,1,2,0:T(2,128)(2,1)} %broadcast_in_dim.110), calls=%async_computation.5 | async-start | bytes 131072 | tf_op jit(solution)/shard_map/all_to_all | solution.py:27
  (6 other events, 7.5 us)
where the time goes:
time: 202 us; the launch traced here: 200 us
  starting transfers between devices  42.9 us (21%)
  waiting for transfers between devices  41.8 us (21%)
  local copies, waits for them, and re-layouts  40.6 us (20%)
  matrix products  34.3 us (17%)
  other arithmetic  25 us (12%)
  between operations  15.5 us (8%)
    all_to_all x4, starting transfers between devices, copy_for_each(): lax.all_to_all(jnp.broadcast_to(shard[None], (size, *shard.shape)), axis,...  34.1 us
    all_to_all x4, waiting for transfers between devices, copy_for_each(): lax.all_to_all(jnp.broadcast_to(shard[None], (size, *shard.shape)), axis,...  22.1 us
    all_to_all x1, waiting for transfers between devices, summed_on_arrival(): pieces = lax.all_to_all(split_up(shard, dim, size), axis, 0, 0, tiled=True)  12.3 us
    concatenate x6, local copies, waits for them, and re-layouts, on_device(): jnp.concatenate([jnp.einsum('hybi,bhyu->ihu', prefix_score_gradient, quer...  7.65 us
    all_to_all x1, waiting for transfers between devices, sum_in_two_steps(): lax.all_to_all(own.astype(jnp.bfloat16), far, 0, 0, tiled=True)  7.36 us
    dot_general x2, matrix products, forward_pieces(): jnp.einsum('gjtk,kgd->tgjd', prefix_probabilities, prompt_values, preferr...  5.86 us
    all_to_all x1, starting transfers between devices, summed_on_arrival(): pieces = lax.all_to_all(split_up(shard, dim, size), axis, 0, 0, tiled=True)  5.42 us
    dot_general x2, matrix products, on_device(): jnp.einsum('hybi,bhyu->ihu', prefix_probabilities, output_gradient, prefe...  4.54 us
  transfers between devices with their start and end apart: 6, of which 5 were waited for; matrix products, arithmetic and copies ran while one was open for 18% of the time, Pallas kernels for 0%

commit v1 on v0

v1 whole, which is shorter than its diff:
```python
import functools
import math

import jax
import jax.numpy as jnp
from jax import lax
from jax.experimental import pallas as pl
from jax.experimental.pallas import tpu as pltpu
from jax.sharding import Mesh
from jax.sharding import PartitionSpec as P

QUERY_HEADS = 14
KEY_VALUE_HEADS = 2
HEAD = 128
GROUP = QUERY_HEADS // KEY_VALUE_HEADS
TOKENS = 128
SCALE = HEAD**-0.5
LOG2_SCALE = SCALE * math.log2(math.e)
MARGIN_BETA = 0.1
LOSS_SCALE = 256.0
PREFIX = ("z", "c")
RESP = ("y", "x")
EVERY = ("z", "c", "y", "x")
SPREAD = ("z", "c", "y")
NT = (((1,), (1,)), ((), ()))
NN = (((1,), (0,)), ((), ()))
bf16 = jnp.bfloat16
f32 = jnp.float32


def attention_kernel(
    response_ref, lengths_ref, pair_prompt_ref, place_ref,
    q_ref, r_ref, own_ref, near_ref, far_ref,
    dq_ref, down_ref, spread_ref, contrib_ref,
    key_s, value_s, probs_s, dscores_s, q_s, r_s, sums_s,
):
    slot = pl.program_id(0)
    group = pl.program_id(1)
    response = response_ref[slot]
    length = lengths_ref[response]
    prompt = pair_prompt_ref[response // 2]
    mine = place_ref[0]
    column = pl.multiple_of(group * HEAD, HEAD)
    for dest, base in ((key_s, 0), (value_s, KEY_VALUE_HEADS * HEAD)):
        at = pl.ds(pl.multiple_of(base + column, HEAD), HEAD)
        dest[0:256, :] = near_ref[:, prompt, :, at].reshape(256, HEAD)
        dest[256:512, :] = far_ref[:, prompt, :, at].reshape(256, HEAD)
        dest[512:640, :] = own_ref[0, :, at]
    key = key_s[...]
    value = value_s[...]
    live = lax.broadcasted_iota(jnp.int32, (TOKENS, HEAD), 0) < length
    for h in range(GROUP):
        rows = slice(h * TOKENS, (h + 1) * TOKENS)
        columns = slice(h * HEAD, (h + 1) * HEAD)
        q_s[rows, :] = q_ref[0, :, columns]
        r_s[rows, :] = jnp.where(live, r_ref[0, :, columns], jnp.zeros((), bf16))
    total = jnp.zeros((1, TOKENS), f32)
    start = 0
    for heads in (2, 2, 2, 1):
        n = heads * TOKENS
        rows = slice(start * TOKENS, start * TOKENS + n)
        scores = lax.dot_general(key, q_s[rows, :], NT, preferred_element_type=f32)
        dprobs = lax.dot_general(value, r_s[rows, :], NT, preferred_element_type=f32)
        j = lax.broadcasted_iota(jnp.int32, (TOKENS, n), 0)
        t = lax.broadcasted_iota(jnp.int32, (TOKENS, n), 1) % TOKENS
        scores = jnp.concatenate(
            [scores[:512], jnp.where(j <= t, scores[512:], -1e30)], axis=0
        )
        top = jnp.max(scores, axis=0, keepdims=True)
        weight = jnp.exp2((scores - top) * LOG2_SCALE)
        probs = weight * (1.0 / jnp.sum(weight, axis=0, keepdims=True))
        delta = jnp.sum(probs * dprobs, axis=0, keepdims=True)
        probs_s[:, rows] = probs.astype(bf16)
        dscores_s[:, rows] = (probs * (dprobs - delta)).astype(bf16)
        for h in range(heads):
            total = total + delta[:, h * TOKENS : (h + 1) * TOKENS]
        start += heads
    dkey = lax.dot_general(dscores_s[...], q_s[...], NN, preferred_element_type=f32) * SCALE
    dvalue = lax.dot_general(probs_s[...], r_s[...], NN, preferred_element_type=f32)
    dq = lax.dot_general(key.T, dscores_s[...], NN, preferred_element_type=f32) * SCALE
    for h in range(GROUP):
        part = slice(h * HEAD, (h + 1) * HEAD)
        dq_ref[0, :, part] = dq[:, part].T.astype(bf16)
    for i, grad in enumerate((dkey, dvalue)):
        grad = grad.astype(bf16)
        base = i * KEY_VALUE_HEADS * HEAD
        down_ref[0, :, pl.ds(pl.multiple_of(base + column, HEAD), HEAD)] = grad[512:]
        pieces = grad[:512].reshape(2, 8, 2, 16, HEAD)
        for core in range(2):
            for half in range(2):
                piece = half * 4 + i * KEY_VALUE_HEADS + group
                spread_ref[:, jnp.bitwise_xor(mine, core), piece, slot] = pieces[core, :, half]
    total = jnp.sum(total, axis=1, keepdims=True)

    @pl.when(group == 0)
    def _():
        sums_s[slot] = jnp.broadcast_to(total, (8, HEAD))

    @pl.when(group == 1)
    def _():
        sums_s[slot] = sums_s[slot] + total

    @pl.when((slot == 1) & (group == 1))
    def _():
        ids = lax.broadcasted_iota(jnp.int32, (4, HEAD), 0) * HEAD
        ids = ids + lax.broadcasted_iota(jnp.int32, (4, HEAD), 1)
        contrib = jnp.zeros((4, HEAD), f32)
        for s in range(2):
            response = response_ref[s]
            sign = (1 - 2 * (response % 2)).astype(f32)
            contrib = contrib + jnp.where(ids == response // 2, sign * sums_s[s][0:4], 0.0)
        contrib_ref[...] = jnp.broadcast_to(contrib[None], contrib_ref.shape)


def attention(slot_response, lengths, pair_prompt, place, queries, readout, own, near, far):
    return pl.pallas_call(
        attention_kernel,
        out_shape=(
            jax.ShapeDtypeStruct((2, TOKENS, QUERY_HEADS * HEAD), bf16),
            jax.ShapeDtypeStruct((2, TOKENS, 512), bf16),
            jax.ShapeDtypeStruct((8, 2, 8, 2, 16, HEAD), bf16),
            jax.ShapeDtypeStruct((64, 4, HEAD), f32),
        ),
        grid_spec=pltpu.PrefetchScalarGridSpec(
            num_scalar_prefetch=4,
            grid=(2, 2),
            in_specs=[
                pl.BlockSpec((1, TOKENS, GROUP * HEAD), lambda s, g, *_: (s, 0, g)),
                pl.BlockSpec((1, TOKENS, GROUP * HEAD), lambda s, g, *_: (s, 0, g)),
                pl.BlockSpec((1, TOKENS, 512), lambda s, g, *_: (s, 0, 0)),
                pl.BlockSpec((8, 2, 32, 512), lambda s, g, *_: (0, 0, 0, 0)),
                pl.BlockSpec((8, 2, 32, 512), lambda s, g, *_: (0, 0, 0, 0)),
            ],
            out_specs=[
                pl.BlockSpec((1, TOKENS, GROUP * HEAD), lambda s, g, *_: (s, 0, g)),
                pl.BlockSpec((1, TOKENS, 512), lambda s, g, *_: (s, 0, 0)),
                pl.BlockSpec((8, 2, 8, 2, 16, HEAD), lambda s, g, *_: (0, 0, 0, 0, 0, 0)),
                pl.BlockSpec((64, 4, HEAD), lambda s, g, *_: (0, 0, 0)),
            ],
            scratch_shapes=[
                pltpu.VMEM((640, HEAD), bf16),
                pltpu.VMEM((640, HEAD), bf16),
                pltpu.VMEM((640, GROUP * TOKENS), bf16),
                pltpu.VMEM((640, GROUP * TOKENS), bf16),
                pltpu.VMEM((GROUP * TOKENS, HEAD), bf16),
                pltpu.VMEM((GROUP * TOKENS, HEAD), bf16),
                pltpu.VMEM((2, 8, HEAD), f32),
            ],
        ),
        compiler_params=pltpu.CompilerParams(vmem_limit_bytes=40 << 20),
        cost_estimate=pl.CostEstimate(
            flops=3_000_000_000, bytes_accessed=6_000_000, transcendentals=2_300_000
        ),
        name="attention",
    )(slot_response, lengths, pair_prompt, place, queries, readout, own, near, far)


def weigh_kernel(weights_ref, pieces_ref, out_ref):
    def step(i, sums):
        sums = list(sums)
        for k in range(4):
            piece = pieces_ref[i * 4 + k].astype(f32)
            for p in range(2):
                sums[k % 2 * 2 + p] += weights_ref[p, i * 4 + k] * piece
        return tuple(sums)

    zero = jnp.zeros((16, HEAD), f32)
    sums = lax.fori_loop(0, pieces_ref.shape[0] // 4, step, (zero,) * 4)
    both = jnp.stack([sums[0] + sums[2], sums[1] + sums[3]]).astype(bf16)
    out_ref[...] = jnp.broadcast_to(both[None], out_ref.shape)


def weigh(weights, pieces):
    return pl.pallas_call(
        weigh_kernel,
        out_shape=jax.ShapeDtypeStruct((32, 2, 16, HEAD), bf16),
        in_specs=[
            pl.BlockSpec(memory_space=pltpu.SMEM),
            pl.BlockSpec(memory_space=pltpu.VMEM),
        ],
        out_specs=pl.BlockSpec(memory_space=pltpu.VMEM),
        name="weigh",
    )(weights, pieces)


def to_all(pieces, axes):
    return lax.all_to_all(pieces, axes, 0, 0, tiled=True)


def copies(shard, axes):
    size = lax.axis_size(axes)
    return to_all(jnp.broadcast_to(shard[None], (size, *shard.shape)), axes)


def looked_up(table, ids):
    pairs = jnp.arange(table.shape[-1])
    return jnp.sum(jnp.where(ids[..., None] == pairs, table, 0.0), axis=-1)


def on_device(
    prompt_kv, response_queries, resp_kv, readout, slot_response, lengths, pair_prompt, ref_margin
):
    near = copies(prompt_kv, "z")
    far = lax.ppermute(near, "c", [(0, 1), (1, 0)])
    place = lax.axis_index("c").astype(jnp.int32)[None]
    sources = copies(slot_response[None, :], SPREAD).reshape(-1)
    dq, down, spread, contrib = attention(
        slot_response, lengths, pair_prompt, place,
        response_queries, readout, resp_kv, near, far,
    )
    pieces = to_all(spread.reshape(128, 2, 16, HEAD), SPREAD)
    some = jnp.sum(to_all(contrib, ("z", "y")), axis=0)
    pair_sums = jnp.sum(copies(some, ("c", "x")), axis=0).reshape(-1)
    margins = MARGIN_BETA * (pair_sums - ref_margin)
    pair_weight = -LOSS_SCALE * MARGIN_BETA * jax.nn.sigmoid(-margins)

    def coefficient(response):
        sign = 1.0 - 2.0 * (response % 2).astype(f32)
        return looked_up(pair_weight, response // 2) * sign

    prompts = jnp.arange(2)[:, None]
    per_prompt = jnp.where(pair_prompt[None, :] == prompts, pair_weight[None, :], 0.0)
    sign = 1.0 - 2.0 * (sources % 2).astype(f32)
    weights = looked_up(per_prompt[:, None, :], (sources // 2)[None, :]) * sign
    own = coefficient(slot_response)[:, None, None]
    grad_q = (own * dq.astype(f32)).astype(bf16)
    grad_own = (own * down.astype(f32)).astype(bf16)
    parts = to_all(weigh(weights, pieces.reshape(256, 16, HEAD)), RESP)
    parts = jnp.sum(parts.reshape(2, 4, 4, 2, 16, HEAD).astype(f32), axis=2)
    grad_prompt = jnp.transpose(parts, (2, 0, 3, 1, 4)).reshape(2, 32, 512).astype(bf16)
    return margins, grad_q, grad_own, grad_prompt


def solution(mesh):
    split = Mesh(mesh.devices.reshape(8, 2, 8, 4), EVERY)
    in_specs = (
        P(None, PREFIX, None),
        P(EVERY, None, None),
        P(EVERY, None, None),
        P(EVERY, None, None),
        P(EVERY),
        P(),
        P(),
        P(),
    )
    out_specs = (P(), P(EVERY, None, None), P(EVERY, None, None), P(None, PREFIX, None))
    return jax.shard_map(
        on_device, mesh=split, in_specs=in_specs, out_specs=out_specs, check_vma=False
    )
```

time: 202 us -> 155 us (0.77)
  blocking collectives: 0 us -> 57.1 us
  local copies, waits for them, and re-layouts: 40.6 us -> 5.17 us
  matrix products: 34.3 us -> 0 us
  starting transfers between devices: 42.9 us -> 21.1 us
  other arithmetic: 25 us -> 4.65 us
  Pallas kernels: 0 us -> 16.1 us
  between operations: 15.5 us -> 0.81 us
  waiting for transfers between devices: 41.8 us -> 49.6 us
    all_to_all x0 -> x3, blocking collectives: none -> 57.1 us  [to_all(): return lax.all_to_all(pieces, axes, 0, 0, tiled=True)]
    dot_general x24 -> x0, matrix products: 34.3 us -> none  [the longest x2 5.86 us: forward_pieces(): jnp.einsum('gjtk,kgd->tgjd', prefix_probabilities, prompt_values, preferr...]
    all_to_all x6 -> x3, starting transfers between devices: 42.9 us -> 19.2 us  [to_all(): return lax.all_to_all(pieces, axes, 0, 0, tiled=True)]
    pallas_call x0 -> x2, Pallas kernels: none -> 16.1 us  [the longest x1 13 us: attention(): pl.pallas_call(attention_kernel, out_shape=(jax.ShapeDtypeStruct((2, TOKE...]
    slice x10 -> x0, local copies, waits for them, and re-layouts: 9.03 us -> none  [the longest x3 2.84 us: unpack(): packed_rows[:, head_width:].reshape(row_block, KEY_VALUE_HEADS, HEAD_SIZE)]
    concatenate x10 -> x0, local copies, waits for them, and re-layouts: 8.08 us -> none  [the longest x6 7.65 us: on_device(): jnp.concatenate([jnp.einsum('hybi,bhyu->ihu', prefix_score_gradient, quer...]
    reduce_sum x12 -> x4, other arithmetic: 8.13 us -> 0.36 us  [the longest x1 0.23 us: looked_up(): return jnp.sum(jnp.where(ids[..., None] == pairs, table, 0.0), axis=-1)]
    convert_element_type x4 -> x2, local copies, waits for them, and re-layouts: 7.11 us -> 0.7 us  [on_device(): jnp.transpose(parts, (2, 0, 3, 1, 4)).reshape(2, 32, 512).astype(bf16)]
  transfers between devices with their start and end apart: 6 -> 4, of which waited for: 5 -> 4; matrix products, arithmetic and copies ran while one was open for 18% -> 3% of each run, Pallas kernels for 0% -> 0%
where the time goes in v1:
time: 155 us; the launch traced here: 154 us
  blocking collectives  57.1 us (37%)
  waiting for transfers between devices  49.6 us (32%)
  starting transfers between devices  21.1 us (14%)
  Pallas kernels  16.1 us (10%)
  local copies, waits for them, and re-layouts  5.17 us (3%)
  other arithmetic  4.65 us (3%)
    all_to_all x3, blocking collectives, to_all(): return lax.all_to_all(pieces, axes, 0, 0, tiled=True)  57.1 us
    all_to_all x3, waiting for transfers between devices, to_all(): return lax.all_to_all(pieces, axes, 0, 0, tiled=True)  47.7 us
    all_to_all x3, starting transfers between devices, to_all(): return lax.all_to_all(pieces, axes, 0, 0, tiled=True)  19.2 us
    pallas_call x1, Pallas kernels, attention(): pl.pallas_call(attention_kernel, out_shape=(jax.ShapeDtypeStruct((2, TOKE...  13 us
  transfers between devices with their start and end apart: 4, of which 4 were waited for; matrix products, arithmetic and copies ran while one was open for 3% of the time, Pallas kernels for 0%

profile of v1, /device:TPU:8, one launch (start us, length us, event | category | flops | bytes accessed | tf_op | source)
XLA Modules:
  0.0 154.4 jit_solution(12429055230105977214)
XLA Ops:
  0.7 1.0 broadcast_in_dim.43
  1.7 27.6 %all_to_all.30.near_ref = bf16[8,2,32,512]{3,2,1,0:T(8,128)(2,1)S(1)} all-to-all(bf16[8,2,32,512]{3,2,1,0:T(8,128)(2,1)S(1)} %broadcast_in_dim.43), channel_id=1, replica_groups=mesh['z'=8,'c'=2,'y'=8,'x'=4] {'z'}, dimensions={0} | all-to-all | bytes 1048576 | tf_op jit(solution)/shard_map/all_to_all | solution.py:187
  29.3 1.9 %collective-permute-start = (bf16[8,2,32,512]{3,2,1,0:T(8,128)(2,1)S(1)}, bf16[8,2,32,512]{3,2,1,0:T(8,128)(2,1)S(1)}, u32[]{:S(2)}, u32[]{:S(2)}) collective-permute-start(bf16[8,2,32,512]{3,2,1,0:T(8,128)(2,1)S(1)} %all_to_all.30.near_ref), channel_id=1, source_target_pairs={{0,32},{32,0},{1,33},{33,1},{2,34},{34,2},{3,35},{35,3},{4,36},{36... | collective-permute-start | bytes 1572872 | tf_op jit(solution)/shard_map/ppermute | solution.py:204
  31.2 1.9 %collective-permute-done.far_ref = bf16[8,2,32,512]{3,2,1,0:T(8,128)(2,1)S(1)} collective-permute-done((bf16[8,2,32,512]{3,2,1,0:T(8,128)(2,1)S(1)}, bf16[8,2,32,512]{3,2,1,0:T(8,128)(2,1)S(1)}, u32[]{:S(2)}, u32[]{:S(2)}) %collective-permute-start) | collective-permute-done | bytes 524320 | tf_op jit(solution)/shard_map/ppermute | solution.py:204
  33.1 1.2 copy-done.3
  34.3 13.0 %attention.1 = (bf16[2,128,1792]{2,1,0:T(8,128)(2,1)S(1)}, bf16[2,128,512]{2,1,0:T(8,128)(2,1)S(1)}, bf16[8,2,8,2,16,128]{5,4,3,2,1,0:T(8,128)(2,1)}, f32[64,4,128]{2,1,0:T(4,128)S(1)}) custom-call(s32[2]{0:T(128)S(1)} %copy-done.1, s32[1024]{0:T(1024)S(1)} %copy-done.5, s32[512]{0:T(512)S(1)} %copy-done, s32[1]{0:T(128)} %bitcast.place_ref, ...), custom_call_target="tpu_custom_call" | custom-call | flops 3000000000 | bytes 6000000 | tf_op jit(solution)/shard_map/attention/pallas_call | solution.py:116
  47.3 20.1 %all_to_all.31 = f32[64,4,128]{2,1,0:T(4,128)S(1)} all-to-all(f32[64,4,128]{2,1,0:T(4,128)S(1)} %get-tuple-element.8), channel_id=1, replica_groups=mesh['z'=8,'c'=2,'y'=8,'x'=4] {'z','y'}, dimensions={0} | all-to-all | bytes 262144 | tf_op jit(solution)/shard_map/all_to_all | solution.py:187
  67.4 0.7 broadcast_in_dim.70
  68.0 6.3 %all-to-all-start.3 = ((s32[128,1,2]{2,1,0:T(1,128)}), s32[128,1,2]{2,1,0:T(1,128)S(1)}, u32[]{:S(2)}, u32[]{:S(2)}) async-start(s32[128,1,2]{2,1,0:T(1,128)} %broadcast_in_dim.70), calls=%async_computation.3 | async-start | bytes 131072 | tf_op jit(solution)/shard_map/all_to_all | solution.py:187
  74.4 11.0 %all-to-all-done.3 = s32[128,1,2]{2,1,0:T(1,128)S(1)} async-done(((s32[128,1,2]{2,1,0:T(1,128)}), s32[128,1,2]{2,1,0:T(1,128)S(1)}, u32[]{:S(2)}, u32[]{:S(2)}) %all-to-all-start.3) | async-done | bytes 1056 | tf_op jit(solution)/shard_map/all_to_all | solution.py:187
  85.4 9.4 %all_to_all.32 = f32[8,4,128]{2,1,0:T(4,128)S(1)} all-to-all(f32[8,4,128]{2,1,0:T(4,128)S(1)} %broadcast_in_dim.46), channel_id=1, replica_groups=mesh['z'=8,'c'=2,'y'=8,'x'=4] {'c','x'}, dimensions={0} | all-to-all | bytes 32768 | tf_op jit(solution)/shard_map/all_to_all | solution.py:187
  94.8 6.7 %all-to-all-start.4 = ((bf16[128,2,16,128]{3,2,1,0:T(8,128)(2,1)}), bf16[128,2,16,128]{3,2,1,0:T(8,128)(2,1)S(1)}, u32[]{:S(2)}, u32[]{:S(2)}) async-start(bf16[128,2,16,128]{3,2,1,0:T(8,128)(2,1)} %bitcast.2), calls=%async_computation.4 | async-start | bytes 2097152 | tf_op jit(solution)/shard_map/all_to_all | solution.py:187
  101.5 0.5 broadcast.171
  102.0 0.8 reduce.5
  103.2 0.6 divide_multiply_fusion
  104.2 0.6 broadcast_multiply_fusion.weights_ref
  104.8 27.0 %all-to-all-done.4 = bf16[128,2,16,128]{3,2,1,0:T(8,128)(2,1)S(1)} async-done(((bf16[128,2,16,128]{3,2,1,0:T(8,128)(2,1)}), bf16[128,2,16,128]{3,2,1,0:T(8,128)(2,1)S(1)}, u32[]{:S(2)}, u32[]{:S(2)}) %all-to-all-start.4) | async-done | bytes 1048608 | tf_op jit(solution)/shard_map/all_to_all | solution.py:187
  131.8 1.0 copy-done.6
  132.8 3.0 %weigh.1 = bf16[32,2,16,128]{3,2,1,0:T(8,128)(2,1)} custom-call(f32[2,256]{1,0:T(2,128)} %broadcast_multiply_fusion.weights_ref, bf16[256,16,128]{2,1,0:T(8,128)(2,1)} %bitcast.11), custom_call_target="tpu_custom_call" | custom-call | tf_op jit(solution)/shard_map/weigh/pallas_call | solution.py:174
  135.8 6.2 %all-to-all-start.5 = ((bf16[32,2,16,128]{3,2,1,0:T(8,128)(2,1)}), bf16[32,2,16,128]{3,2,1,0:T(8,128)(2,1)S(1)}, u32[]{:S(2)}, u32[]{:S(2)}) async-start(bf16[32,2,16,128]{3,2,1,0:T(8,128)(2,1)} %weigh.1), calls=%async_computation.5 | async-start | bytes 524288 | tf_op jit(solution)/shard_map/all_to_all | solution.py:187
  142.1 0.8 multiply_convert_fusion.1
  142.9 1.1 multiply_convert_fusion
  144.0 9.7 %all-to-all-done.5 = bf16[32,2,16,128]{3,2,1,0:T(8,128)(2,1)S(1)} async-done(((bf16[32,2,16,128]{3,2,1,0:T(8,128)(2,1)}), bf16[32,2,16,128]{3,2,1,0:T(8,128)(2,1)S(1)}, u32[]{:S(2)}, u32[]{:S(2)}) %all-to-all-start.5) | async-done | bytes 262176 | tf_op jit(solution)/shard_map/all_to_all | solution.py:187
  153.8 0.7 convert_element_type.47
  (27 shorter events, 0.9 us)
Async XLA Ops:
  0.6 32.4 %copy-start.4 = (bf16[2,128,512]{2,1,0:T(8,128)(2,1)S(1)}, bf16[2,128,512]{2,1,0:T(8,128)(2,1)}, u32[]{:S(2)}) copy-start(bf16[2,128,512]{2,1,0:T(8,128)(2,1)} %own_ref.1) | copy-start | bytes 786436
  0.6 32.4 %copy-start.1 = (s32[2]{0:T(128)S(1)}, s32[2]{0:T(128)}, u32[]{:S(2)}) copy-start(s32[2]{0:T(128)} %response_ref.1) | copy-start | bytes 28
  0.7 32.4 %copy-start.5 = (s32[1024]{0:T(1024)S(1)}, s32[1024]{0:T(1024)}, u32[]{:S(2)}) copy-start(s32[1024]{0:T(1024)} %lengths_ref.1) | copy-start | bytes 12292
  0.7 32.4 %copy-start = (s32[512]{0:T(512)S(1)}, s32[512]{0:T(512)}, u32[]{:S(2)}) copy-start(s32[512]{0:T(512)} %pair_prompt_ref.1) | copy-start | bytes 6148
  0.7 32.4 %copy-start.2 = (bf16[2,128,1792]{2,1,0:T(8,128)(2,1)S(1)}, bf16[2,128,1792]{2,1,0:T(8,128)(2,1)}, u32[]{:S(2)}) copy-start(bf16[2,128,1792]{2,1,0:T(8,128)(2,1)} %q_ref.1) | copy-start | bytes 2752516
  29.3 3.8 %collective-permute-start = (bf16[8,2,32,512]{3,2,1,0:T(8,128)(2,1)S(1)}, bf16[8,2,32,512]{3,2,1,0:T(8,128)(2,1)S(1)}, u32[]{:S(2)}, u32[]{:S(2)}) collective-permute-start(bf16[8,2,32,512]{3,2,1,0:T(8,128)(2,1)S(1)} %all_to_all.30.near_ref), channel_id=1, source_target_pairs={{0,32},{32,0},{1,33},{33,1},{2,34},{34,2},{3,35},{35,3},{4,36},{36... | collective-permute-start | bytes 1572872 | tf_op jit(solution)/shard_map/ppermute | solution.py:204
  33.1 1.2 copy-start.3
  68.0 17.4 %all-to-all-start.3 = ((s32[128,1,2]{2,1,0:T(1,128)}), s32[128,1,2]{2,1,0:T(1,128)S(1)}, u32[]{:S(2)}, u32[]{:S(2)}) async-start(s32[128,1,2]{2,1,0:T(1,128)} %broadcast_in_dim.70), calls=%async_computation.3 | async-start | bytes 131072 | tf_op jit(solution)/shard_map/all_to_all | solution.py:187
  94.8 8.4 %copy-start.7 = (f32[512]{0:T(512)S(1)}, f32[512]{0:T(512)}, u32[]{:S(2)}) copy-start(f32[512]{0:T(512)} %param.15) | copy-start | bytes 6148
  94.8 37.0 %all-to-all-start.4 = ((bf16[128,2,16,128]{3,2,1,0:T(8,128)(2,1)}), bf16[128,2,16,128]{3,2,1,0:T(8,128)(2,1)S(1)}, u32[]{:S(2)}, u32[]{:S(2)}) async-start(bf16[128,2,16,128]{3,2,1,0:T(8,128)(2,1)} %bitcast.2), calls=%async_computation.4 | async-start | bytes 2097152 | tf_op jit(solution)/shard_map/all_to_all | solution.py:187
  131.8 1.0 copy-start.6
  135.8 17.9 %all-to-all-start.5 = ((bf16[32,2,16,128]{3,2,1,0:T(8,128)(2,1)}), bf16[32,2,16,128]{3,2,1,0:T(8,128)(2,1)S(1)}, u32[]{:S(2)}, u32[]{:S(2)}) async-start(bf16[32,2,16,128]{3,2,1,0:T(8,128)(2,1)} %weigh.1), calls=%async_computation.5 | async-start | bytes 524288 | tf_op jit(solution)/shard_map/all_to_all | solution.py:187

commit v2 on v1

v2 whole, which is shorter than its diff:
```python
import math

import jax
import jax.numpy as jnp
from jax import lax
from jax.experimental import pallas as pl
from jax.experimental.pallas import tpu as pltpu
from jax.sharding import Mesh
from jax.sharding import PartitionSpec as P

QUERY_HEADS = 14
KEY_VALUE_HEADS = 2
HEAD = 128
GROUP = QUERY_HEADS // KEY_VALUE_HEADS
TOKENS = 128
WIDTH = GROUP * HEAD
KEYS = 640
SCALE = HEAD**-0.5
LOG2_SCALE = SCALE * math.log2(math.e)
MARGIN_BETA = 0.1
LOSS_SCALE = 256.0
EVERY = ("z", "c", "yh", "yl", "x")
PREFIX = ("z", "c")
RESP = ("yh", "yl", "x")
CLOSE = ("c", "yl", "x")
APART = ("z", "yh")
LOAD_ROWS = 272
NT = (((1,), (1,)), ((), ()))
NN = (((1,), (0,)), ((), ()))
bf16 = jnp.bfloat16
f32 = jnp.float32


def pair_grid():
    ids = lax.broadcasted_iota(jnp.int32, (4, HEAD), 0) * HEAD
    return ids + lax.broadcasted_iota(jnp.int32, (4, HEAD), 1)


def fill(dest, near_ref, far_ref, own_ref, prompt, column):
    at = pl.ds(pl.multiple_of(column, HEAD), HEAD)
    dest[0:256, :] = near_ref[:, prompt, :, at].reshape(256, HEAD)
    dest[256:512, :] = far_ref[:, prompt, :, at].reshape(256, HEAD)
    dest[512:640, :] = own_ref[0, :, at]


def stack(q_ref, r_ref, q_s, r_s, length):
    live = lax.broadcasted_iota(jnp.int32, (TOKENS, HEAD), 0) < length
    for h in range(GROUP):
        rows = slice(h * TOKENS, (h + 1) * TOKENS)
        columns = slice(h * HEAD, (h + 1) * HEAD)
        q_s[rows, :] = q_ref[0, :, columns]
        r_s[rows, :] = jnp.where(live, r_ref[0, :, columns], jnp.zeros((), bf16))


def forward_kernel(
    response_ref, lengths_ref, pair_prompt_ref,
    q_ref, r_ref, own_ref, near_ref, far_ref,
    probs_ref, dscores_ref, contrib_ref,
    key_s, value_s, q_s, r_s, sums_s,
):
    slot = pl.program_id(0)
    group = pl.program_id(1)
    response = response_ref[slot]
    prompt = pair_prompt_ref[response // 2]
    fill(key_s, near_ref, far_ref, own_ref, prompt, group * HEAD)
    fill(value_s, near_ref, far_ref, own_ref, prompt, (KEY_VALUE_HEADS + group) * HEAD)
    key = key_s[...]
    value = value_s[...]
    stack(q_ref, r_ref, q_s, r_s, lengths_ref[response])
    total = jnp.zeros((1, TOKENS), f32)
    start = 0
    for heads in (2, 2, 2, 1):
        n = heads * TOKENS
        rows = slice(start * TOKENS, start * TOKENS + n)
        scores = lax.dot_general(key, q_s[rows, :], NT, preferred_element_type=f32)
        dprobs = lax.dot_general(value, r_s[rows, :], NT, preferred_element_type=f32)
        j = lax.broadcasted_iota(jnp.int32, (TOKENS, n), 0)
        t = lax.broadcasted_iota(jnp.int32, (TOKENS, n), 1) % TOKENS
        scores = jnp.concatenate(
            [scores[:512], jnp.where(j <= t, scores[512:], -1e30)], axis=0
        )
        top = jnp.max(scores, axis=0, keepdims=True)
        weight = jnp.exp2((scores - top) * LOG2_SCALE)
        probs = weight * (1.0 / jnp.sum(weight, axis=0, keepdims=True))
        delta = jnp.sum(probs * dprobs, axis=0, keepdims=True)
        probs_ref[0, :, rows] = probs.astype(bf16)
        dscores_ref[0, :, rows] = (probs * (dprobs - delta)).astype(bf16)
        for h in range(heads):
            total = total + delta[:, h * TOKENS : (h + 1) * TOKENS]
        start += heads
    total = jnp.sum(total, axis=1, keepdims=True)

    @pl.when(group == 0)
    def _():
        sums_s[slot] = jnp.broadcast_to(total, (8, HEAD))

    @pl.when(group == 1)
    def _():
        sums_s[slot] = sums_s[slot] + total

    @pl.when((slot == 1) & (group == 1))
    def _():
        ids = pair_grid()
        contrib = jnp.zeros((4, HEAD), f32)
        for s in range(2):
            response = response_ref[s]
            sign = (1 - 2 * (response % 2)).astype(f32)
            contrib = contrib + jnp.where(ids == response // 2, sign * sums_s[s][0:4], 0.0)
        contrib_ref[...] = jnp.broadcast_to(contrib[None], contrib_ref.shape)


def backward_kernel(
    response_ref, lengths_ref, pair_prompt_ref, place_ref,
    probs_ref, dscores_ref, q_ref, r_ref, own_ref, near_ref, far_ref,
    dq_ref, down_ref, load_ref,
    key_s, q_s, r_s,
):
    slot = pl.program_id(0)
    group = pl.program_id(1)
    response = response_ref[slot]
    prompt = pair_prompt_ref[response // 2]
    mine = place_ref[0]
    fill(key_s, near_ref, far_ref, own_ref, prompt, group * HEAD)
    stack(q_ref, r_ref, q_s, r_s, lengths_ref[response])
    dscores = dscores_ref[0]
    dkey = lax.dot_general(dscores, q_s[...], NN, preferred_element_type=f32) * SCALE
    dvalue = lax.dot_general(probs_ref[0], r_s[...], NN, preferred_element_type=f32)
    dq = lax.dot_general(key_s[...].T, dscores, NN, preferred_element_type=f32) * SCALE
    for h in range(GROUP):
        part = slice(h * HEAD, (h + 1) * HEAD)
        dq_ref[0, :, part] = dq[:, part].T.astype(bf16)
    for i, grad in enumerate((dkey, dvalue)):
        grad = grad.astype(bf16)
        part = i * KEY_VALUE_HEADS + group
        down_ref[0, :, pl.ds(pl.multiple_of(part * HEAD, HEAD), HEAD)] = grad[512:]
        pieces = grad[:512].reshape(2, 8, 2, 16, HEAD)
        rows = pl.ds(pl.multiple_of(slot * 128, 128), 128)
        for core in range(2):
            for half in range(2):
                dest = jnp.bitwise_xor(mine, core) * 8 + half * 4 + part
                load_ref[dest, rows, :] = pieces[core, :, half].reshape(128, HEAD)


def whole(shape):
    return pl.BlockSpec(shape, lambda s, g, *_: (0,) * len(shape))


def by_slot(shape):
    return pl.BlockSpec(shape, lambda s, g, *_: (s, 0, 0))


def by_group(shape):
    return pl.BlockSpec(shape, lambda s, g, *_: (s, 0, g))


def by_both(shape):
    return pl.BlockSpec(shape, lambda s, g, *_: (s * 2 + g, 0, 0))


def forward(slot_response, lengths, pair_prompt, queries, readout, own, near, far):
    return pl.pallas_call(
        forward_kernel,
        out_shape=(
            jax.ShapeDtypeStruct((4, KEYS, WIDTH), bf16),
            jax.ShapeDtypeStruct((4, KEYS, WIDTH), bf16),
            jax.ShapeDtypeStruct((32, 4, HEAD), f32),
        ),
        grid_spec=pltpu.PrefetchScalarGridSpec(
            num_scalar_prefetch=3,
            grid=(2, 2),
            in_specs=[
                by_group((1, TOKENS, WIDTH)),
                by_group((1, TOKENS, WIDTH)),
                by_slot((1, TOKENS, 512)),
                whole((8, 2, 32, 512)),
                whole((8, 2, 32, 512)),
            ],
            out_specs=[
                by_both((1, KEYS, WIDTH)),
                by_both((1, KEYS, WIDTH)),
                whole((32, 4, HEAD)),
            ],
            scratch_shapes=[
                pltpu.VMEM((KEYS, HEAD), bf16),
                pltpu.VMEM((KEYS, HEAD), bf16),
                pltpu.VMEM((WIDTH, HEAD), bf16),
                pltpu.VMEM((WIDTH, HEAD), bf16),
                pltpu.VMEM((2, 8, HEAD), f32),
            ],
        ),
        compiler_params=pltpu.CompilerParams(vmem_limit_bytes=58 << 20),
        cost_estimate=pl.CostEstimate(
            flops=1_200_000_000, bytes_accessed=12_000_000, transcendentals=2_300_000
        ),
        name="forward",
    )(slot_response, lengths, pair_prompt, queries, readout, own, near, far)


def backward(
    slot_response, lengths, pair_prompt, place, probs, dscores, queries, readout, own, near, far
):
    return pl.pallas_call(
        backward_kernel,
        out_shape=(
            jax.ShapeDtypeStruct((2, TOKENS, QUERY_HEADS * HEAD), bf16),
            jax.ShapeDtypeStruct((2, TOKENS, 512), bf16),
            jax.ShapeDtypeStruct((16, LOAD_ROWS, HEAD), bf16),
        ),
        grid_spec=pltpu.PrefetchScalarGridSpec(
            num_scalar_prefetch=4,
            grid=(2, 2),
            in_specs=[
                by_both((1, KEYS, WIDTH)),
                by_both((1, KEYS, WIDTH)),
                by_group((1, TOKENS, WIDTH)),
                by_group((1, TOKENS, WIDTH)),
                by_slot((1, TOKENS, 512)),
                whole((8, 2, 32, 512)),
                whole((8, 2, 32, 512)),
            ],
            out_specs=[
                by_group((1, TOKENS, WIDTH)),
                by_slot((1, TOKENS, 512)),
                whole((16, LOAD_ROWS, HEAD)),
            ],
            scratch_shapes=[
                pltpu.VMEM((KEYS, HEAD), bf16),
                pltpu.VMEM((WIDTH, HEAD), bf16),
                pltpu.VMEM((WIDTH, HEAD), bf16),
            ],
        ),
        compiler_params=pltpu.CompilerParams(vmem_limit_bytes=58 << 20),
        cost_estimate=pl.CostEstimate(
            flops=1_800_000_000, bytes_accessed=14_000_000, transcendentals=0
        ),
        name="backward",
    )(slot_response, lengths, pair_prompt, place, probs, dscores, queries, readout, own, near, far)


def news_kernel(response_ref, contribs_ref, load_ref, out_ref, news_s, sems):
    share = contribs_ref[0]
    for i in range(1, 32):
        share = share + contribs_ref[i]
    high = share.astype(bf16).astype(f32)
    middle = (share - high).astype(bf16).astype(f32)
    low = share - high - middle
    names = []
    for slot in range(2):
        response = response_ref[slot]
        for part in (response // 32, response % 32):
            names.append(jnp.full((1, HEAD), part.astype(f32)))
    news_s[...] = jnp.concatenate([high, middle, low, *names], axis=0).astype(bf16)
    copies = [
        pltpu.make_async_copy(news_s, out_ref.at[i, 256:272], sems.at[i]) for i in range(16)
    ]
    for copy in copies:
        copy.start()
    for copy in copies:
        copy.wait()


def with_news(slot_response, contribs, load):
    return pl.pallas_call(
        news_kernel,
        out_shape=jax.ShapeDtypeStruct(load.shape, bf16),
        in_specs=[
            pl.BlockSpec(memory_space=pltpu.SMEM),
            pl.BlockSpec(memory_space=pltpu.VMEM),
            pl.BlockSpec(memory_space=pltpu.HBM),
        ],
        out_specs=pl.BlockSpec(memory_space=pltpu.HBM),
        scratch_shapes=[pltpu.VMEM((16, HEAD), bf16), pltpu.SemaphoreType.DMA((16,))],
        input_output_aliases={2: 0},
        compiler_params=pltpu.CompilerParams(vmem_limit_bytes=58 << 20),
        name="news",
    )(slot_response, contribs, load)


def weigh_kernel(ref_margin_ref, pair_prompt_ref, load_ref, margins_ref, weights_ref, out_ref, factor_s):
    pair_sums = jnp.zeros((4, HEAD), f32)
    names = []
    for source in range(16):
        n = load_ref[source, 256:272, :].astype(f32)
        pair_sums = pair_sums + (n[0:4] + n[4:8] + n[8:12])
        names += [n[12:13] * 32.0 + n[13:14], n[14:15] * 32.0 + n[15:16]]
    margins = MARGIN_BETA * (pair_sums - ref_margin_ref[...])
    margins_ref[...] = margins
    weights = -LOSS_SCALE * MARGIN_BETA * jax.nn.sigmoid(-margins)
    weights_ref[...] = weights
    responses = jnp.concatenate(names, axis=0).astype(jnp.int32)
    sign = (1 - 2 * (responses % 2)).astype(f32)
    lane = lax.broadcasted_iota(jnp.int32, (32, HEAD), 1)
    for p in range(2):
        table = jnp.where(pair_prompt_ref[...] == p, weights, 0.0)
        found = jnp.zeros((32, HEAD), f32)
        for k in range(4):
            found = jnp.where(responses // 2 == lane + k * HEAD, table[k : k + 1], found)
        factor_s[p] = sign * jnp.sum(found, axis=1, keepdims=True)

    def step(z, _):
        sums = [jnp.zeros((16, HEAD), f32) for _ in range(2)]
        for source in range(16):
            for slot in range(2):
                rows = pl.ds(pl.multiple_of(slot * 128 + z * 16, 16), 16)
                piece = load_ref[source, rows, :].astype(f32)
                at = source * 2 + slot
                for p in range(2):
                    sums[p] = sums[p] + factor_s[p, at : at + 1, :] * piece
        for p in range(2):
            out_ref[z, :, p] = sums[p].reshape(4, 4, HEAD).astype(bf16)
        return 0

    lax.fori_loop(0, 8, step, 0)


def weigh(ref_margin, pair_prompt, load):
    vmem = pl.BlockSpec(memory_space=pltpu.VMEM)
    return pl.pallas_call(
        weigh_kernel,
        out_shape=(
            jax.ShapeDtypeStruct((4, HEAD), f32),
            jax.ShapeDtypeStruct((4, HEAD), f32),
            jax.ShapeDtypeStruct((8, 4, 2, 4, HEAD), bf16),
        ),
        in_specs=[vmem, vmem, vmem],
        out_specs=(vmem, vmem, vmem),
        scratch_shapes=[pltpu.VMEM((2, 32, HEAD), f32)],
        compiler_params=pltpu.CompilerParams(vmem_limit_bytes=8 << 20),
        name="weigh",
    )(ref_margin, pair_prompt, load)


def join_kernel(parts_ref, out_ref):
    total = parts_ref[0].astype(f32)
    for i in range(1, 32):
        total = total + parts_ref[i].astype(f32)
    out_ref[...] = jnp.broadcast_to(total.astype(bf16)[None], out_ref.shape)


def join(parts):
    vmem = pl.BlockSpec(memory_space=pltpu.VMEM)
    return pl.pallas_call(
        join_kernel,
        out_shape=jax.ShapeDtypeStruct((32, 8, HEAD), bf16),
        in_specs=[vmem],
        out_specs=vmem,
        compiler_params=pltpu.CompilerParams(vmem_limit_bytes=8 << 20),
        name="join",
    )(parts)


def to_all(pieces, axes):
    return lax.all_to_all(pieces, axes, 0, 0, tiled=True)


def copies_to_all(shard, axes):
    size = lax.axis_size(axes)
    return to_all(jnp.broadcast_to(shard[None], (size, *shard.shape)), axes)


def on_device(
    prompt_kv, response_queries, resp_kv, readout, slot_response, lengths, pair_prompt, ref_margin
):
    near = copies_to_all(prompt_kv, "z")
    far = lax.ppermute(near, "c", [(0, 1), (1, 0)])
    place = lax.axis_index("c").astype(jnp.int32)[None]
    data = (response_queries, readout, resp_kv, near, far)
    probs, dscores, contrib = forward(slot_response, lengths, pair_prompt, *data)
    contribs = to_all(contrib, APART)
    dq, down, load = backward(
        slot_response, lengths, pair_prompt, place, probs, dscores, *data
    )
    load = to_all(with_news(slot_response, contribs, load), CLOSE)
    margins, weights, parts = weigh(
        ref_margin.reshape(4, HEAD), pair_prompt.reshape(4, HEAD), load
    )
    pairs = jnp.arange(ref_margin.shape[0])
    sign = 1.0 - 2.0 * (slot_response % 2).astype(f32)
    found = jnp.where((slot_response // 2)[:, None] == pairs, weights.reshape(1, -1), 0.0)
    own = (jnp.sum(found, axis=1) * sign)[:, None, None]
    grad_q = (own * dq.astype(f32)).astype(bf16)
    grad_own = (own * down.astype(f32)).astype(bf16)
    total = join(to_all(parts.reshape(32, 8, HEAD), APART))
    total = to_all(total, RESP).reshape(4, 2, 4, 2, 4, HEAD)
    grad_prompt = jnp.transpose(total, (3, 1, 0, 4, 2, 5)).reshape(2, 32, 512)
    return margins.reshape(-1), grad_q, grad_own, grad_prompt


def solution(mesh):
    split = Mesh(mesh.devices.reshape(8, 2, 4, 2, 4), EVERY)
    in_specs = (
        P(None, PREFIX, None),
        P(EVERY, None, None),
        P(EVERY, None, None),
        P(EVERY, None, None),
        P(EVERY),
        P(),
        P(),
        P(),
    )
    out_specs = (P(), P(EVERY, None, None), P(EVERY, None, None), P(None, PREFIX, None))
    return jax.shard_map(
        on_device, mesh=split, in_specs=in_specs, out_specs=out_specs, check_vma=False
    )
```

time: 155 us -> 127 us (0.82)
  blocking collectives: 57.1 us -> 27.6 us
  waiting for transfers between devices: 49.6 us -> 40.2 us
  Pallas kernels: 16.1 us -> 24.3 us
  starting transfers between devices: 21.1 us -> 28.3 us
  other arithmetic: 4.65 us -> 2.16 us
  local copies, waits for them, and re-layouts: 5.17 us -> 3.02 us
    all_to_all x3 -> x1, blocking collectives: 57.1 us -> 27.6 us  [to_all(): return lax.all_to_all(pieces, axes, 0, 0, tiled=True)]
    all_to_all x3 -> x4, waiting for transfers between devices: 47.7 us -> 38.3 us  [to_all(): return lax.all_to_all(pieces, axes, 0, 0, tiled=True)]
    pallas_call x2 -> x5, Pallas kernels: 16.1 us -> 24.3 us  [the longest x1 11 us: forward(): pl.pallas_call(forward_kernel, out_shape=(jax.ShapeDtypeStruct((4, KEYS,...]
    all_to_all x3 -> x4, starting transfers between devices: 19.2 us -> 26.4 us  [to_all(): return lax.all_to_all(pieces, axes, 0, 0, tiled=True)]
  transfers between devices with their start and end apart: 4 -> 5, of which waited for: 4 -> 5; matrix products, arithmetic and copies ran while one was open for 3% -> 2% of each run, Pallas kernels for 0% -> 8%
where the time goes in v2:
time: 127 us; the launch traced here: 126 us
  waiting for transfers between devices  40.2 us (32%)
  starting transfers between devices  28.3 us (22%)
  blocking collectives  27.6 us (22%)
  Pallas kernels  24.3 us (19%)
  local copies, waits for them, and re-layouts  3.02 us (2%)
  other arithmetic  2.16 us (2%)
    all_to_all x4, waiting for transfers between devices, to_all(): return lax.all_to_all(pieces, axes, 0, 0, tiled=True)  38.3 us
    all_to_all x1, blocking collectives, to_all(): return lax.all_to_all(pieces, axes, 0, 0, tiled=True)  27.6 us
    all_to_all x4, starting transfers between devices, to_all(): return lax.all_to_all(pieces, axes, 0, 0, tiled=True)  26.4 us
    pallas_call x1, Pallas kernels, forward(): pl.pallas_call(forward_kernel, out_shape=(jax.ShapeDtypeStruct((4, KEYS,...  11 us
    pallas_call x1, Pallas kernels, backward(): pl.pallas_call(backward_kernel, out_shape=(jax.ShapeDtypeStruct((2, TOKEN...  9.48 us
  transfers between devices with their start and end apart: 5, of which 5 were waited for; matrix products, arithmetic and copies ran while one was open for 2% of the time, Pallas kernels for 8%

profile of v2, /device:TPU:8, one launch (start us, length us, event | category | flops | bytes accessed | tf_op | source)
XLA Modules:
  0.0 126.3 jit_solution(15929601048160481337)
XLA Ops:
  0.6 0.9 broadcast_in_dim.26
  1.5 27.6 %all_to_all.25.near_ref = bf16[8,2,32,512]{3,2,1,0:T(8,128)(2,1)S(1)} all-to-all(bf16[8,2,32,512]{3,2,1,0:T(8,128)(2,1)S(1)} %broadcast_in_dim.26), channel_id=1, replica_groups=mesh['z'=8,'c'=2,'yh'=4,'yl'=2,'x'=4] {'z'}, dimensions={0} | all-to-all | bytes 1048576 | tf_op jit(solution)/shard_map/all_to_all | solution.py:353
  29.1 1.9 %collective-permute-start = (bf16[8,2,32,512]{3,2,1,0:T(8,128)(2,1)S(1)}, bf16[8,2,32,512]{3,2,1,0:T(8,128)(2,1)S(1)}, u32[]{:S(2)}, u32[]{:S(2)}) collective-permute-start(bf16[8,2,32,512]{3,2,1,0:T(8,128)(2,1)S(1)} %all_to_all.25.near_ref), channel_id=1, source_target_pairs={{0,32},{32,0},{1,33},{33,1},{2,34},{34,2},{3,35},{35,3},{4,36},{36... | collective-permute-start | bytes 1572872 | tf_op jit(solution)/shard_map/ppermute | solution.py:365
  31.1 1.9 %collective-permute-done.far_ref = bf16[8,2,32,512]{3,2,1,0:T(8,128)(2,1)S(1)} collective-permute-done((bf16[8,2,32,512]{3,2,1,0:T(8,128)(2,1)S(1)}, bf16[8,2,32,512]{3,2,1,0:T(8,128)(2,1)S(1)}, u32[]{:S(2)}, u32[]{:S(2)}) %collective-permute-start) | collective-permute-done | bytes 524320 | tf_op jit(solution)/shard_map/ppermute | solution.py:365
  32.9 0.8 copy-done.4
  33.7 11.0 %forward.1 = (bf16[4,640,896]{2,1,0:T(8,128)(2,1)}, bf16[4,640,896]{2,1,0:T(8,128)(2,1)}, f32[32,4,128]{2,1,0:T(4,128)}) custom-call(s32[2]{0:T(128)} %response_ref.5, s32[1024]{0:T(1024)} %lengths_ref.3, s32[512]{0:T(512)} %pair_prompt_ref.3, bf16[2,128,1792]{2,1,0:T(8,128)(2,1)} %q_ref.3, bf16[2,128,1792]{2,1,0:T(8,128)(2,1)} %r_ref.3, ...), custom_call_target="tpu_custom_call" | custom-call | flops 1200000000 | bytes 12000000 | tf_op jit(solution)/shard_map/forward/pallas_call | solution.py:161
  44.8 6.6 %all-to-all-start.1 = ((f32[32,4,128]{2,1,0:T(4,128)}), f32[32,4,128]{2,1,0:T(4,128)S(1)}, u32[]{:S(2)}, u32[]{:S(2)}) async-start(f32[32,4,128]{2,1,0:T(4,128)} %get-tuple-element.13), calls=%async_computation.1 | async-start | bytes 131072 | tf_op jit(solution)/shard_map/all_to_all | solution.py:353
  51.4 9.5 %backward.1 = (bf16[2,128,1792]{2,1,0:T(8,128)(2,1)}, bf16[2,128,512]{2,1,0:T(8,128)(2,1)}, bf16[16,272,128]{2,1,0:T(8,128)(2,1)}) custom-call(s32[2]{0:T(128)} %response_ref.5, s32[1024]{0:T(1024)} %lengths_ref.3, s32[512]{0:T(512)} %pair_prompt_ref.3, s32[1]{0:T(128)} %bitcast.2.place_ref, bf16[4,640,896]{2,1,0:T(8,128)(2,1)} %get-tuple-element.14.probs_ref, ...), custom_call_target="tpu_custom_call" | custom-call | flops 1800000000 | bytes 14000000 | tf_op jit(solution)/shard_map/backward/pallas_call | solution.py:202
  60.9 2.9 %all-to-all-done.1.contribs_ref = f32[32,4,128]{2,1,0:T(4,128)S(1)} async-done(((f32[32,4,128]{2,1,0:T(4,128)}), f32[32,4,128]{2,1,0:T(4,128)S(1)}, u32[]{:S(2)}, u32[]{:S(2)}) %all-to-all-start.1) | async-done | bytes 65568 | tf_op jit(solution)/shard_map/all_to_all | solution.py:353
  63.7 0.6 copy-done.6
  64.4 1.7 %news.1 = bf16[16,272,128]{2,1,0:T(8,128)(2,1)} custom-call(s32[2]{0:T(128)} %response_ref.5, f32[32,4,128]{2,1,0:T(4,128)} %copy-done.6, bf16[16,272,128]{2,1,0:T(8,128)(2,1)} %get-tuple-element.16.load_ref), custom_call_target="tpu_custom_call", output_to_operand_aliasing={{}: (2, {})} | custom-call | tf_op jit(solution)/shard_map/news/pallas_call | solution.py:263
  66.1 0.0 copy-start.3
  66.1 5.9 %all-to-all-start.2 = ((bf16[16,272,128]{2,1,0:T(8,128)(2,1)}), bf16[16,272,128]{2,1,0:T(8,128)(2,1)S(1)}, u32[]{:S(2)}, u32[]{:S(2)}) async-start(bf16[16,272,128]{2,1,0:T(8,128)(2,1)} %news.1), calls=%async_computation.2 | async-start | bytes 2228224 | tf_op jit(solution)/shard_map/all_to_all | solution.py:353
  72.1 16.1 %all-to-all-done.2.load_ref = bf16[16,272,128]{2,1,0:T(8,128)(2,1)S(1)} async-done(((bf16[16,272,128]{2,1,0:T(8,128)(2,1)}), bf16[16,272,128]{2,1,0:T(8,128)(2,1)S(1)}, u32[]{:S(2)}, u32[]{:S(2)}) %all-to-all-start.2) | async-done | bytes 1114144 | tf_op jit(solution)/shard_map/all_to_all | solution.py:353
  88.2 1.3 %weigh.1 = (f32[4,128]{1,0:T(4,128)}, f32[4,128]{1,0:T(4,128)S(1)}, bf16[8,4,2,4,128]{4,3,2,1,0:T(4,128)(2,1)}) custom-call(f32[4,128]{1,0:T(4,128)S(1)} %bitcast.10, s32[4,128]{1,0:T(4,128)S(1)} %bitcast.9, bf16[16,272,128]{2,1,0:T(8,128)(2,1)S(1)} %all-to-all-done.2.load_ref), custom_call_target="tpu_custom_call" | custom-call | tf_op jit(solution)/shard_map/weigh/pallas_call | solution.py:318
  89.5 0.2 fusion
  89.7 9.3 %all-to-all-start.3 = ((bf16[32,8,128]{2,1,0:T(8,128)(2,1)}), bf16[32,8,128]{2,1,0:T(8,128)(2,1)S(1)}, u32[]{:S(2)}, u32[]{:S(2)}) async-start(bf16[32,8,128]{2,1,0:T(8,128)(2,1)} %bitcast.5), calls=%async_computation.3 | async-start | bytes 131072 | tf_op jit(solution)/shard_map/all_to_all | solution.py:353
  99.1 1.1 multiply_convert_fusion
  100.2 11.1 %all-to-all-done.3.parts_ref = bf16[32,8,128]{2,1,0:T(8,128)(2,1)S(1)} async-done(((bf16[32,8,128]{2,1,0:T(8,128)(2,1)}), bf16[32,8,128]{2,1,0:T(8,128)(2,1)S(1)}, u32[]{:S(2)}, u32[]{:S(2)}) %all-to-all-start.3) | async-done | bytes 65568 | tf_op jit(solution)/shard_map/all_to_all | solution.py:353
  111.3 0.7 join.1
  112.0 4.6 %all-to-all-start.4 = ((bf16[32,8,128]{2,1,0:T(8,128)(2,1)}), bf16[32,8,128]{2,1,0:T(8,128)(2,1)S(1)}, u32[]{:S(2)}, u32[]{:S(2)}) async-start(bf16[32,8,128]{2,1,0:T(8,128)(2,1)} %join.1), calls=%async_computation.4 | async-start | bytes 131072 | tf_op jit(solution)/shard_map/all_to_all | solution.py:353
  116.6 0.8 multiply_convert_fusion.1
  117.4 8.2 %all-to-all-done.4 = bf16[32,8,128]{2,1,0:T(8,128)(2,1)S(1)} async-done(((bf16[32,8,128]{2,1,0:T(8,128)(2,1)}), bf16[32,8,128]{2,1,0:T(8,128)(2,1)S(1)}, u32[]{:S(2)}, u32[]{:S(2)}) %all-to-all-start.4) | async-done | bytes 65568 | tf_op jit(solution)/shard_map/all_to_all | solution.py:353
  125.6 0.7 reshape.36
  (16 shorter events, 0.1 us)
Async XLA Ops:
  29.1 3.8 %copy-start.2 = (bf16[8,2,32,512]{3,2,1,0:T(8,128)(2,1)}, bf16[8,2,32,512]{3,2,1,0:T(8,128)(2,1)S(1)}, u32[]{:S(2)}) copy-start(bf16[8,2,32,512]{3,2,1,0:T(8,128)(2,1)S(1)} %all_to_all.25.near_ref) | copy-start | bytes 1572868
  29.1 3.8 %collective-permute-start = (bf16[8,2,32,512]{3,2,1,0:T(8,128)(2,1)S(1)}, bf16[8,2,32,512]{3,2,1,0:T(8,128)(2,1)S(1)}, u32[]{:S(2)}, u32[]{:S(2)}) collective-permute-start(bf16[8,2,32,512]{3,2,1,0:T(8,128)(2,1)S(1)} %all_to_all.25.near_ref), channel_id=1, source_target_pairs={{0,32},{32,0},{1,33},{33,1},{2,34},{34,2},{3,35},{35,3},{4,36},{36... | collective-permute-start | bytes 1572872 | tf_op jit(solution)/shard_map/ppermute | solution.py:365
  32.9 0.8 copy-start.4
  44.8 19.0 %all-to-all-start.1 = ((f32[32,4,128]{2,1,0:T(4,128)}), f32[32,4,128]{2,1,0:T(4,128)S(1)}, u32[]{:S(2)}, u32[]{:S(2)}) async-start(f32[32,4,128]{2,1,0:T(4,128)} %get-tuple-element.13), calls=%async_computation.1 | async-start | bytes 131072 | tf_op jit(solution)/shard_map/all_to_all | solution.py:353
  63.7 0.6 copy-start.6
  64.4 7.7 %copy-start.7 = (s32[2]{0:T(128)S(1)}, s32[2]{0:T(128)}, u32[]{:S(2)}) copy-start(s32[2]{0:T(128)} %response_ref.5) | copy-start | bytes 28
  64.4 23.8 %copy-start = (s32[512]{0:T(512)S(1)}, s32[512]{0:T(512)}, u32[]{:S(2)}) copy-start(s32[512]{0:T(512)} %pair_prompt_ref.3) | copy-start | bytes 6148
  64.4 23.8 %copy-start.1 = (f32[512]{0:T(512)S(1)}, f32[512]{0:T(512)}, u32[]{:S(2)}) copy-start(f32[512]{0:T(512)} %param.15) | copy-start | bytes 6148
  66.1 32.9 %copy-start.3 = (bf16[2,128,1792]{2,1,0:T(8,128)(2,1)S(1)}, bf16[2,128,1792]{2,1,0:T(8,128)(2,1)}, u32[]{:S(2)}) copy-start(bf16[2,128,1792]{2,1,0:T(8,128)(2,1)} %get-tuple-element.19) | copy-start | bytes 2752516
  66.1 22.1 %all-to-all-start.2 = ((bf16[16,272,128]{2,1,0:T(8,128)(2,1)}), bf16[16,272,128]{2,1,0:T(8,128)(2,1)S(1)}, u32[]{:S(2)}, u32[]{:S(2)}) async-start(bf16[16,272,128]{2,1,0:T(8,128)(2,1)} %news.1), calls=%async_computation.2 | async-start | bytes 2228224 | tf_op jit(solution)/shard_map/all_to_all | solution.py:353
  72.0 44.5 %copy-start.5 = (bf16[2,128,512]{2,1,0:T(8,128)(2,1)S(1)}, bf16[2,128,512]{2,1,0:T(8,128)(2,1)}, u32[]{:S(2)}) copy-start(bf16[2,128,512]{2,1,0:T(8,128)(2,1)} %get-tuple-element.20) | copy-start | bytes 786436
  89.7 21.6 %all-to-all-start.3 = ((bf16[32,8,128]{2,1,0:T(8,128)(2,1)}), bf16[32,8,128]{2,1,0:T(8,128)(2,1)S(1)}, u32[]{:S(2)}, u32[]{:S(2)}) async-start(bf16[32,8,128]{2,1,0:T(8,128)(2,1)} %bitcast.5), calls=%async_computation.3 | async-start | bytes 131072 | tf_op jit(solution)/shard_map/all_to_all | solution.py:353
  112.0 13.6 %all-to-all-start.4 = ((bf16[32,8,128]{2,1,0:T(8,128)(2,1)}), bf16[32,8,128]{2,1,0:T(8,128)(2,1)S(1)}, u32[]{:S(2)}, u32[]{:S(2)}) async-start(bf16[32,8,128]{2,1,0:T(8,128)(2,1)} %join.1), calls=%async_computation.4 | async-start | bytes 131072 | tf_op jit(solution)/shard_map/all_to_all | solution.py:353

commit v3 on v2

v3 whole, which is shorter than its diff:
```python
import math

import jax
import jax.numpy as jnp
from jax import lax
from jax.experimental import pallas as pl
from jax.experimental.pallas import tpu as pltpu
from jax.sharding import Mesh
from jax.sharding import PartitionSpec as P

QUERY_HEADS = 14
KEY_VALUE_HEADS = 2
HEAD = 128
GROUP = QUERY_HEADS // KEY_VALUE_HEADS
TOKENS = 128
WIDTH = GROUP * HEAD
KEYS = 640
SCALE = HEAD**-0.5
LOG2_SCALE = SCALE * math.log2(math.e)
MARGIN_BETA = 0.1
LOSS_SCALE = 256.0
EVERY = ("z", "c", "y", "x")
PREFIX = ("z", "c")
RESP = ("y", "x")
CLOSE = ("c", "x")
APART = ("z", "y")
LOAD_ROWS = 528
NT = (((1,), (1,)), ((), ()))
NN = (((1,), (0,)), ((), ()))
bf16 = jnp.bfloat16
f32 = jnp.float32


def pair_grid():
    ids = lax.broadcasted_iota(jnp.int32, (4, HEAD), 0) * HEAD
    return ids + lax.broadcasted_iota(jnp.int32, (4, HEAD), 1)


def fill(dest, near_ref, far_ref, own_ref, prompt, column):
    at = pl.ds(pl.multiple_of(column, HEAD), HEAD)
    dest[0:256, :] = near_ref[:, prompt, :, at].reshape(256, HEAD)
    dest[256:512, :] = far_ref[:, prompt, :, at].reshape(256, HEAD)
    dest[512:640, :] = own_ref[0, :, at]


def stack(q_ref, r_ref, q_s, r_s, length):
    live = lax.broadcasted_iota(jnp.int32, (TOKENS, HEAD), 0) < length
    for h in range(GROUP):
        rows = slice(h * TOKENS, (h + 1) * TOKENS)
        columns = slice(h * HEAD, (h + 1) * HEAD)
        q_s[rows, :] = q_ref[0, :, columns]
        r_s[rows, :] = jnp.where(live, r_ref[0, :, columns], jnp.zeros((), bf16))


def forward_kernel(
    response_ref, lengths_ref, pair_prompt_ref,
    q_ref, r_ref, own_ref, near_ref, far_ref,
    stats_ref, contrib_ref,
    key_s, value_s, q_s, r_s, sums_s,
):
    slot = pl.program_id(0)
    group = pl.program_id(1)
    response = response_ref[slot]
    prompt = pair_prompt_ref[response // 2]
    fill(key_s, near_ref, far_ref, own_ref, prompt, group * HEAD)
    fill(value_s, near_ref, far_ref, own_ref, prompt, (KEY_VALUE_HEADS + group) * HEAD)
    stack(q_ref, r_ref, q_s, r_s, lengths_ref[response])
    scores = lax.dot_general(key_s[...], q_s[...], NT, preferred_element_type=f32)
    dprobs = lax.dot_general(value_s[...], r_s[...], NT, preferred_element_type=f32)
    scores = masked(scores)
    top = jnp.max(scores, axis=0, keepdims=True)
    weight = jnp.exp2((scores - top) * LOG2_SCALE)
    share = 1.0 / jnp.sum(weight, axis=0, keepdims=True)
    delta = jnp.sum(weight * dprobs, axis=0, keepdims=True) * share
    at = slot * KEY_VALUE_HEADS + group
    stats_ref[at, 0:1, :] = top
    stats_ref[at, 1:2, :] = share
    stats_ref[at, 2:3, :] = delta
    total = jnp.sum(delta, axis=1, keepdims=True)

    @pl.when(group == 0)
    def _():
        sums_s[slot] = jnp.broadcast_to(total, (8, HEAD))

    @pl.when(group == 1)
    def _():
        sums_s[slot] = sums_s[slot] + total

    @pl.when((slot == 1) & (group == 1))
    def _():
        ids = pair_grid()
        contrib = jnp.zeros((4, HEAD), f32)
        for s in range(2):
            response = response_ref[s]
            sign = (1 - 2 * (response % 2)).astype(f32)
            contrib = contrib + jnp.where(ids == response // 2, sign * sums_s[s][0:4], 0.0)
        contrib_ref[...] = jnp.broadcast_to(contrib[None], contrib_ref.shape)


def masked(scores):
    j = lax.broadcasted_iota(jnp.int32, (TOKENS, WIDTH), 0)
    t = lax.broadcasted_iota(jnp.int32, (TOKENS, WIDTH), 1) % TOKENS
    return jnp.concatenate([scores[:512], jnp.where(j <= t, scores[512:], -1e30)], axis=0)


def backward_kernel(
    response_ref, lengths_ref, pair_prompt_ref, place_ref,
    stats_ref, q_ref, r_ref, own_ref, near_ref, far_ref,
    dq_ref, down_ref, load_ref,
    key_s, value_s, q_s, r_s, probs_s, dscores_s,
):
    slot = pl.program_id(0)
    group = pl.program_id(1)
    response = response_ref[slot]
    prompt = pair_prompt_ref[response // 2]
    mine = place_ref[0]
    fill(key_s, near_ref, far_ref, own_ref, prompt, group * HEAD)
    fill(value_s, near_ref, far_ref, own_ref, prompt, (KEY_VALUE_HEADS + group) * HEAD)
    stack(q_ref, r_ref, q_s, r_s, lengths_ref[response])
    scores = lax.dot_general(key_s[...], q_s[...], NT, preferred_element_type=f32)
    dprobs = lax.dot_general(value_s[...], r_s[...], NT, preferred_element_type=f32)
    at = slot * KEY_VALUE_HEADS + group
    top, share, delta = (stats_ref[at, i : i + 1, :] for i in range(3))
    probs = jnp.exp2((masked(scores) - top) * LOG2_SCALE) * share
    probs_s[...] = probs.astype(bf16)
    dscores_s[...] = (probs * (dprobs - delta)).astype(bf16)
    dkey = lax.dot_general(dscores_s[...], q_s[...], NN, preferred_element_type=f32) * SCALE
    dvalue = lax.dot_general(probs_s[...], r_s[...], NN, preferred_element_type=f32)
    dq = lax.dot_general(key_s[...].T, dscores_s[...], NN, preferred_element_type=f32) * SCALE
    for h in range(GROUP):
        part = slice(h * HEAD, (h + 1) * HEAD)
        dq_ref[0, :, part] = dq[:, part].T.astype(bf16)
    for i, grad in enumerate((dkey, dvalue)):
        grad = grad.astype(bf16)
        part = i * KEY_VALUE_HEADS + group
        down_ref[0, :, pl.ds(pl.multiple_of(part * HEAD, HEAD), HEAD)] = grad[512:]
        rows = pl.ds(pl.multiple_of(slot * 256, 256), 256)
        for core in range(2):
            dest = jnp.bitwise_xor(mine, core) * 4 + part
            load_ref[dest, rows, :] = grad[core * 256 : (core + 1) * 256]


def whole(shape):
    return pl.BlockSpec(shape, lambda s, g, *_: (0,) * len(shape))


def by_slot(shape):
    return pl.BlockSpec(shape, lambda s, g, *_: (s, 0, 0))


def by_group(shape):
    return pl.BlockSpec(shape, lambda s, g, *_: (s, 0, g))


def forward(slot_response, lengths, pair_prompt, queries, readout, own, near, far):
    return pl.pallas_call(
        forward_kernel,
        out_shape=(
            jax.ShapeDtypeStruct((4, 8, WIDTH), f32),
            jax.ShapeDtypeStruct((64, 4, HEAD), f32),
        ),
        grid_spec=pltpu.PrefetchScalarGridSpec(
            num_scalar_prefetch=3,
            grid=(2, 2),
            in_specs=[
                by_group((1, TOKENS, WIDTH)),
                by_group((1, TOKENS, WIDTH)),
                by_slot((1, TOKENS, 512)),
                whole((8, 2, 32, 512)),
                whole((8, 2, 32, 512)),
            ],
            out_specs=[
                whole((4, 8, WIDTH)),
                whole((64, 4, HEAD)),
            ],
            scratch_shapes=[
                pltpu.VMEM((KEYS, HEAD), bf16),
                pltpu.VMEM((KEYS, HEAD), bf16),
                pltpu.VMEM((WIDTH, HEAD), bf16),
                pltpu.VMEM((WIDTH, HEAD), bf16),
                pltpu.VMEM((2, 8, HEAD), f32),
            ],
        ),
        compiler_params=pltpu.CompilerParams(vmem_limit_bytes=52 << 20),
        cost_estimate=pl.CostEstimate(
            flops=1_200_000_000, bytes_accessed=4_000_000, transcendentals=2_300_000
        ),
        name="forward",
    )(slot_response, lengths, pair_prompt, queries, readout, own, near, far)


def backward(
    slot_response, lengths, pair_prompt, place, stats, queries, readout, own, near, far
):
    return pl.pallas_call(
        backward_kernel,
        out_shape=(
            jax.ShapeDtypeStruct((2, TOKENS, QUERY_HEADS * HEAD), bf16),
            jax.ShapeDtypeStruct((2, TOKENS, 512), bf16),
            jax.ShapeDtypeStruct((8, LOAD_ROWS, HEAD), bf16),
        ),
        grid_spec=pltpu.PrefetchScalarGridSpec(
            num_scalar_prefetch=4,
            grid=(2, 2),
            in_specs=[
                whole((4, 8, WIDTH)),
                by_group((1, TOKENS, WIDTH)),
                by_group((1, TOKENS, WIDTH)),
                by_slot((1, TOKENS, 512)),
                whole((8, 2, 32, 512)),
                whole((8, 2, 32, 512)),
            ],
            out_specs=[
                by_group((1, TOKENS, WIDTH)),
                by_slot((1, TOKENS, 512)),
                whole((8, LOAD_ROWS, HEAD)),
            ],
            scratch_shapes=[
                pltpu.VMEM((KEYS, HEAD), bf16),
                pltpu.VMEM((KEYS, HEAD), bf16),
                pltpu.VMEM((WIDTH, HEAD), bf16),
                pltpu.VMEM((WIDTH, HEAD), bf16),
                pltpu.VMEM((KEYS, WIDTH), bf16),
                pltpu.VMEM((KEYS, WIDTH), bf16),
            ],
        ),
        compiler_params=pltpu.CompilerParams(vmem_limit_bytes=52 << 20),
        cost_estimate=pl.CostEstimate(
            flops=3_000_000_000, bytes_accessed=6_000_000, transcendentals=2_300_000
        ),
        name="backward",
    )(slot_response, lengths, pair_prompt, place, stats, queries, readout, own, near, far)


def news_kernel(response_ref, contribs_ref, load_ref, out_ref, news_s, sems):
    share = contribs_ref[0]
    for i in range(1, 64):
        share = share + contribs_ref[i]
    high = share.astype(bf16).astype(f32)
    middle = (share - high).astype(bf16).astype(f32)
    low = share - high - middle
    names = []
    for slot in range(2):
        response = response_ref[slot]
        for part in (response // 32, response % 32):
            names.append(jnp.full((1, HEAD), part.astype(f32)))
    news_s[...] = jnp.concatenate([high, middle, low, *names], axis=0).astype(bf16)
    copies = [
        pltpu.make_async_copy(news_s, out_ref.at[i, 512:528], sems.at[i]) for i in range(8)
    ]
    for copy in copies:
        copy.start()
    for copy in copies:
        copy.wait()


def with_news(slot_response, contribs, load):
    return pl.pallas_call(
        news_kernel,
        out_shape=jax.ShapeDtypeStruct(load.shape, bf16),
        in_specs=[
            pl.BlockSpec(memory_space=pltpu.SMEM),
            pl.BlockSpec(memory_space=pltpu.VMEM),
            pl.BlockSpec(memory_space=pltpu.HBM),
        ],
        out_specs=pl.BlockSpec(memory_space=pltpu.HBM),
        scratch_shapes=[pltpu.VMEM((16, HEAD), bf16), pltpu.SemaphoreType.DMA((8,))],
        input_output_aliases={2: 0},
        compiler_params=pltpu.CompilerParams(vmem_limit_bytes=58 << 20),
        name="news",
    )(slot_response, contribs, load)


def weigh_kernel(ref_margin_ref, pair_prompt_ref, load_ref, margins_ref, weights_ref, out_ref, factor_s):
    pair_sums = jnp.zeros((4, HEAD), f32)
    names = []
    for source in range(8):
        n = load_ref[source, 512:528, :].astype(f32)
        pair_sums = pair_sums + (n[0:4] + n[4:8] + n[8:12])
        names += [n[12:13] * 32.0 + n[13:14], n[14:15] * 32.0 + n[15:16]]
    margins = MARGIN_BETA * (pair_sums - ref_margin_ref[...])
    margins_ref[...] = margins
    weights = -LOSS_SCALE * MARGIN_BETA * jax.nn.sigmoid(-margins)
    weights_ref[...] = weights
    responses = jnp.concatenate(names, axis=0).astype(jnp.int32)
    sign = (1 - 2 * (responses % 2)).astype(f32)
    lane = lax.broadcasted_iota(jnp.int32, (16, HEAD), 1)
    for p in range(2):
        table = jnp.where(pair_prompt_ref[...] == p, weights, 0.0)
        found = jnp.zeros((16, HEAD), f32)
        for k in range(4):
            found = jnp.where(responses // 2 == lane + k * HEAD, table[k : k + 1], found)
        factor_s[p] = sign * jnp.sum(found, axis=1, keepdims=True)

    def step(z, _):
        sums = [jnp.zeros((32, HEAD), f32) for _ in range(2)]
        for source in range(8):
            for slot in range(2):
                rows = pl.ds(pl.multiple_of(slot * 256 + z * 32, 32), 32)
                piece = load_ref[source, rows, :].astype(f32)
                at = source * 2 + slot
                for p in range(2):
                    sums[p] = sums[p] + factor_s[p, at : at + 1, :] * piece
        for p in range(2):
            out_ref[z, :, p] = sums[p].reshape(8, 4, HEAD).astype(bf16)
        return 0

    lax.fori_loop(0, 8, step, 0)


def weigh(ref_margin, pair_prompt, load):
    vmem = pl.BlockSpec(memory_space=pltpu.VMEM)
    return pl.pallas_call(
        weigh_kernel,
        out_shape=(
            jax.ShapeDtypeStruct((4, HEAD), f32),
            jax.ShapeDtypeStruct((4, HEAD), f32),
            jax.ShapeDtypeStruct((8, 8, 2, 4, HEAD), bf16),
        ),
        in_specs=[vmem, vmem, vmem],
        out_specs=(vmem, vmem, vmem),
        scratch_shapes=[pltpu.VMEM((2, 16, HEAD), f32)],
        compiler_params=pltpu.CompilerParams(vmem_limit_bytes=8 << 20),
        name="weigh",
    )(ref_margin, pair_prompt, load)


def join_kernel(parts_ref, out_ref):
    total = parts_ref[0].astype(f32)
    for i in range(1, 64):
        total = total + parts_ref[i].astype(f32)
    out_ref[...] = jnp.broadcast_to(total.astype(bf16)[None], out_ref.shape)


def join(parts):
    vmem = pl.BlockSpec(memory_space=pltpu.VMEM)
    return pl.pallas_call(
        join_kernel,
        out_shape=jax.ShapeDtypeStruct((32, 8, HEAD), bf16),
        in_specs=[vmem],
        out_specs=vmem,
        compiler_params=pltpu.CompilerParams(vmem_limit_bytes=8 << 20),
        name="join",
    )(parts)


def to_all(pieces, axes):
    return lax.all_to_all(pieces, axes, 0, 0, tiled=True)


def copies_to_all(shard, axes):
    size = lax.axis_size(axes)
    return to_all(jnp.broadcast_to(shard[None], (size, *shard.shape)), axes)


def on_device(
    prompt_kv, response_queries, resp_kv, readout, slot_response, lengths, pair_prompt, ref_margin
):
    near = copies_to_all(prompt_kv, "z")
    far = lax.ppermute(near, "c", [(0, 1), (1, 0)])
    place = lax.axis_index("c").astype(jnp.int32)[None]
    data = (response_queries, readout, resp_kv, near, far)
    stats, contrib = forward(slot_response, lengths, pair_prompt, *data)
    contribs = to_all(contrib, APART)
    dq, down, load = backward(slot_response, lengths, pair_prompt, place, stats, *data)
    load = to_all(with_news(slot_response, contribs, load), CLOSE)
    margins, weights, parts = weigh(
        ref_margin.reshape(4, HEAD), pair_prompt.reshape(4, HEAD), load
    )
    pairs = jnp.arange(ref_margin.shape[0])
    sign = 1.0 - 2.0 * (slot_response % 2).astype(f32)
    found = jnp.where((slot_response // 2)[:, None] == pairs, weights.reshape(1, -1), 0.0)
    own = (jnp.sum(found, axis=1) * sign)[:, None, None]
    grad_q = (own * dq.astype(f32)).astype(bf16)
    grad_own = (own * down.astype(f32)).astype(bf16)
    total = join(to_all(parts.reshape(64, 8, HEAD), APART))
    total = to_all(total, RESP).reshape(8, 4, 2, 4, HEAD)
    grad_prompt = jnp.transpose(total, (2, 0, 3, 1, 4)).reshape(2, 32, 512)
    return margins.reshape(-1), grad_q, grad_own, grad_prompt


def solution(mesh):
    split = Mesh(mesh.devices.reshape(8, 2, 8, 4), EVERY)
    in_specs = (
        P(None, PREFIX, None),
        P(EVERY, None, None),
        P(EVERY, None, None),
        P(EVERY, None, None),
        P(EVERY),
        P(),
        P(),
        P(),
    )
    out_specs = (P(), P(EVERY, None, None), P(EVERY, None, None), P(None, PREFIX, None))
    return jax.shard_map(
        on_device, mesh=split, in_specs=in_specs, out_specs=out_specs, check_vma=False
    )
```

time: 127 us -> 123 us (0.969)
  Pallas kernels: 24.3 us -> 20.9 us
    pallas_call x1, Pallas kernels: 11 us -> 7.31 us  [forward(): pl.pallas_call(forward_kernel, out_shape=(jax.ShapeDtypeStruct((4, 8, WID...]
where the time goes in v3:
time: 123 us; the launch traced here: 122 us
  waiting for transfers between devices  39.1 us (32%)
  starting transfers between devices  29.5 us (24%)
  blocking collectives  27.6 us (22%)
  Pallas kernels  20.9 us (17%)
  local copies, waits for them, and re-layouts  2.31 us (2%)
  other arithmetic  2.17 us (2%)
    all_to_all x4, waiting for transfers between devices, to_all(): return lax.all_to_all(pieces, axes, 0, 0, tiled=True)  37.2 us
    all_to_all x1, blocking collectives, to_all(): return lax.all_to_all(pieces, axes, 0, 0, tiled=True)  27.6 us
    all_to_all x4, starting transfers between devices, to_all(): return lax.all_to_all(pieces, axes, 0, 0, tiled=True)  27.6 us
    pallas_call x1, Pallas kernels, backward(): pl.pallas_call(backward_kernel, out_shape=(jax.ShapeDtypeStruct((2, TOKEN...  9.96 us
    pallas_call x1, Pallas kernels, forward(): pl.pallas_call(forward_kernel, out_shape=(jax.ShapeDtypeStruct((4, 8, WID...  7.31 us
  transfers between devices with their start and end apart: 5, of which 5 were waited for; matrix products, arithmetic and copies ran while one was open for 2% of the time, Pallas kernels for 8%

profile of v3, /device:TPU:8, one launch (start us, length us, event | category | flops | bytes accessed | tf_op | source)
XLA Modules:
  0.0 122.3 jit_solution(3048905247981574039)
XLA Ops:
  0.6 0.0 copy-start.2
  0.7 0.9 broadcast_in_dim.26
  1.6 27.6 %all_to_all.25.near_ref = bf16[8,2,32,512]{3,2,1,0:T(8,128)(2,1)S(1)} all-to-all(bf16[8,2,32,512]{3,2,1,0:T(8,128)(2,1)S(1)} %broadcast_in_dim.26), channel_id=1, replica_groups=mesh['z'=8,'c'=2,'y'=8,'x'=4] {'z'}, dimensions={0} | all-to-all | bytes 1048576 | tf_op jit(solution)/shard_map/all_to_all | solution.py:348
  29.2 1.9 %collective-permute-start = (bf16[8,2,32,512]{3,2,1,0:T(8,128)(2,1)S(1)}, bf16[8,2,32,512]{3,2,1,0:T(8,128)(2,1)S(1)}, u32[]{:S(2)}, u32[]{:S(2)}) collective-permute-start(bf16[8,2,32,512]{3,2,1,0:T(8,128)(2,1)S(1)} %all_to_all.25.near_ref), channel_id=1, source_target_pairs={{0,32},{32,0},{1,33},{33,1},{2,34},{34,2},{3,35},{35,3},{4,36},{36... | collective-permute-start | bytes 1572872 | tf_op jit(solution)/shard_map/ppermute | solution.py:360
  31.1 1.9 %collective-permute-done.far_ref = bf16[8,2,32,512]{3,2,1,0:T(8,128)(2,1)S(1)} collective-permute-done((bf16[8,2,32,512]{3,2,1,0:T(8,128)(2,1)S(1)}, bf16[8,2,32,512]{3,2,1,0:T(8,128)(2,1)S(1)}, u32[]{:S(2)}, u32[]{:S(2)}) %collective-permute-start) | collective-permute-done | bytes 524320 | tf_op jit(solution)/shard_map/ppermute | solution.py:360
  33.0 7.3 %forward.1 = (f32[4,8,896]{2,1,0:T(8,128)S(1)}, f32[64,4,128]{2,1,0:T(4,128)}) custom-call(s32[2]{0:T(128)S(1)} %copy-done.2, s32[1024]{0:T(1024)S(1)} %copy-done.5, s32[512]{0:T(512)S(1)} %copy-done.1, bf16[2,128,1792]{2,1,0:T(8,128)(2,1)} %q_ref.3, bf16[2,128,1792]{2,1,0:T(8,128)(2,1)} %r_ref.3, bf16[2,128,512]{2,1,0:T(8,128)(2,1)S(1)} %copy-done.4, ...), custom_call_target="tpu_custom_call" | custom-call | flops 1200000000 | bytes 4000000 | tf_op jit(solution)/shard_map/forward/pallas_call | solution.py:156
  40.3 8.1 %all-to-all-start.1 = ((f32[64,4,128]{2,1,0:T(4,128)}), f32[64,4,128]{2,1,0:T(4,128)S(1)}, u32[]{:S(2)}, u32[]{:S(2)}) async-start(f32[64,4,128]{2,1,0:T(4,128)} %get-tuple-element.12), calls=%async_computation.1 | async-start | bytes 262144 | tf_op jit(solution)/shard_map/all_to_all | solution.py:348
  48.5 10.0 %backward.1 = (bf16[2,128,1792]{2,1,0:T(8,128)(2,1)}, bf16[2,128,512]{2,1,0:T(8,128)(2,1)S(1)}, bf16[8,528,128]{2,1,0:T(8,128)(2,1)}) custom-call(s32[2]{0:T(128)S(1)} %copy-done.2, s32[1024]{0:T(1024)S(1)} %copy-done.5, s32[512]{0:T(512)S(1)} %copy-done.1, s32[1]{0:T(128)} %bitcast.2.place_ref, f32[4,8,896]{2,1,0:T(8,128)S(1)} %get-tuple-element.13.stats_ref, ...), custom_call_target="tpu_custom_call" | custom-call | flops 3000000000 | bytes 6000000 | tf_op jit(solution)/shard_map/backward/pallas_call | solution.py:195
  58.4 2.2 %all-to-all-done.1.contribs_ref = f32[64,4,128]{2,1,0:T(4,128)S(1)} async-done(((f32[64,4,128]{2,1,0:T(4,128)}), f32[64,4,128]{2,1,0:T(4,128)S(1)}, u32[]{:S(2)}, u32[]{:S(2)}) %all-to-all-start.1) | async-done | bytes 131104 | tf_op jit(solution)/shard_map/all_to_all | solution.py:348
  60.6 0.7 copy-done.7
  61.3 1.7 %news.1 = bf16[8,528,128]{2,1,0:T(8,128)(2,1)} custom-call(s32[2]{0:T(128)} %response_ref.5, f32[64,4,128]{2,1,0:T(4,128)} %copy-done.7, bf16[8,528,128]{2,1,0:T(8,128)(2,1)} %get-tuple-element.14.load_ref), custom_call_target="tpu_custom_call", output_to_operand_aliasing={{}: (2, {})} | custom-call | tf_op jit(solution)/shard_map/news/pallas_call | solution.py:258
  63.0 0.0 copy-start.3
  63.0 4.3 %all-to-all-start.2 = ((bf16[8,528,128]{2,1,0:T(8,128)(2,1)}), bf16[8,528,128]{2,1,0:T(8,128)(2,1)S(1)}, u32[]{:S(2)}, u32[]{:S(2)}) async-start(bf16[8,528,128]{2,1,0:T(8,128)(2,1)} %news.1), calls=%async_computation.2 | async-start | bytes 2162688 | tf_op jit(solution)/shard_map/all_to_all | solution.py:348
  67.4 15.7 %all-to-all-done.2.load_ref = bf16[8,528,128]{2,1,0:T(8,128)(2,1)S(1)} async-done(((bf16[8,528,128]{2,1,0:T(8,128)(2,1)}), bf16[8,528,128]{2,1,0:T(8,128)(2,1)S(1)}, u32[]{:S(2)}, u32[]{:S(2)}) %all-to-all-start.2) | async-done | bytes 1081376 | tf_op jit(solution)/shard_map/all_to_all | solution.py:348
  83.0 1.3 %weigh.1 = (f32[4,128]{1,0:T(4,128)}, f32[4,128]{1,0:T(4,128)S(1)}, bf16[8,8,2,4,128]{4,3,2,1,0:T(4,128)(2,1)}) custom-call(f32[4,128]{1,0:T(4,128)S(1)} %bitcast.9, s32[4,128]{1,0:T(4,128)S(1)} %bitcast.10, bf16[8,528,128]{2,1,0:T(8,128)(2,1)S(1)} %all-to-all-done.2.load_ref), custom_call_target="tpu_custom_call" | custom-call | tf_op jit(solution)/shard_map/weigh/pallas_call | solution.py:313
  84.3 0.2 fusion
  84.5 10.5 %all-to-all-start.3 = ((bf16[64,8,128]{2,1,0:T(8,128)(2,1)}), bf16[64,8,128]{2,1,0:T(8,128)(2,1)S(1)}, u32[]{:S(2)}, u32[]{:S(2)}) async-start(bf16[64,8,128]{2,1,0:T(8,128)(2,1)} %bitcast.5), calls=%async_computation.3 | async-start | bytes 262144 | tf_op jit(solution)/shard_map/all_to_all | solution.py:348
  95.0 1.1 multiply_convert_fusion
  96.1 11.0 %all-to-all-done.3.parts_ref = bf16[64,8,128]{2,1,0:T(8,128)(2,1)S(1)} async-done(((bf16[64,8,128]{2,1,0:T(8,128)(2,1)}), bf16[64,8,128]{2,1,0:T(8,128)(2,1)S(1)}, u32[]{:S(2)}, u32[]{:S(2)}) %all-to-all-start.3) | async-done | bytes 131104 | tf_op jit(solution)/shard_map/all_to_all | solution.py:348
  107.2 0.7 join.1
  107.9 4.7 %all-to-all-start.4 = ((bf16[32,8,128]{2,1,0:T(8,128)(2,1)}), bf16[32,8,128]{2,1,0:T(8,128)(2,1)S(1)}, u32[]{:S(2)}, u32[]{:S(2)}) async-start(bf16[32,8,128]{2,1,0:T(8,128)(2,1)} %join.1), calls=%async_computation.4 | async-start | bytes 131072 | tf_op jit(solution)/shard_map/all_to_all | solution.py:348
  112.6 0.8 multiply_convert_fusion.1
  113.4 8.3 %all-to-all-done.4 = bf16[32,8,128]{2,1,0:T(8,128)(2,1)S(1)} async-done(((bf16[32,8,128]{2,1,0:T(8,128)(2,1)}), bf16[32,8,128]{2,1,0:T(8,128)(2,1)S(1)}, u32[]{:S(2)}, u32[]{:S(2)}) %all-to-all-start.4) | async-done | bytes 65568 | tf_op jit(solution)/shard_map/all_to_all | solution.py:348
  121.7 0.7 reshape.36
  (16 shorter events, 0.1 us)
Async XLA Ops:
  0.6 32.4 %copy-start.1 = (s32[512]{0:T(512)S(1)}, s32[512]{0:T(512)}, u32[]{:S(2)}) copy-start(s32[512]{0:T(512)} %pair_prompt_ref.3) | copy-start | bytes 6148
  0.6 32.4 %copy-start.2 = (s32[2]{0:T(128)S(1)}, s32[2]{0:T(128)}, u32[]{:S(2)}) copy-start(s32[2]{0:T(128)} %response_ref.5) | copy-start | bytes 28
  0.7 32.4 %copy-start.5 = (s32[1024]{0:T(1024)S(1)}, s32[1024]{0:T(1024)}, u32[]{:S(2)}) copy-start(s32[1024]{0:T(1024)} %lengths_ref.3) | copy-start | bytes 12292
  0.7 32.4 %copy-start.4 = (bf16[2,128,512]{2,1,0:T(8,128)(2,1)S(1)}, bf16[2,128,512]{2,1,0:T(8,128)(2,1)}, u32[]{:S(2)}) copy-start(bf16[2,128,512]{2,1,0:T(8,128)(2,1)} %own_ref.3) | copy-start | bytes 786436
  29.2 3.8 %collective-permute-start = (bf16[8,2,32,512]{3,2,1,0:T(8,128)(2,1)S(1)}, bf16[8,2,32,512]{3,2,1,0:T(8,128)(2,1)S(1)}, u32[]{:S(2)}, u32[]{:S(2)}) collective-permute-start(bf16[8,2,32,512]{3,2,1,0:T(8,128)(2,1)S(1)} %all_to_all.25.near_ref), channel_id=1, source_target_pairs={{0,32},{32,0},{1,33},{33,1},{2,34},{34,2},{3,35},{35,3},{4,36},{36... | collective-permute-start | bytes 1572872 | tf_op jit(solution)/shard_map/ppermute | solution.py:360
  40.3 20.3 %all-to-all-start.1 = ((f32[64,4,128]{2,1,0:T(4,128)}), f32[64,4,128]{2,1,0:T(4,128)S(1)}, u32[]{:S(2)}, u32[]{:S(2)}) async-start(f32[64,4,128]{2,1,0:T(4,128)} %get-tuple-element.12), calls=%async_computation.1 | async-start | bytes 262144 | tf_op jit(solution)/shard_map/all_to_all | solution.py:348
  60.6 0.7 copy-start.7
  63.0 4.3 %copy-start.3 = (s32[2]{0:T(128)S(1)}, s32[2]{0:T(128)}, u32[]{:S(2)}) copy-start(s32[2]{0:T(128)} %response_ref.5) | copy-start | bytes 28
  63.0 20.0 %copy-start = (f32[512]{0:T(512)S(1)}, f32[512]{0:T(512)}, u32[]{:S(2)}) copy-start(f32[512]{0:T(512)} %param.15) | copy-start | bytes 6148
  63.0 20.0 %all-to-all-start.2 = ((bf16[8,528,128]{2,1,0:T(8,128)(2,1)}), bf16[8,528,128]{2,1,0:T(8,128)(2,1)S(1)}, u32[]{:S(2)}, u32[]{:S(2)}) async-start(bf16[8,528,128]{2,1,0:T(8,128)(2,1)} %news.1), calls=%async_computation.2 | async-start | bytes 2162688 | tf_op jit(solution)/shard_map/all_to_all | solution.py:348
  67.3 27.7 %copy-start.6 = (bf16[2,128,1792]{2,1,0:T(8,128)(2,1)S(1)}, bf16[2,128,1792]{2,1,0:T(8,128)(2,1)}, u32[]{:S(2)}) copy-start(bf16[2,128,1792]{2,1,0:T(8,128)(2,1)} %get-tuple-element.17) | copy-start | bytes 2752516
  84.5 22.7 %all-to-all-start.3 = ((bf16[64,8,128]{2,1,0:T(8,128)(2,1)}), bf16[64,8,128]{2,1,0:T(8,128)(2,1)S(1)}, u32[]{:S(2)}, u32[]{:S(2)}) async-start(bf16[64,8,128]{2,1,0:T(8,128)(2,1)} %bitcast.5), calls=%async_computation.3 | async-start | bytes 262144 | tf_op jit(solution)/shard_map/all_to_all | solution.py:348
  107.9 13.7 %all-to-all-start.4 = ((bf16[32,8,128]{2,1,0:T(8,128)(2,1)}), bf16[32,8,128]{2,1,0:T(8,128)(2,1)S(1)}, u32[]{:S(2)}, u32[]{:S(2)}) async-start(bf16[32,8,128]{2,1,0:T(8,128)(2,1)} %join.1), calls=%async_computation.4 | async-start | bytes 131072 | tf_op jit(solution)/shard_map/all_to_all | solution.py:348

commit v4 on v3

v4 whole, which is shorter than its diff:
```python
import math

import jax
import jax.numpy as jnp
from jax import lax
from jax.experimental import pallas as pl
from jax.experimental.pallas import tpu as pltpu
from jax.sharding import Mesh
from jax.sharding import PartitionSpec as P

QUERY_HEADS = 14
KEY_VALUE_HEADS = 2
HEAD = 128
GROUP = QUERY_HEADS // KEY_VALUE_HEADS
TOKENS = 128
WIDTH = GROUP * HEAD
KEYS = 640
SCALE = HEAD**-0.5
LOG2_SCALE = SCALE * math.log2(math.e)
MARGIN_BETA = 0.1
LOSS_SCALE = 256.0
EVERY = ("z", "c", "y", "x")
PREFIX = ("z", "c")
RESP = ("y", "x")
CLOSE = ("c", "x")
APART = ("z", "y")
LOAD_ROWS = 528
GRANT = 52
NT = (((1,), (1,)), ((), ()))
NN = (((1,), (0,)), ((), ()))
bf16 = jnp.bfloat16
f32 = jnp.float32


def pair_grid():
    ids = lax.broadcasted_iota(jnp.int32, (4, HEAD), 0) * HEAD
    return ids + lax.broadcasted_iota(jnp.int32, (4, HEAD), 1)


def fill(dest, near_ref, far_ref, prompt, column):
    at = pl.ds(pl.multiple_of(column, HEAD), HEAD)
    dest[0:256, :] = near_ref[:, prompt, :, at].reshape(256, HEAD)
    dest[256:512, :] = far_ref[:, prompt, :, at].reshape(256, HEAD)


def dots(keys, values, q, r):
    scores = lax.dot_general(keys, q, NT, preferred_element_type=f32)
    return scores, lax.dot_general(values, r, NT, preferred_element_type=f32)


def causal(scores):
    j = lax.broadcasted_iota(jnp.int32, (TOKENS, WIDTH), 0)
    t = lax.broadcasted_iota(jnp.int32, (TOKENS, WIDTH), 1) % TOKENS
    return jnp.where(j <= t, scores, -1e30)


def own_part(own_ref, group, is_value):
    column = (is_value * KEY_VALUE_HEADS + group) * HEAD
    return own_ref[0, :, pl.ds(pl.multiple_of(column, HEAD), HEAD)]


def prepare_kernel(
    response_ref, lengths_ref, q_ref, r_ref, own_ref, q_out, r_out, stats_ref
):
    group = pl.program_id(1)
    length = lengths_ref[response_ref[pl.program_id(0)]]
    live = lax.broadcasted_iota(jnp.int32, (TOKENS, HEAD), 0) < length
    for h in range(GROUP):
        rows = slice(h * TOKENS, (h + 1) * TOKENS)
        columns = slice(h * HEAD, (h + 1) * HEAD)
        q_out[0, rows, :] = q_ref[0, :, columns]
        r_out[0, rows, :] = jnp.where(live, r_ref[0, :, columns], jnp.zeros((), bf16))
    scores, dprobs = dots(
        own_part(own_ref, group, 0), own_part(own_ref, group, 1), q_out[0], r_out[0]
    )
    scores = causal(scores)
    top = jnp.max(scores, axis=0, keepdims=True)
    weight = jnp.exp2((scores - top) * LOG2_SCALE)
    stats_ref[0, 0:1, :] = top
    stats_ref[0, 1:2, :] = jnp.sum(weight, axis=0, keepdims=True)
    stats_ref[0, 2:3, :] = jnp.sum(weight * dprobs, axis=0, keepdims=True)


def forward_kernel(
    response_ref, pair_prompt_ref, q_ref, r_ref, part_ref, near_ref, far_ref,
    stats_ref, contrib_ref, key_s, value_s, sums_s,
):
    slot = pl.program_id(0)
    group = pl.program_id(1)
    prompt = pair_prompt_ref[response_ref[slot] // 2]
    fill(key_s, near_ref, far_ref, prompt, group * HEAD)
    fill(value_s, near_ref, far_ref, prompt, (KEY_VALUE_HEADS + group) * HEAD)
    top, total, delta = (part_ref[0, i : i + 1, :] for i in range(3))
    for start in range(0, 512, 128):
        keys = slice(start, start + 128)
        scores, dprobs = dots(key_s[keys, :], value_s[keys, :], q_ref[0], r_ref[0])
        higher = jnp.maximum(top, jnp.max(scores, axis=0, keepdims=True))
        weight = jnp.exp2((scores - higher) * LOG2_SCALE)
        fade = jnp.exp2((top - higher) * LOG2_SCALE)
        total = total * fade + jnp.sum(weight, axis=0, keepdims=True)
        delta = delta * fade + jnp.sum(weight * dprobs, axis=0, keepdims=True)
        top = higher
    share = 1.0 / total
    delta = delta * share
    stats_ref[0, 0:1, :] = top
    stats_ref[0, 1:2, :] = share
    stats_ref[0, 2:3, :] = delta
    total = jnp.sum(delta, axis=1, keepdims=True)

    @pl.when(group == 0)
    def _():
        sums_s[slot] = jnp.broadcast_to(total, (8, HEAD))

    @pl.when(group == 1)
    def _():
        sums_s[slot] = sums_s[slot] + total

    @pl.when((slot == 1) & (group == 1))
    def _():
        ids = pair_grid()
        contrib = jnp.zeros((4, HEAD), f32)
        for s in range(2):
            response = response_ref[s]
            sign = (1 - 2 * (response % 2)).astype(f32)
            contrib = contrib + jnp.where(ids == response // 2, sign * sums_s[s][0:4], 0.0)
        contrib_ref[...] = jnp.broadcast_to(contrib[None], contrib_ref.shape)


def backward_parts(scores, dprobs, stats_ref):
    top, share, delta = (stats_ref[0, i : i + 1, :] for i in range(3))
    probs = jnp.exp2((scores - top) * LOG2_SCALE) * share
    return probs.astype(bf16), (probs * (dprobs - delta)).astype(bf16)


def backward_kernel(
    response_ref, pair_prompt_ref, place_ref, q_ref, r_ref, stats_ref, near_ref, far_ref,
    load_ref, key_s, value_s, probs_s, dscores_s,
):
    slot = pl.program_id(0)
    group = pl.program_id(1)
    prompt = pair_prompt_ref[response_ref[slot] // 2]
    mine = place_ref[0]
    fill(key_s, near_ref, far_ref, prompt, group * HEAD)
    fill(value_s, near_ref, far_ref, prompt, (KEY_VALUE_HEADS + group) * HEAD)
    scores, dprobs = dots(key_s[...], value_s[...], q_ref[0], r_ref[0])
    probs_s[...], dscores_s[...] = backward_parts(scores, dprobs, stats_ref)
    dkey = lax.dot_general(dscores_s[...], q_ref[0], NN, preferred_element_type=f32) * SCALE
    dvalue = lax.dot_general(probs_s[...], r_ref[0], NN, preferred_element_type=f32)
    rows = pl.ds(pl.multiple_of(slot * 256, 256), 256)
    for i, grad in enumerate((dkey, dvalue)):
        grad = grad.astype(bf16)
        for core in range(2):
            dest = jnp.bitwise_xor(mine, core) * 4 + i * KEY_VALUE_HEADS + group
            load_ref[dest, rows, :] = grad[core * 256 : (core + 1) * 256]


def finish_kernel(
    response_ref, pair_prompt_ref, q_ref, r_ref, stats_ref, near_ref, far_ref, own_ref,
    dq_ref, down_ref, done_ref, key_s, value_s, probs_s, dscores_s,
):
    group = pl.program_id(1)
    prompt = pair_prompt_ref[response_ref[pl.program_id(0)] // 2]
    fill(key_s, near_ref, far_ref, prompt, group * HEAD)
    fill(value_s, near_ref, far_ref, prompt, (KEY_VALUE_HEADS + group) * HEAD)
    key_s[512:640, :] = own_part(own_ref, group, 0)
    value_s[512:640, :] = own_part(own_ref, group, 1)
    scores, dprobs = dots(key_s[...], value_s[...], q_ref[0], r_ref[0])
    scores = jnp.concatenate([scores[:512], causal(scores[512:])], axis=0)
    probs, dscores_s[...] = backward_parts(scores, dprobs, stats_ref)
    probs_s[...] = probs[512:]
    dq = lax.dot_general(key_s[...].T, dscores_s[...], NN, preferred_element_type=f32) * SCALE
    for h in range(GROUP):
        part = slice(h * HEAD, (h + 1) * HEAD)
        dq_ref[0, :, part] = dq[:, part].T.astype(bf16)
    dkey = lax.dot_general(dscores_s[512:640, :], q_ref[0], NN, preferred_element_type=f32)
    dvalue = lax.dot_general(probs_s[...], r_ref[0], NN, preferred_element_type=f32)
    column = pl.multiple_of(group * HEAD, HEAD)
    down_ref[0, :, pl.ds(column, HEAD)] = (dkey * SCALE).astype(bf16)
    column = pl.multiple_of((KEY_VALUE_HEADS + group) * HEAD, HEAD)
    down_ref[0, :, pl.ds(column, HEAD)] = dvalue.astype(bf16)
    done_ref[...] = jnp.zeros((8, HEAD), f32)


def whole(shape):
    return pl.BlockSpec(shape, lambda s, g, *_: (0,) * len(shape))


def by_slot(shape):
    return pl.BlockSpec(shape, lambda s, g, *_: (s, 0, 0))


def by_group(shape):
    return pl.BlockSpec(shape, lambda s, g, *_: (s, 0, g))


def by_both(shape):
    return pl.BlockSpec(shape, lambda s, g, *_: (s * 2 + g, 0, 0))


VMEM = pl.BlockSpec(memory_space=pltpu.VMEM)
STACK = by_both((1, WIDTH, HEAD))
STATS = by_both((1, 8, WIDTH))
STACK_SHAPE = jax.ShapeDtypeStruct((4, WIDTH, HEAD), bf16)
STATS_SHAPE = jax.ShapeDtypeStruct((4, 8, WIDTH), f32)


def per_group(kernel, name, scalars, arrays, in_specs, out_specs, out_shape, scratch, flops, exps):
    return pl.pallas_call(
        kernel,
        out_shape=out_shape,
        grid_spec=pltpu.PrefetchScalarGridSpec(
            num_scalar_prefetch=len(scalars),
            grid=(2, 2),
            in_specs=in_specs,
            out_specs=out_specs,
            scratch_shapes=scratch,
        ),
        compiler_params=pltpu.CompilerParams(vmem_limit_bytes=GRANT << 20),
        cost_estimate=pl.CostEstimate(
            flops=flops, bytes_accessed=4_000_000, transcendentals=exps
        ),
        name=name,
    )(*scalars, *arrays)


def prepare(slot_response, lengths, queries, readout, own):
    return per_group(
        prepare_kernel, "prepare",
        (slot_response, lengths), (queries, readout, own),
        [by_group((1, TOKENS, WIDTH)), by_group((1, TOKENS, WIDTH)), by_slot((1, TOKENS, 512))],
        [STACK, STACK, STATS],
        (STACK_SHAPE, STACK_SHAPE, STATS_SHAPE),
        [], 240_000_000, 460_000,
    )


def forward(slot_response, pair_prompt, q, r, part, near, far):
    return per_group(
        forward_kernel, "forward",
        (slot_response, pair_prompt), (q, r, part, near, far),
        [STACK, STACK, STATS, VMEM, VMEM],
        [STATS, whole((64, 4, HEAD))],
        (STATS_SHAPE, jax.ShapeDtypeStruct((64, 4, HEAD), f32)),
        [
            pltpu.VMEM((512, HEAD), bf16),
            pltpu.VMEM((512, HEAD), bf16),
            pltpu.VMEM((2, 8, HEAD), f32),
        ],
        940_000_000, 1_800_000,
    )


def backward(slot_response, pair_prompt, place, q, r, stats, near, far):
    return per_group(
        backward_kernel, "backward",
        (slot_response, pair_prompt, place), (q, r, stats, near, far),
        [STACK, STACK, STATS, VMEM, VMEM],
        whole((8, LOAD_ROWS, HEAD)),
        jax.ShapeDtypeStruct((8, LOAD_ROWS, HEAD), bf16),
        [
            pltpu.VMEM((512, HEAD), bf16),
            pltpu.VMEM((512, HEAD), bf16),
            pltpu.VMEM((512, WIDTH), bf16),
            pltpu.VMEM((512, WIDTH), bf16),
        ],
        1_880_000_000, 1_800_000,
    )


def finish(slot_response, pair_prompt, q, r, stats, near, far, own):
    return per_group(
        finish_kernel, "finish",
        (slot_response, pair_prompt), (q, r, stats, near, far, own),
        [STACK, STACK, STATS, VMEM, VMEM, by_slot((1, TOKENS, 512))],
        [by_group((1, TOKENS, WIDTH)), by_slot((1, TOKENS, 512)), whole((8, HEAD))],
        (
            jax.ShapeDtypeStruct((2, TOKENS, QUERY_HEADS * HEAD), bf16),
            jax.ShapeDtypeStruct((2, TOKENS, 512), bf16),
            jax.ShapeDtypeStruct((8, HEAD), f32),
        ),
        [
            pltpu.VMEM((KEYS, HEAD), bf16),
            pltpu.VMEM((KEYS, HEAD), bf16),
            pltpu.VMEM((TOKENS, WIDTH), bf16),
            pltpu.VMEM((KEYS, WIDTH), bf16),
        ],
        2_000_000_000, 2_300_000,
    )


def with_news(slot_response, share, load):
    high = lax.reduce_precision(share, 8, 7)
    middle = lax.reduce_precision(share - high, 8, 7)
    low = share - high - middle
    names = jnp.stack([slot_response // 32, slot_response % 32], axis=1).reshape(4, 1)
    names = jnp.broadcast_to(names.astype(f32), (4, HEAD))
    news = jnp.concatenate([high, middle, low, names], axis=0).astype(bf16)
    news = jnp.broadcast_to(news[None], (8, 16, HEAD))
    return lax.dynamic_update_slice(load, news, (0, 512, 0))


def weigh_kernel(
    ref_margin_ref, pair_prompt_ref, load_ref, done_ref, margins_ref, weights_ref, out_ref, factor_s
):
    del done_ref
    pair_sums = jnp.zeros((4, HEAD), f32)
    names = []
    for source in range(8):
        n = load_ref[source, 512:528, :].astype(f32)
        pair_sums = pair_sums + (n[0:4] + n[4:8] + n[8:12])
        names += [n[12:13] * 32.0 + n[13:14], n[14:15] * 32.0 + n[15:16]]
    margins = MARGIN_BETA * (pair_sums - ref_margin_ref[...])
    margins_ref[...] = margins
    weights = -LOSS_SCALE * MARGIN_BETA * jax.nn.sigmoid(-margins)
    weights_ref[...] = weights
    responses = jnp.concatenate(names, axis=0).astype(jnp.int32)
    sign = (1 - 2 * (responses % 2)).astype(f32)
    lane = lax.broadcasted_iota(jnp.int32, (16, HEAD), 1)
    for p in range(2):
        table = jnp.where(pair_prompt_ref[...] == p, weights, 0.0)
        found = jnp.zeros((16, HEAD), f32)
        for k in range(4):
            found = jnp.where(responses // 2 == lane + k * HEAD, table[k : k + 1], found)
        factor_s[p] = sign * jnp.sum(found, axis=1, keepdims=True)

    def step(z, _):
        sums = [jnp.zeros((32, HEAD), f32) for _ in range(2)]
        for source in range(8):
            for slot in range(2):
                rows = pl.ds(pl.multiple_of(slot * 256 + z * 32, 32), 32)
                piece = load_ref[source, rows, :].astype(f32)
                at = source * 2 + slot
                for p in range(2):
                    sums[p] = sums[p] + factor_s[p, at : at + 1, :] * piece
        both = jnp.concatenate([s.reshape(8, 1, 4, HEAD) for s in sums], axis=1)
        out_ref[z] = both.reshape(8, 8, HEAD).astype(bf16)
        return 0

    lax.fori_loop(0, 8, step, 0)


def weigh(ref_margin, pair_prompt, load, done):
    vmem = pl.BlockSpec(memory_space=pltpu.VMEM)
    return pl.pallas_call(
        weigh_kernel,
        out_shape=(
            jax.ShapeDtypeStruct((4, HEAD), f32),
            jax.ShapeDtypeStruct((4, HEAD), f32),
            jax.ShapeDtypeStruct((8, 8, 8, HEAD), bf16),
        ),
        in_specs=[vmem, vmem, vmem, pl.BlockSpec(memory_space=pl.ANY)],
        out_specs=(vmem, vmem, vmem),
        scratch_shapes=[pltpu.VMEM((2, 16, HEAD), f32)],
        compiler_params=pltpu.CompilerParams(vmem_limit_bytes=8 << 20),
        name="weigh",
    )(ref_margin, pair_prompt, load, done)


def join_kernel(parts_ref, out_ref):
    total = parts_ref[0].astype(f32)
    for i in range(1, 64):
        total = total + parts_ref[i].astype(f32)
    out_ref[...] = jnp.broadcast_to(total.astype(bf16)[None], out_ref.shape)


def join(parts):
    vmem = pl.BlockSpec(memory_space=pltpu.VMEM)
    return pl.pallas_call(
        join_kernel,
        out_shape=jax.ShapeDtypeStruct((32, 8, HEAD), bf16),
        in_specs=[vmem],
        out_specs=vmem,
        compiler_params=pltpu.CompilerParams(vmem_limit_bytes=8 << 20),
        name="join",
    )(parts)


def to_all(pieces, axes):
    return lax.all_to_all(pieces, axes, 0, 0, tiled=True)


def copies_to_all(shard, axes):
    size = lax.axis_size(axes)
    return to_all(jnp.broadcast_to(shard[None], (size, *shard.shape)), axes)


def on_device(
    prompt_kv, response_queries, resp_kv, readout, slot_response, lengths, pair_prompt, ref_margin
):
    near = copies_to_all(prompt_kv, "z")
    place = lax.axis_index("c").astype(jnp.int32)[None]
    q, r, part = prepare(slot_response, lengths, response_queries, readout, resp_kv)
    near, q, r, part = lax.optimization_barrier((near, q, r, part))
    far = lax.ppermute(near, "c", [(0, 1), (1, 0)])
    stats, contrib = forward(slot_response, pair_prompt, q, r, part, near, far)
    contribs = to_all(contrib, APART)
    load = backward(slot_response, pair_prompt, place, q, r, stats, near, far)
    share = jnp.sum(contribs, axis=0)
    load = to_all(with_news(slot_response, share, load), CLOSE)
    dq, down, done = finish(slot_response, pair_prompt, q, r, stats, near, far, resp_kv)
    margins, weights, parts = weigh(
        ref_margin.reshape(4, HEAD), pair_prompt.reshape(4, HEAD), load, done
    )
    pairs = jnp.arange(ref_margin.shape[0])
    sign = 1.0 - 2.0 * (slot_response % 2).astype(f32)
    found = jnp.where((slot_response // 2)[:, None] == pairs, weights.reshape(1, -1), 0.0)
    own = (jnp.sum(found, axis=1) * sign)[:, None, None]
    grad_q = (own * dq.astype(f32)).astype(bf16)
    grad_own = (own * down.astype(f32)).astype(bf16)
    total = join(to_all(parts.reshape(64, 8, HEAD), APART))
    total = to_all(total, RESP).reshape(8, 4, 2, 4, HEAD)
    grad_prompt = jnp.transpose(total, (2, 0, 3, 1, 4)).reshape(2, 32, 512)
    return margins.reshape(-1), grad_q, grad_own, grad_prompt


def solution(mesh):
    split = Mesh(mesh.devices.reshape(8, 2, 8, 4), EVERY)
    in_specs = (
        P(None, PREFIX, None),
        P(EVERY, None, None),
        P(EVERY, None, None),
        P(EVERY, None, None),
        P(EVERY),
        P(),
        P(),
        P(),
    )
    out_specs = (P(), P(EVERY, None, None), P(EVERY, None, None), P(None, PREFIX, None))
    return jax.shard_map(
        on_device, mesh=split, in_specs=in_specs, out_specs=out_specs, check_vma=False
    )
```

time: 123 us -> 119 us (0.967)
  blocking collectives: 27.6 us -> 0 us
  starting transfers between devices: 29.5 us -> 37.7 us
  waiting for transfers between devices: 39.1 us -> 46 us
  Pallas kernels: 20.9 us -> 27.4 us
  local copies, waits for them, and re-layouts: 2.31 us -> 4.28 us
    all_to_all x1 -> x0, blocking collectives: 27.6 us -> none  [to_all(): return lax.all_to_all(pieces, axes, 0, 0, tiled=True)]
    all_to_all x4 -> x5, starting transfers between devices: 27.6 us -> 35.8 us  [to_all(): return lax.all_to_all(pieces, axes, 0, 0, tiled=True)]
    all_to_all x4 -> x5, waiting for transfers between devices: 37.2 us -> 44.1 us  [to_all(): return lax.all_to_all(pieces, axes, 0, 0, tiled=True)]
    pallas_call x3 -> x4, Pallas kernels: 19 us -> 25.5 us  [per_group(): pl.pallas_call(kernel, out_shape=out_shape, grid_spec=pltpu.PrefetchScala...]
  transfers between devices with their start and end apart: 5 -> 6, of which waited for: 5 -> 6; matrix products, arithmetic and copies ran while one was open for 2% -> 2% of each run, Pallas kernels for 8% -> 16%
where the time goes in v4:
time: 119 us; the launch traced here: 118 us
  waiting for transfers between devices  46 us (39%)
  starting transfers between devices  37.7 us (32%)
  Pallas kernels  27.4 us (23%)
  local copies, waits for them, and re-layouts  4.28 us (4%)
  other arithmetic  2.34 us (2%)
    all_to_all x5, waiting for transfers between devices, to_all(): return lax.all_to_all(pieces, axes, 0, 0, tiled=True)  44.1 us
    all_to_all x5, starting transfers between devices, to_all(): return lax.all_to_all(pieces, axes, 0, 0, tiled=True)  35.8 us
    pallas_call x4, Pallas kernels, per_group(): pl.pallas_call(kernel, out_shape=out_shape, grid_spec=pltpu.PrefetchScala...  25.5 us
  transfers between devices with their start and end apart: 6, of which 6 were waited for; matrix products, arithmetic and copies ran while one was open for 2% of the time, Pallas kernels for 16%

profile of v4, /device:TPU:8, one launch (start us, length us, event | category | flops | bytes accessed | tf_op | source)
XLA Modules:
  0.0 118.5 jit_solution(2599172348532206181)
XLA Ops:
  0.7 1.7 %broadcast_in_dim.17 = bf16[8,2,32,512]{3,2,1,0:T(8,128)(2,1)} broadcast(bf16[2,32,512]{2,1,0:T(8,128)(2,1)} %param.8), dimensions={1,2,3} | broadcast | bytes 589824 | tf_op jit(solution)/shard_map/broadcast_in_dim | solution.py:384
  2.4 10.3 %all-to-all-start = ((bf16[8,2,32,512]{3,2,1,0:T(8,128)(2,1)}), bf16[8,2,32,512]{3,2,1,0:T(8,128)(2,1)S(1)}, u32[]{:S(2)}, u32[]{:S(2)}) async-start(bf16[8,2,32,512]{3,2,1,0:T(8,128)(2,1)} %broadcast_in_dim.17), calls=%async_computation | async-start | bytes 1048576 | tf_op jit(solution)/shard_map/all_to_all | solution.py:379
  12.8 4.5 %prepare.1 = (bf16[4,896,128]{2,1,0:T(8,128)(2,1)S(1)}, bf16[4,896,128]{2,1,0:T(8,128)(2,1)}, f32[4,8,896]{2,1,0:T(8,128)S(1)}) custom-call(s32[2]{0:T(128)S(1)} %copy-done.4, s32[1024]{0:T(1024)S(1)} %copy-done.1, bf16[2,128,1792]{2,1,0:T(8,128)(2,1)} %q_ref.1, bf16[2,128,1792]{2,1,0:T(8,128)(2,1)} %r_ref.1, bf16[2,128,512]{2,1,0:T(8,128)(2,1)S(1)} %copy-done), custom_call_target="tpu_custom_call" | custom-call | flops 240000000 | bytes 4000000 | tf_op jit(solution)/shard_map/prepare/pallas_call | solution.py:208
  17.2 0.9 copy-done.5
  18.2 12.1 %all-to-all-done.near_ref = bf16[8,2,32,512]{3,2,1,0:T(8,128)(2,1)S(1)} async-done(((bf16[8,2,32,512]{3,2,1,0:T(8,128)(2,1)}), bf16[8,2,32,512]{3,2,1,0:T(8,128)(2,1)S(1)}, u32[]{:S(2)}, u32[]{:S(2)}) %all-to-all-start) | async-done | bytes 524320 | tf_op jit(solution)/shard_map/all_to_all | solution.py:379
  30.2 1.9 %collective-permute-start = (bf16[8,2,32,512]{3,2,1,0:T(8,128)(2,1)S(1)}, bf16[8,2,32,512]{3,2,1,0:T(8,128)(2,1)S(1)}, u32[]{:S(2)}, u32[]{:S(2)}) collective-permute-start(bf16[8,2,32,512]{3,2,1,0:T(8,128)(2,1)S(1)} %all-to-all-done.near_ref), channel_id=1, source_target_pairs={{0,32},{32,0},{1,33},{33,1},{2,34},{34,2},{3,35},{35,3},{4,36},{36... | collective-permute-start | bytes 1572872 | tf_op jit(solution)/shard_map/ppermute | solution.py:394
  32.2 1.8 %collective-permute-done.far_ref = bf16[8,2,32,512]{3,2,1,0:T(8,128)(2,1)S(1)} collective-permute-done((bf16[8,2,32,512]{3,2,1,0:T(8,128)(2,1)S(1)}, bf16[8,2,32,512]{3,2,1,0:T(8,128)(2,1)S(1)}, u32[]{:S(2)}, u32[]{:S(2)}) %collective-permute-start) | collective-permute-done | bytes 524320 | tf_op jit(solution)/shard_map/ppermute | solution.py:394
  34.0 6.2 %forward.1 = (f32[4,8,896]{2,1,0:T(8,128)S(1)}, f32[64,4,128]{2,1,0:T(4,128)}) custom-call(s32[2]{0:T(128)S(1)} %copy-done.4, s32[512]{0:T(512)S(1)} %copy-done.3, bf16[4,896,128]{2,1,0:T(8,128)(2,1)} %copy-done.5, bf16[4,896,128]{2,1,0:T(8,128)(2,1)} %get-tuple-element.23.r_ref, f32[4,8,896]{2,1,0:T(8,128)S(1)} %get-tuple-element.24.part_ref, ...), custom_call_target="tpu_custom_call" | custom-call | flops 940000000 | bytes 4000000 | tf_op jit(solution)/shard_map/forward/pallas_call | solution.py:208
  40.3 8.1 %all-to-all-start.1 = ((f32[64,4,128]{2,1,0:T(4,128)}), f32[64,4,128]{2,1,0:T(4,128)S(1)}, u32[]{:S(2)}, u32[]{:S(2)}) async-start(f32[64,4,128]{2,1,0:T(4,128)} %get-tuple-element.27), calls=%async_computation.1 | async-start | bytes 262144 | tf_op jit(solution)/shard_map/all_to_all | solution.py:379
  48.7 7.6 %backward.1 = bf16[8,528,128]{2,1,0:T(8,128)(2,1)} custom-call(s32[2]{0:T(128)S(1)} %copy-done.4, s32[512]{0:T(512)S(1)} %copy-done.3, s32[1]{0:T(128)} %bitcast.2.place_ref, bf16[4,896,128]{2,1,0:T(8,128)(2,1)} %copy-done.5, bf16[4,896,128]{2,1,0:T(8,128)(2,1)} %get-tuple-element.23.r_ref, f32[4,8,896]{2,1,0:T(8,128)S(1)} %get-tuple-element.26.stats_ref, ...), custom_call_target="tpu_custom_call" | custom-call | flops 1880000000 | bytes 4000000 | tf_op jit(solution)/shard_map/backward/pallas_call | solution.py:208
  56.2 4.3 %all-to-all-done.1 = f32[64,4,128]{2,1,0:T(4,128)S(1)} async-done(((f32[64,4,128]{2,1,0:T(4,128)}), f32[64,4,128]{2,1,0:T(4,128)S(1)}, u32[]{:S(2)}, u32[]{:S(2)}) %all-to-all-start.1) | async-done | bytes 131104 | tf_op jit(solution)/shard_map/all_to_all | solution.py:379
  60.7 0.6 broadcast_dynamic-update-slice_fusion
  61.3 4.3 %all-to-all-start.2 = ((bf16[8,528,128]{2,1,0:T(8,128)(2,1)}), bf16[8,528,128]{2,1,0:T(8,128)(2,1)S(1)}, u32[]{:S(2)}, u32[]{:S(2)}) async-start(bf16[8,528,128]{2,1,0:T(8,128)(2,1)} %broadcast_dynamic-update-slice_fusion), calls=%async_computation.2 | async-start | bytes 2162688 | tf_op jit(solution)/shard_map/all_to_all | solution.py:379
  65.6 7.2 %finish.1 = (bf16[2,128,1792]{2,1,0:T(8,128)(2,1)}, bf16[2,128,512]{2,1,0:T(8,128)(2,1)S(1)}, f32[8,128]{1,0:T(8,128)S(1)}) custom-call(s32[2]{0:T(128)S(1)} %copy-done.4, s32[512]{0:T(512)S(1)} %copy-done.3, bf16[4,896,128]{2,1,0:T(8,128)(2,1)} %copy-done.5, bf16[4,896,128]{2,1,0:T(8,128)(2,1)} %get-tuple-element.23.r_ref, ...), custom_call_target="tpu_custom_call" | custom-call | flops 2000000000 | bytes 4000000 | tf_op jit(solution)/shard_map/finish/pallas_call | solution.py:208
  72.9 8.4 %all-to-all-done.2.load_ref = bf16[8,528,128]{2,1,0:T(8,128)(2,1)S(1)} async-done(((bf16[8,528,128]{2,1,0:T(8,128)(2,1)}), bf16[8,528,128]{2,1,0:T(8,128)(2,1)S(1)}, u32[]{:S(2)}, u32[]{:S(2)}) %all-to-all-start.2) | async-done | bytes 1081376 | tf_op jit(solution)/shard_map/all_to_all | solution.py:379
  81.3 1.2 %weigh.1 = (f32[4,128]{1,0:T(4,128)}, f32[4,128]{1,0:T(4,128)S(1)}, bf16[8,8,8,128]{3,2,1,0:T(8,128)(2,1)}) custom-call(f32[4,128]{1,0:T(4,128)S(1)} %bitcast.13, s32[4,128]{1,0:T(4,128)S(1)} %bitcast.14, bf16[8,528,128]{2,1,0:T(8,128)(2,1)S(1)} %all-to-all-done.2.load_ref, f32[8,128]{1,0:T(8,128)S(1)} %get-tuple-element.28.done_ref), custom_call_target="tpu_custom_call" | custom-call | tf_op jit(solution)/shard_map/weigh/pallas_call | solution.py:344
  82.7 8.4 %all-to-all-start.3 = ((bf16[64,8,128]{2,1,0:T(8,128)(2,1)}), bf16[64,8,128]{2,1,0:T(8,128)(2,1)S(1)}, u32[]{:S(2)}, u32[]{:S(2)}) async-start(bf16[64,8,128]{2,1,0:T(8,128)(2,1)} %bitcast.7), calls=%async_computation.3 | async-start | bytes 262144 | tf_op jit(solution)/shard_map/all_to_all | solution.py:379
  91.1 1.1 multiply_convert_fusion
  92.3 11.0 %all-to-all-done.3.parts_ref = bf16[64,8,128]{2,1,0:T(8,128)(2,1)S(1)} async-done(((bf16[64,8,128]{2,1,0:T(8,128)(2,1)}), bf16[64,8,128]{2,1,0:T(8,128)(2,1)S(1)}, u32[]{:S(2)}, u32[]{:S(2)}) %all-to-all-start.3) | async-done | bytes 131104 | tf_op jit(solution)/shard_map/all_to_all | solution.py:379
  103.3 0.7 join.1
  104.0 4.7 %all-to-all-start.4 = ((bf16[32,8,128]{2,1,0:T(8,128)(2,1)}), bf16[32,8,128]{2,1,0:T(8,128)(2,1)S(1)}, u32[]{:S(2)}, u32[]{:S(2)}) async-start(bf16[32,8,128]{2,1,0:T(8,128)(2,1)} %join.1), calls=%async_computation.4 | async-start | bytes 131072 | tf_op jit(solution)/shard_map/all_to_all | solution.py:379
  108.7 0.8 multiply_convert_fusion.1
  109.5 8.3 %all-to-all-done.4 = bf16[32,8,128]{2,1,0:T(8,128)(2,1)S(1)} async-done(((bf16[32,8,128]{2,1,0:T(8,128)(2,1)}), bf16[32,8,128]{2,1,0:T(8,128)(2,1)S(1)}, u32[]{:S(2)}, u32[]{:S(2)}) %all-to-all-start.4) | async-done | bytes 65568 | tf_op jit(solution)/shard_map/all_to_all | solution.py:379
  117.8 0.7 reshape.74
  (24 shorter events, 0.7 us)
Async XLA Ops:
  0.6 12.1 %copy-start.4 = (s32[2]{0:T(128)S(1)}, s32[2]{0:T(128)}, u32[]{:S(2)}) copy-start(s32[2]{0:T(128)} %response_ref.7) | copy-start | bytes 28
  0.6 12.1 %copy-start.1 = (s32[1024]{0:T(1024)S(1)}, s32[1024]{0:T(1024)}, u32[]{:S(2)}) copy-start(s32[1024]{0:T(1024)} %lengths_ref.1) | copy-start | bytes 12292
  0.7 12.1 %copy-start = (bf16[2,128,512]{2,1,0:T(8,128)(2,1)S(1)}, bf16[2,128,512]{2,1,0:T(8,128)(2,1)}, u32[]{:S(2)}) copy-start(bf16[2,128,512]{2,1,0:T(8,128)(2,1)} %own_ref.3) | copy-start | bytes 786436
  2.4 27.8 %all-to-all-start = ((bf16[8,2,32,512]{3,2,1,0:T(8,128)(2,1)}), bf16[8,2,32,512]{3,2,1,0:T(8,128)(2,1)S(1)}, u32[]{:S(2)}, u32[]{:S(2)}) async-start(bf16[8,2,32,512]{3,2,1,0:T(8,128)(2,1)} %broadcast_in_dim.17), calls=%async_computation | async-start | bytes 1048576 | tf_op jit(solution)/shard_map/all_to_all | solution.py:379
  12.7 21.3 %copy-start.3 = (s32[512]{0:T(512)S(1)}, s32[512]{0:T(512)}, u32[]{:S(2)}) copy-start(s32[512]{0:T(512)} %pair_prompt_ref.5) | copy-start | bytes 6148
  17.2 0.9 copy-start.5
  30.2 3.8 %collective-permute-start = (bf16[8,2,32,512]{3,2,1,0:T(8,128)(2,1)S(1)}, bf16[8,2,32,512]{3,2,1,0:T(8,128)(2,1)S(1)}, u32[]{:S(2)}, u32[]{:S(2)}) collective-permute-start(bf16[8,2,32,512]{3,2,1,0:T(8,128)(2,1)S(1)} %all-to-all-done.near_ref), channel_id=1, source_target_pairs={{0,32},{32,0},{1,33},{33,1},{2,34},{34,2},{3,35},{35,3},{4,36},{36... | collective-permute-start | bytes 1572872 | tf_op jit(solution)/shard_map/ppermute | solution.py:394
  40.3 20.3 %all-to-all-start.1 = ((f32[64,4,128]{2,1,0:T(4,128)}), f32[64,4,128]{2,1,0:T(4,128)S(1)}, u32[]{:S(2)}, u32[]{:S(2)}) async-start(f32[64,4,128]{2,1,0:T(4,128)} %get-tuple-element.27), calls=%async_computation.1 | async-start | bytes 262144 | tf_op jit(solution)/shard_map/all_to_all | solution.py:379
  61.3 20.0 %all-to-all-start.2 = ((bf16[8,528,128]{2,1,0:T(8,128)(2,1)}), bf16[8,528,128]{2,1,0:T(8,128)(2,1)S(1)}, u32[]{:S(2)}, u32[]{:S(2)}) async-start(bf16[8,528,128]{2,1,0:T(8,128)(2,1)} %broadcast_dynamic-update-slice_fusion), calls=%async_computation.2 | async-start | bytes 2162688 | tf_op jit(solution)/shard_map/all_to_all | solution.py:379
  65.6 15.7 %copy-start.2 = (f32[512]{0:T(512)S(1)}, f32[512]{0:T(512)}, u32[]{:S(2)}) copy-start(f32[512]{0:T(512)} %param.15) | copy-start | bytes 6148
  72.9 18.2 %copy-start.6 = (bf16[2,128,1792]{2,1,0:T(8,128)(2,1)S(1)}, bf16[2,128,1792]{2,1,0:T(8,128)(2,1)}, u32[]{:S(2)}) copy-start(bf16[2,128,1792]{2,1,0:T(8,128)(2,1)} %get-tuple-element.31) | copy-start | bytes 2752516
  82.7 20.6 %all-to-all-start.3 = ((bf16[64,8,128]{2,1,0:T(8,128)(2,1)}), bf16[64,8,128]{2,1,0:T(8,128)(2,1)S(1)}, u32[]{:S(2)}, u32[]{:S(2)}) async-start(bf16[64,8,128]{2,1,0:T(8,128)(2,1)} %bitcast.7), calls=%async_computation.3 | async-start | bytes 262144 | tf_op jit(solution)/shard_map/all_to_all | solution.py:379
  104.0 13.8 %all-to-all-start.4 = ((bf16[32,8,128]{2,1,0:T(8,128)(2,1)}), bf16[32,8,128]{2,1,0:T(8,128)(2,1)S(1)}, u32[]{:S(2)}, u32[]{:S(2)}) async-start(bf16[32,8,128]{2,1,0:T(8,128)(2,1)} %join.1), calls=%async_computation.4 | async-start | bytes 131072 | tf_op jit(solution)/shard_map/all_to_all | solution.py:379

commit v5 on v4

--- a/solution.py
+++ b/solution.py
@@ -332,8 +332,8 @@
                 at = source * 2 + slot
                 for p in range(2):
                     sums[p] = sums[p] + factor_s[p, at : at + 1, :] * piece
-        both = jnp.concatenate([s.reshape(8, 1, 4, HEAD) for s in sums], axis=1)
-        out_ref[z] = both.reshape(8, 8, HEAD).astype(bf16)
+        for p in range(2):
+            out_ref[z, p * 4 : p * 4 + 4] = sums[p].reshape(4, 8, HEAD).astype(bf16)
         return 0
 
     lax.fori_loop(0, 8, step, 0)
@@ -379,9 +379,29 @@
     return lax.all_to_all(pieces, axes, 0, 0, tiled=True)
 
 
+def repeat_kernel(shard_ref, out_ref, sems):
+    copies = [
+        pltpu.make_async_copy(shard_ref, out_ref.at[i], sems.at[i])
+        for i in range(out_ref.shape[0])
+    ]
+    for copy in copies:
+        copy.start()
+    for copy in copies:
+        copy.wait()
+
+
 def copies_to_all(shard, axes):
     size = lax.axis_size(axes)
-    return to_all(jnp.broadcast_to(shard[None], (size, *shard.shape)), axes)
+    hbm = pl.BlockSpec(memory_space=pltpu.HBM)
+    repeated = pl.pallas_call(
+        repeat_kernel,
+        out_shape=jax.ShapeDtypeStruct((size, *shard.shape), shard.dtype),
+        in_specs=[hbm],
+        out_specs=hbm,
+        scratch_shapes=[pltpu.SemaphoreType.DMA((size,))],
+        name="repeat",
+    )(shard)
+    return to_all(repeated, axes)
 
 
 def on_device(
@@ -408,8 +428,8 @@
     grad_q = (own * dq.astype(f32)).astype(bf16)
     grad_own = (own * down.astype(f32)).astype(bf16)
     total = join(to_all(parts.reshape(64, 8, HEAD), APART))
-    total = to_all(total, RESP).reshape(8, 4, 2, 4, HEAD)
-    grad_prompt = jnp.transpose(total, (2, 0, 3, 1, 4)).reshape(2, 32, 512)
+    total = to_all(total, RESP).reshape(2, 4, 4, 8, HEAD)
+    grad_prompt = jnp.transpose(total, (0, 1, 3, 2, 4)).reshape(2, 32, 512)
     return margins.reshape(-1), grad_q, grad_own, grad_prompt
 
 

time: 119 us -> 134 us (1.13)
  Pallas kernels: 27.4 us -> 44.5 us
  local copies, waits for them, and re-layouts: 4.28 us -> 2.48 us
    pallas_call x0 -> x1, Pallas kernels: none -> 17.1 us  [copies_to_all(): pl.pallas_call(repeat_kernel, out_shape=jax.ShapeDtypeStruct((size, *shar...]
    broadcast_in_dim x1 -> x0, local copies, waits for them, and re-layouts: 1.74 us -> none  [copies_to_all(): return to_all(jnp.broadcast_to(shard[None], (size, *shard.shape)), axes)]
  transfers between devices with their start and end apart: 6 -> 6, of which waited for: 6 -> 6; matrix products, arithmetic and copies ran while one was open for 2% -> 2% of each run, Pallas kernels for 16% -> 14%
where the time goes in v5:
time: 134 us
  waiting for transfers between devices  46 us (34%)
  Pallas kernels  44.5 us (33%)
  starting transfers between devices  37.7 us (28%)
  local copies, waits for them, and re-layouts  2.48 us (2%)
  other arithmetic  2.34 us (2%)
    all_to_all x5, waiting for transfers between devices, to_all(): return lax.all_to_all(pieces, axes, 0, 0, tiled=True)  44.1 us
    all_to_all x5, starting transfers between devices, to_all(): return lax.all_to_all(pieces, axes, 0, 0, tiled=True)  35.8 us
    pallas_call x4, Pallas kernels, per_group(): pl.pallas_call(kernel, out_shape=out_shape, grid_spec=pltpu.PrefetchScala...  25.5 us
    pallas_call x1, Pallas kernels, copies_to_all(): pl.pallas_call(repeat_kernel, out_shape=jax.ShapeDtypeStruct((size, *shar...  17.1 us
  transfers between devices with their start and end apart: 6, of which 6 were waited for; matrix products, arithmetic and copies ran while one was open for 2% of the time, Pallas kernels for 14%

profile of v5, /device:TPU:8, one launch (start us, length us, event | category | flops | bytes accessed | tf_op | source)
XLA Modules:
  0.0 133.8 jit_solution(216472272940261092)
XLA Ops:
  0.7 17.1 %repeat.1 = bf16[8,2,32,512]{3,2,1,0:T(8,128)(2,1)} custom-call(bf16[2,32,512]{2,1,0:T(8,128)(2,1)} %shard_ref.1), custom_call_target="tpu_custom_call" | custom-call | tf_op jit(solution)/shard_map/repeat/pallas_call | solution.py:396
  17.7 10.3 %all-to-all-start = ((bf16[8,2,32,512]{3,2,1,0:T(8,128)(2,1)}), bf16[8,2,32,512]{3,2,1,0:T(8,128)(2,1)S(1)}, u32[]{:S(2)}, u32[]{:S(2)}) async-start(bf16[8,2,32,512]{3,2,1,0:T(8,128)(2,1)} %repeat.1), calls=%async_computation | async-start | bytes 1048576 | tf_op jit(solution)/shard_map/all_to_all | solution.py:379
  28.1 4.5 %prepare.1 = (bf16[4,896,128]{2,1,0:T(8,128)(2,1)S(1)}, bf16[4,896,128]{2,1,0:T(8,128)(2,1)}, f32[4,8,896]{2,1,0:T(8,128)S(1)}) custom-call(s32[2]{0:T(128)S(1)} %copy-done.4, s32[1024]{0:T(1024)S(1)} %copy-done.1, bf16[2,128,1792]{2,1,0:T(8,128)(2,1)} %q_ref.1, bf16[2,128,1792]{2,1,0:T(8,128)(2,1)} %r_ref.1, bf16[2,128,512]{2,1,0:T(8,128)(2,1)S(1)} %copy-done), custom_call_target="tpu_custom_call" | custom-call | flops 240000000 | bytes 4000000 | tf_op jit(solution)/shard_map/prepare/pallas_call | solution.py:208
  32.6 0.9 copy-done.5
  33.5 12.1 %all-to-all-done.near_ref = bf16[8,2,32,512]{3,2,1,0:T(8,128)(2,1)S(1)} async-done(((bf16[8,2,32,512]{3,2,1,0:T(8,128)(2,1)}), bf16[8,2,32,512]{3,2,1,0:T(8,128)(2,1)S(1)}, u32[]{:S(2)}, u32[]{:S(2)}) %all-to-all-start) | async-done | bytes 524320 | tf_op jit(solution)/shard_map/all_to_all | solution.py:379
  45.5 1.9 %collective-permute-start = (bf16[8,2,32,512]{3,2,1,0:T(8,128)(2,1)S(1)}, bf16[8,2,32,512]{3,2,1,0:T(8,128)(2,1)S(1)}, u32[]{:S(2)}, u32[]{:S(2)}) collective-permute-start(bf16[8,2,32,512]{3,2,1,0:T(8,128)(2,1)S(1)} %all-to-all-done.near_ref), channel_id=1, source_target_pairs={{0,32},{32,0},{1,33},{33,1},{2,34},{34,2},{3,35},{35,3},{4,36},{36... | collective-permute-start | bytes 1572872 | tf_op jit(solution)/shard_map/ppermute | solution.py:414
  47.5 1.8 %collective-permute-done.far_ref = bf16[8,2,32,512]{3,2,1,0:T(8,128)(2,1)S(1)} collective-permute-done((bf16[8,2,32,512]{3,2,1,0:T(8,128)(2,1)S(1)}, bf16[8,2,32,512]{3,2,1,0:T(8,128)(2,1)S(1)}, u32[]{:S(2)}, u32[]{:S(2)}) %collective-permute-start) | collective-permute-done | bytes 524320 | tf_op jit(solution)/shard_map/ppermute | solution.py:414
  49.3 6.2 %forward.1 = (f32[4,8,896]{2,1,0:T(8,128)S(1)}, f32[64,4,128]{2,1,0:T(4,128)}) custom-call(s32[2]{0:T(128)S(1)} %copy-done.4, s32[512]{0:T(512)S(1)} %copy-done.3, bf16[4,896,128]{2,1,0:T(8,128)(2,1)} %copy-done.5, bf16[4,896,128]{2,1,0:T(8,128)(2,1)} %get-tuple-element.23.r_ref, f32[4,8,896]{2,1,0:T(8,128)S(1)} %get-tuple-element.24.part_ref, ...), custom_call_target="tpu_custom_call" | custom-call | flops 940000000 | bytes 4000000 | tf_op jit(solution)/shard_map/forward/pallas_call | solution.py:208
  55.6 8.1 %all-to-all-start.1 = ((f32[64,4,128]{2,1,0:T(4,128)}), f32[64,4,128]{2,1,0:T(4,128)S(1)}, u32[]{:S(2)}, u32[]{:S(2)}) async-start(f32[64,4,128]{2,1,0:T(4,128)} %get-tuple-element.27), calls=%async_computation.1 | async-start | bytes 262144 | tf_op jit(solution)/shard_map/all_to_all | solution.py:379
  64.0 7.6 %backward.1 = bf16[8,528,128]{2,1,0:T(8,128)(2,1)} custom-call(s32[2]{0:T(128)S(1)} %copy-done.4, s32[512]{0:T(512)S(1)} %copy-done.3, s32[1]{0:T(128)} %bitcast.2.place_ref, bf16[4,896,128]{2,1,0:T(8,128)(2,1)} %copy-done.5, bf16[4,896,128]{2,1,0:T(8,128)(2,1)} %get-tuple-element.23.r_ref, f32[4,8,896]{2,1,0:T(8,128)S(1)} %get-tuple-element.26.stats_ref, ...), custom_call_target="tpu_custom_call" | custom-call | flops 1880000000 | bytes 4000000 | tf_op jit(solution)/shard_map/backward/pallas_call | solution.py:208
  71.6 4.3 %all-to-all-done.1 = f32[64,4,128]{2,1,0:T(4,128)S(1)} async-done(((f32[64,4,128]{2,1,0:T(4,128)}), f32[64,4,128]{2,1,0:T(4,128)S(1)}, u32[]{:S(2)}, u32[]{:S(2)}) %all-to-all-start.1) | async-done | bytes 131104 | tf_op jit(solution)/shard_map/all_to_all | solution.py:379
  76.0 0.6 broadcast_dynamic-update-slice_fusion
  76.7 4.3 %all-to-all-start.2 = ((bf16[8,528,128]{2,1,0:T(8,128)(2,1)}), bf16[8,528,128]{2,1,0:T(8,128)(2,1)S(1)}, u32[]{:S(2)}, u32[]{:S(2)}) async-start(bf16[8,528,128]{2,1,0:T(8,128)(2,1)} %broadcast_dynamic-update-slice_fusion), calls=%async_computation.2 | async-start | bytes 2162688 | tf_op jit(solution)/shard_map/all_to_all | solution.py:379
  81.0 7.2 %finish.1 = (bf16[2,128,1792]{2,1,0:T(8,128)(2,1)}, bf16[2,128,512]{2,1,0:T(8,128)(2,1)S(1)}, f32[8,128]{1,0:T(8,128)S(1)}) custom-call(s32[2]{0:T(128)S(1)} %copy-done.4, s32[512]{0:T(512)S(1)} %copy-done.3, bf16[4,896,128]{2,1,0:T(8,128)(2,1)} %copy-done.5, bf16[4,896,128]{2,1,0:T(8,128)(2,1)} %get-tuple-element.23.r_ref, ...), custom_call_target="tpu_custom_call" | custom-call | flops 2000000000 | bytes 4000000 | tf_op jit(solution)/shard_map/finish/pallas_call | solution.py:208
  88.2 8.4 %all-to-all-done.2.load_ref = bf16[8,528,128]{2,1,0:T(8,128)(2,1)S(1)} async-done(((bf16[8,528,128]{2,1,0:T(8,128)(2,1)}), bf16[8,528,128]{2,1,0:T(8,128)(2,1)S(1)}, u32[]{:S(2)}, u32[]{:S(2)}) %all-to-all-start.2) | async-done | bytes 1081376 | tf_op jit(solution)/shard_map/all_to_all | solution.py:379
  96.7 1.2 weigh.1
  98.1 8.4 %all-to-all-start.3 = ((bf16[64,8,128]{2,1,0:T(8,128)(2,1)}), bf16[64,8,128]{2,1,0:T(8,128)(2,1)S(1)}, u32[]{:S(2)}, u32[]{:S(2)}) async-start(bf16[64,8,128]{2,1,0:T(8,128)(2,1)} %bitcast.7), calls=%async_computation.3 | async-start | bytes 262144 | tf_op jit(solution)/shard_map/all_to_all | solution.py:379
  106.5 1.1 multiply_convert_fusion
  107.6 11.0 %all-to-all-done.3.parts_ref = bf16[64,8,128]{2,1,0:T(8,128)(2,1)S(1)} async-done(((bf16[64,8,128]{2,1,0:T(8,128)(2,1)}), bf16[64,8,128]{2,1,0:T(8,128)(2,1)S(1)}, u32[]{:S(2)}, u32[]{:S(2)}) %all-to-all-start.3) | async-done | bytes 131104 | tf_op jit(solution)/shard_map/all_to_all | solution.py:379
  118.7 0.7 join.1
  119.4 4.7 %all-to-all-start.4 = ((bf16[32,8,128]{2,1,0:T(8,128)(2,1)}), bf16[32,8,128]{2,1,0:T(8,128)(2,1)S(1)}, u32[]{:S(2)}, u32[]{:S(2)}) async-start(bf16[32,8,128]{2,1,0:T(8,128)(2,1)} %join.1), calls=%async_computation.4 | async-start | bytes 131072 | tf_op jit(solution)/shard_map/all_to_all | solution.py:379
  124.1 0.8 multiply_convert_fusion.1
  124.9 8.3 %all-to-all-done.4 = bf16[32,8,128]{2,1,0:T(8,128)(2,1)S(1)} async-done(((bf16[32,8,128]{2,1,0:T(8,128)(2,1)}), bf16[32,8,128]{2,1,0:T(8,128)(2,1)S(1)}, u32[]{:S(2)}, u32[]{:S(2)}) %all-to-all-start.4) | async-done | bytes 65568 | tf_op jit(solution)/shard_map/all_to_all | solution.py:379
  133.1 0.6 copy.16
  (23 shorter events, 0.7 us)
Async XLA Ops:
  0.6 27.4 %copy-start.4 = (s32[2]{0:T(128)S(1)}, s32[2]{0:T(128)}, u32[]{:S(2)}) copy-start(s32[2]{0:T(128)} %response_ref.7) | copy-start | bytes 28
  0.6 27.4 %copy-start.1 = (s32[1024]{0:T(1024)S(1)}, s32[1024]{0:T(1024)}, u32[]{:S(2)}) copy-start(s32[1024]{0:T(1024)} %lengths_ref.1) | copy-start | bytes 12292
  0.7 27.4 %copy-start = (bf16[2,128,512]{2,1,0:T(8,128)(2,1)S(1)}, bf16[2,128,512]{2,1,0:T(8,128)(2,1)}, u32[]{:S(2)}) copy-start(bf16[2,128,512]{2,1,0:T(8,128)(2,1)} %own_ref.3) | copy-start | bytes 786436
  17.7 27.8 %all-to-all-start = ((bf16[8,2,32,512]{3,2,1,0:T(8,128)(2,1)}), bf16[8,2,32,512]{3,2,1,0:T(8,128)(2,1)S(1)}, u32[]{:S(2)}, u32[]{:S(2)}) async-start(bf16[8,2,32,512]{3,2,1,0:T(8,128)(2,1)} %repeat.1), calls=%async_computation | async-start | bytes 1048576 | tf_op jit(solution)/shard_map/all_to_all | solution.py:379
  28.1 21.3 %copy-start.3 = (s32[512]{0:T(512)S(1)}, s32[512]{0:T(512)}, u32[]{:S(2)}) copy-start(s32[512]{0:T(512)} %pair_prompt_ref.5) | copy-start | bytes 6148
  32.6 0.9 copy-start.5
  45.5 3.8 %collective-permute-start = (bf16[8,2,32,512]{3,2,1,0:T(8,128)(2,1)S(1)}, bf16[8,2,32,512]{3,2,1,0:T(8,128)(2,1)S(1)}, u32[]{:S(2)}, u32[]{:S(2)}) collective-permute-start(bf16[8,2,32,512]{3,2,1,0:T(8,128)(2,1)S(1)} %all-to-all-done.near_ref), channel_id=1, source_target_pairs={{0,32},{32,0},{1,33},{33,1},{2,34},{34,2},{3,35},{35,3},{4,36},{36... | collective-permute-start | bytes 1572872 | tf_op jit(solution)/shard_map/ppermute | solution.py:414
  55.6 20.3 %all-to-all-start.1 = ((f32[64,4,128]{2,1,0:T(4,128)}), f32[64,4,128]{2,1,0:T(4,128)S(1)}, u32[]{:S(2)}, u32[]{:S(2)}) async-start(f32[64,4,128]{2,1,0:T(4,128)} %get-tuple-element.27), calls=%async_computation.1 | async-start | bytes 262144 | tf_op jit(solution)/shard_map/all_to_all | solution.py:379
  76.7 20.0 %all-to-all-start.2 = ((bf16[8,528,128]{2,1,0:T(8,128)(2,1)}), bf16[8,528,128]{2,1,0:T(8,128)(2,1)S(1)}, u32[]{:S(2)}, u32[]{:S(2)}) async-start(bf16[8,528,128]{2,1,0:T(8,128)(2,1)} %broadcast_dynamic-update-slice_fusion), calls=%async_computation.2 | async-start | bytes 2162688 | tf_op jit(solution)/shard_map/all_to_all | solution.py:379
  81.0 15.7 %copy-start.2 = (f32[512]{0:T(512)S(1)}, f32[512]{0:T(512)}, u32[]{:S(2)}) copy-start(f32[512]{0:T(512)} %param.15) | copy-start | bytes 6148
  88.2 18.3 %copy-start.6 = (bf16[2,128,1792]{2,1,0:T(8,128)(2,1)S(1)}, bf16[2,128,1792]{2,1,0:T(8,128)(2,1)}, u32[]{:S(2)}) copy-start(bf16[2,128,1792]{2,1,0:T(8,128)(2,1)} %get-tuple-element.31) | copy-start | bytes 2752516
  98.1 20.6 %all-to-all-start.3 = ((bf16[64,8,128]{2,1,0:T(8,128)(2,1)}), bf16[64,8,128]{2,1,0:T(8,128)(2,1)S(1)}, u32[]{:S(2)}, u32[]{:S(2)}) async-start(bf16[64,8,128]{2,1,0:T(8,128)(2,1)} %bitcast.7), calls=%async_computation.3 | async-start | bytes 262144 | tf_op jit(solution)/shard_map/all_to_all | solution.py:379
  119.4 13.8 %all-to-all-start.4 = ((bf16[32,8,128]{2,1,0:T(8,128)(2,1)}), bf16[32,8,128]{2,1,0:T(8,128)(2,1)S(1)}, u32[]{:S(2)}, u32[]{:S(2)}) async-start(bf16[32,8,128]{2,1,0:T(8,128)(2,1)} %join.1), calls=%async_computation.4 | async-start | bytes 131072 | tf_op jit(solution)/shard_map/all_to_all | solution.py:379

commit v6 on v4

--- a/solution.py
+++ b/solution.py
@@ -22,9 +22,10 @@
 EVERY = ("z", "c", "y", "x")
 PREFIX = ("z", "c")
 RESP = ("y", "x")
-CLOSE = ("c", "x")
 APART = ("z", "y")
-LOAD_ROWS = 528
+SHARERS = ("z", "c", "y")
+HALF_ROWS = 528
+LOAD_ROWS = 2 * HALF_ROWS + 16
 GRANT = 52
 NT = (((1,), (1,)), ((), ()))
 NN = (((1,), (0,)), ((), ()))
@@ -133,13 +134,12 @@
 
 
 def backward_kernel(
-    response_ref, pair_prompt_ref, place_ref, q_ref, r_ref, stats_ref, near_ref, far_ref,
-    load_ref, key_s, value_s, probs_s, dscores_s,
+    response_ref, pair_prompt_ref, q_ref, r_ref, stats_ref, near_ref, far_ref,
+    load_ref, other_ref, key_s, value_s, probs_s, dscores_s,
 ):
     slot = pl.program_id(0)
     group = pl.program_id(1)
     prompt = pair_prompt_ref[response_ref[slot] // 2]
-    mine = place_ref[0]
     fill(key_s, near_ref, far_ref, prompt, group * HEAD)
     fill(value_s, near_ref, far_ref, prompt, (KEY_VALUE_HEADS + group) * HEAD)
     scores, dprobs = dots(key_s[...], value_s[...], q_ref[0], r_ref[0])
@@ -149,9 +149,21 @@
     rows = pl.ds(pl.multiple_of(slot * 256, 256), 256)
     for i, grad in enumerate((dkey, dvalue)):
         grad = grad.astype(bf16)
-        for core in range(2):
-            dest = jnp.bitwise_xor(mine, core) * 4 + i * KEY_VALUE_HEADS + group
-            load_ref[dest, rows, :] = grad[core * 256 : (core + 1) * 256]
+        dest = i * KEY_VALUE_HEADS + group
+        load_ref[dest, rows, :] = grad[:256]
+        other_ref[dest, rows, :] = grad[256:]
+
+    @pl.when((slot == 0) & (group == 0))
+    def _():
+        row = lax.broadcasted_iota(jnp.int32, (16, HEAD), 0)
+        names = jnp.zeros((16, HEAD), f32)
+        for s in range(2):
+            response = response_ref[s]
+            names = jnp.where(row == 2 * s, (response // 32).astype(f32), names)
+            names = jnp.where(row == 2 * s + 1, (response % 32).astype(f32), names)
+        for dest in range(4):
+            load_ref[dest, 512:528, :] = names.astype(bf16)
+            other_ref[dest, 512:528, :] = names.astype(bf16)
 
 
 def finish_kernel(
@@ -239,8 +251,8 @@
         forward_kernel, "forward",
         (slot_response, pair_prompt), (q, r, part, near, far),
         [STACK, STACK, STATS, VMEM, VMEM],
-        [STATS, whole((64, 4, HEAD))],
-        (STATS_SHAPE, jax.ShapeDtypeStruct((64, 4, HEAD), f32)),
+        [STATS, whole((128, 4, HEAD))],
+        (STATS_SHAPE, jax.ShapeDtypeStruct((128, 4, HEAD), f32)),
         [
             pltpu.VMEM((512, HEAD), bf16),
             pltpu.VMEM((512, HEAD), bf16),
@@ -250,13 +262,16 @@
     )
 
 
-def backward(slot_response, pair_prompt, place, q, r, stats, near, far):
+def backward(slot_response, pair_prompt, q, r, stats, near, far):
     return per_group(
         backward_kernel, "backward",
-        (slot_response, pair_prompt, place), (q, r, stats, near, far),
+        (slot_response, pair_prompt), (q, r, stats, near, far),
         [STACK, STACK, STATS, VMEM, VMEM],
-        whole((8, LOAD_ROWS, HEAD)),
-        jax.ShapeDtypeStruct((8, LOAD_ROWS, HEAD), bf16),
+        [whole((4, LOAD_ROWS, HEAD)), whole((4, HALF_ROWS, HEAD))],
+        (
+            jax.ShapeDtypeStruct((4, LOAD_ROWS, HEAD), bf16),
+            jax.ShapeDtypeStruct((4, HALF_ROWS, HEAD), bf16),
+        ),
         [
             pltpu.VMEM((512, HEAD), bf16),
             pltpu.VMEM((512, HEAD), bf16),
@@ -288,15 +303,13 @@
     )
 
 
-def with_news(slot_response, share, load):
+def with_news(share, load):
     high = lax.reduce_precision(share, 8, 7)
     middle = lax.reduce_precision(share - high, 8, 7)
     low = share - high - middle
-    names = jnp.stack([slot_response // 32, slot_response % 32], axis=1).reshape(4, 1)
-    names = jnp.broadcast_to(names.astype(f32), (4, HEAD))
-    news = jnp.concatenate([high, middle, low, names], axis=0).astype(bf16)
-    news = jnp.broadcast_to(news[None], (8, 16, HEAD))
-    return lax.dynamic_update_slice(load, news, (0, 512, 0))
+    news = jnp.concatenate([high, middle, low, jnp.zeros_like(low)], axis=0).astype(bf16)
+    news = jnp.broadcast_to(news[None], (4, 16, HEAD))
+    return lax.dynamic_update_slice(load, news, (0, 2 * HALF_ROWS, 0))
 
 
 def weigh_kernel(
@@ -305,10 +318,12 @@
     del done_ref
     pair_sums = jnp.zeros((4, HEAD), f32)
     names = []
-    for source in range(8):
-        n = load_ref[source, 512:528, :].astype(f32)
+    for source in range(4):
+        n = load_ref[source, 2 * HALF_ROWS : LOAD_ROWS, :].astype(f32)
         pair_sums = pair_sums + (n[0:4] + n[4:8] + n[8:12])
-        names += [n[12:13] * 32.0 + n[13:14], n[14:15] * 32.0 + n[15:16]]
+        for core in range(2):
+            n = load_ref[source, core * HALF_ROWS + 512 : (core + 1) * HALF_ROWS, :].astype(f32)
+            names += [n[0:1] * 32.0 + n[1:2], n[2:3] * 32.0 + n[3:4]]
     margins = MARGIN_BETA * (pair_sums - ref_margin_ref[...])
     margins_ref[...] = margins
     weights = -LOSS_SCALE * MARGIN_BETA * jax.nn.sigmoid(-margins)
@@ -325,15 +340,16 @@
 
     def step(z, _):
         sums = [jnp.zeros((32, HEAD), f32) for _ in range(2)]
-        for source in range(8):
-            for slot in range(2):
-                rows = pl.ds(pl.multiple_of(slot * 256 + z * 32, 32), 32)
+        for source in range(4):
+            for at in range(4):
+                base = at // 2 * HALF_ROWS + at % 2 * 256
+                rows = pl.ds(pl.multiple_of(base + z * 32, 16), 32)
                 piece = load_ref[source, rows, :].astype(f32)
-                at = source * 2 + slot
                 for p in range(2):
-                    sums[p] = sums[p] + factor_s[p, at : at + 1, :] * piece
-        both = jnp.concatenate([s.reshape(8, 1, 4, HEAD) for s in sums], axis=1)
-        out_ref[z] = both.reshape(8, 8, HEAD).astype(bf16)
+                    which = source * 4 + at
+                    sums[p] = sums[p] + factor_s[p, which : which + 1, :] * piece
+        for p in range(2):
+            out_ref[z, p * 4 : p * 4 + 4] = sums[p].reshape(4, 8, HEAD).astype(bf16)
         return 0
 
     lax.fori_loop(0, 8, step, 0)
@@ -388,15 +404,17 @@
     prompt_kv, response_queries, resp_kv, readout, slot_response, lengths, pair_prompt, ref_margin
 ):
     near = copies_to_all(prompt_kv, "z")
-    place = lax.axis_index("c").astype(jnp.int32)[None]
     q, r, part = prepare(slot_response, lengths, response_queries, readout, resp_kv)
     near, q, r, part = lax.optimization_barrier((near, q, r, part))
     far = lax.ppermute(near, "c", [(0, 1), (1, 0)])
     stats, contrib = forward(slot_response, pair_prompt, q, r, part, near, far)
-    contribs = to_all(contrib, APART)
-    load = backward(slot_response, pair_prompt, place, q, r, stats, near, far)
+    contribs = to_all(contrib, SHARERS)
+    load, other = backward(slot_response, pair_prompt, q, r, stats, near, far)
+    got = lax.ppermute(other, "c", [(0, 1), (1, 0)])
+    load = lax.dynamic_update_slice(load, got, (0, HALF_ROWS, 0))
+    contribs, load = lax.optimization_barrier((contribs, load))
     share = jnp.sum(contribs, axis=0)
-    load = to_all(with_news(slot_response, share, load), CLOSE)
+    load = to_all(with_news(share, load), "x")
     dq, down, done = finish(slot_response, pair_prompt, q, r, stats, near, far, resp_kv)
     margins, weights, parts = weigh(
         ref_margin.reshape(4, HEAD), pair_prompt.reshape(4, HEAD), load, done
@@ -408,8 +426,8 @@
     grad_q = (own * dq.astype(f32)).astype(bf16)
     grad_own = (own * down.astype(f32)).astype(bf16)
     total = join(to_all(parts.reshape(64, 8, HEAD), APART))
-    total = to_all(total, RESP).reshape(8, 4, 2, 4, HEAD)
-    grad_prompt = jnp.transpose(total, (2, 0, 3, 1, 4)).reshape(2, 32, 512)
+    total = to_all(total, RESP).reshape(2, 4, 4, 8, HEAD)
+    grad_prompt = jnp.transpose(total, (0, 1, 3, 2, 4)).reshape(2, 32, 512)
     return margins.reshape(-1), grad_q, grad_own, grad_prompt
 
 

time: 119 us -> 129 us (1.084)
  waiting for transfers between devices: 46 us -> 54.8 us
    all_to_all x5, waiting for transfers between devices: 44.1 us -> 52.9 us  [to_all(): return lax.all_to_all(pieces, axes, 0, 0, tiled=True)]
    all_to_all x5, starting transfers between devices: 35.8 us -> 33.7 us  [to_all(): return lax.all_to_all(pieces, axes, 0, 0, tiled=True)]
    ppermute x0 -> x1, starting transfers between devices: none -> 2.03 us  [on_device(): got = lax.ppermute(other, 'c', [(0, 1), (1, 0)])]
  transfers between devices with their start and end apart: 6 -> 7, of which waited for: 6 -> 6; matrix products, arithmetic and copies ran while one was open for 2% -> 2% of each run, Pallas kernels for 16% -> 9%
where the time goes in v6:
time: 129 us; the launch traced here: 128 us
  waiting for transfers between devices  54.8 us (42%)
  starting transfers between devices  37.6 us (29%)
  Pallas kernels  27.5 us (21%)
  local copies, waits for them, and re-layouts  4.91 us (4%)
  other arithmetic  2.4 us (2%)
    all_to_all x5, waiting for transfers between devices, to_all(): return lax.all_to_all(pieces, axes, 0, 0, tiled=True)  52.9 us
    all_to_all x5, starting transfers between devices, to_all(): return lax.all_to_all(pieces, axes, 0, 0, tiled=True)  33.7 us
    pallas_call x4, Pallas kernels, per_group(): pl.pallas_call(kernel, out_shape=out_shape, grid_spec=pltpu.PrefetchScala...  25.6 us
  transfers between devices with their start and end apart: 7, of which 6 were waited for; matrix products, arithmetic and copies ran while one was open for 2% of the time, Pallas kernels for 9%

profile of v6, /device:TPU:8, one launch (start us, length us, event | category | flops | bytes accessed | tf_op | source)
XLA Modules:
  0.0 128.0 jit_solution(15707889249162090690)
XLA Ops:
  0.7 1.7 %broadcast_in_dim.32 = bf16[8,2,32,512]{3,2,1,0:T(8,128)(2,1)} broadcast(bf16[2,32,512]{2,1,0:T(8,128)(2,1)} %param.8), dimensions={1,2,3} | broadcast | bytes 589824 | tf_op jit(solution)/shard_map/broadcast_in_dim | solution.py:400
  2.4 10.3 %all-to-all-start = ((bf16[8,2,32,512]{3,2,1,0:T(8,128)(2,1)}), bf16[8,2,32,512]{3,2,1,0:T(8,128)(2,1)S(1)}, u32[]{:S(2)}, u32[]{:S(2)}) async-start(bf16[8,2,32,512]{3,2,1,0:T(8,128)(2,1)} %broadcast_in_dim.32), calls=%async_computation | async-start | bytes 1048576 | tf_op jit(solution)/shard_map/all_to_all | solution.py:395
  12.7 4.5 %prepare.1 = (bf16[4,896,128]{2,1,0:T(8,128)(2,1)S(1)}, bf16[4,896,128]{2,1,0:T(8,128)(2,1)}, f32[4,8,896]{2,1,0:T(8,128)S(1)}) custom-call(s32[2]{0:T(128)S(1)} %copy-done.4, s32[1024]{0:T(1024)S(1)} %copy-done.1, bf16[2,128,1792]{2,1,0:T(8,128)(2,1)} %q_ref.1, bf16[2,128,1792]{2,1,0:T(8,128)(2,1)} %r_ref.1, bf16[2,128,512]{2,1,0:T(8,128)(2,1)S(1)} %copy-done), custom_call_target="tpu_custom_call" | custom-call | flops 240000000 | bytes 4000000 | tf_op jit(solution)/shard_map/prepare/pallas_call | solution.py:220
  17.2 0.9 copy-done.5
  18.1 12.1 %all-to-all-done.near_ref = bf16[8,2,32,512]{3,2,1,0:T(8,128)(2,1)S(1)} async-done(((bf16[8,2,32,512]{3,2,1,0:T(8,128)(2,1)}), bf16[8,2,32,512]{3,2,1,0:T(8,128)(2,1)S(1)}, u32[]{:S(2)}, u32[]{:S(2)}) %all-to-all-start) | async-done | bytes 524320 | tf_op jit(solution)/shard_map/all_to_all | solution.py:395
  30.2 1.9 %collective-permute-start = (bf16[8,2,32,512]{3,2,1,0:T(8,128)(2,1)S(1)}, bf16[8,2,32,512]{3,2,1,0:T(8,128)(2,1)S(1)}, u32[]{:S(2)}, u32[]{:S(2)}) collective-permute-start(bf16[8,2,32,512]{3,2,1,0:T(8,128)(2,1)S(1)} %all-to-all-done.near_ref), channel_id=1, source_target_pairs={{0,32},{32,0},{1,33},{33,1},{2,34},{34,2},{3,35},{35,3},{4,36},{36... | collective-permute-start | bytes 1572872 | tf_op jit(solution)/shard_map/ppermute | solution.py:409
  32.1 1.9 %collective-permute-done.far_ref = bf16[8,2,32,512]{3,2,1,0:T(8,128)(2,1)S(1)} collective-permute-done((bf16[8,2,32,512]{3,2,1,0:T(8,128)(2,1)S(1)}, bf16[8,2,32,512]{3,2,1,0:T(8,128)(2,1)S(1)}, u32[]{:S(2)}, u32[]{:S(2)}) %collective-permute-start) | collective-permute-done | bytes 524320 | tf_op jit(solution)/shard_map/ppermute | solution.py:409
  34.0 6.3 %forward.1 = (f32[4,8,896]{2,1,0:T(8,128)S(1)}, f32[128,4,128]{2,1,0:T(4,128)}) custom-call(s32[2]{0:T(128)S(1)} %copy-done.4, s32[512]{0:T(512)S(1)} %copy-done.3, bf16[4,896,128]{2,1,0:T(8,128)(2,1)} %copy-done.5, bf16[4,896,128]{2,1,0:T(8,128)(2,1)} %get-tuple-element.27.r_ref, f32[4,8,896]{2,1,0:T(8,128)S(1)} %get-tuple-element.28.part_ref, ...), custom_call_target="tpu_custom_call" | custom-call | flops 940000000 | bytes 4000000 | tf_op jit(solution)/shard_map/forward/pallas_call | solution.py:220
  40.3 7.6 %backward.1 = (bf16[4,1072,128]{2,1,0:T(8,128)(2,1)}, bf16[4,528,128]{2,1,0:T(8,128)(2,1)S(1)}) custom-call(s32[2]{0:T(128)S(1)} %copy-done.4, s32[512]{0:T(512)S(1)} %copy-done.3, bf16[4,896,128]{2,1,0:T(8,128)(2,1)} %copy-done.5, bf16[4,896,128]{2,1,0:T(8,128)(2,1)} %get-tuple-element.27.r_ref, f32[4,8,896]{2,1,0:T(8,128)S(1)} %get-tuple-element.31.stats_ref, ...), custom_call_target="tpu_custom_call" | custom-call | flops 1880000000 | bytes 4000000 | tf_op jit(solution)/shard_map/backward/pallas_call | solution.py:220
  47.9 2.0 %collective-permute-start.1 = (bf16[4,528,128]{2,1,0:T(8,128)(2,1)S(1)}, bf16[4,528,128]{2,1,0:T(8,128)(2,1)S(1)}, u32[]{:S(2)}, u32[]{:S(2)}) collective-permute-start(bf16[4,528,128]{2,1,0:T(8,128)(2,1)S(1)} %get-tuple-element.33), channel_id=1, source_target_pairs={{0,32},{32,0},{1,33},{33,1},{2,34},{34,2},{3,35},{35,3},{4,36},{36... | collective-permute-start | bytes 1622024 | tf_op jit(solution)/shard_map/ppermute | solution.py:413
  49.9 8.9 %all-to-all-start.1 = ((f32[128,4,128]{2,1,0:T(4,128)}), f32[128,4,128]{2,1,0:T(4,128)S(1)}, u32[]{:S(2)}, u32[]{:S(2)}) async-start(f32[128,4,128]{2,1,0:T(4,128)} %get-tuple-element.30), calls=%async_computation.1 | async-start | bytes 524288 | tf_op jit(solution)/shard_map/all_to_all | solution.py:395
  59.0 0.9 constant_dynamic-update-slice_fusion
  59.9 13.2 %all-to-all-done.1 = f32[128,4,128]{2,1,0:T(4,128)S(1)} async-done(((f32[128,4,128]{2,1,0:T(4,128)}), f32[128,4,128]{2,1,0:T(4,128)S(1)}, u32[]{:S(2)}, u32[]{:S(2)}) %all-to-all-start.1) | async-done | bytes 262176 | tf_op jit(solution)/shard_map/all_to_all | solution.py:395
  73.9 4.3 %all-to-all-start.2 = ((bf16[4,1072,128]{2,1,0:T(8,128)(2,1)}), bf16[4,1072,128]{2,1,0:T(8,128)(2,1)S(1)}, u32[]{:S(2)}, u32[]{:S(2)}) async-start(bf16[4,1072,128]{2,1,0:T(8,128)(2,1)} %broadcast_dynamic-update-slice_fusion), calls=%async_computation.2 | async-start | bytes 2195456 | tf_op jit(solution)/shard_map/all_to_all | solution.py:395
  78.2 7.3 %finish.1 = (bf16[2,128,1792]{2,1,0:T(8,128)(2,1)}, bf16[2,128,512]{2,1,0:T(8,128)(2,1)S(1)}, f32[8,128]{1,0:T(8,128)S(1)}) custom-call(s32[2]{0:T(128)S(1)} %copy-done.4, s32[512]{0:T(512)S(1)} %copy-done.3, bf16[4,896,128]{2,1,0:T(8,128)(2,1)} %copy-done.5, bf16[4,896,128]{2,1,0:T(8,128)(2,1)} %get-tuple-element.27.r_ref, ...), custom_call_target="tpu_custom_call" | custom-call | flops 2000000000 | bytes 4000000 | tf_op jit(solution)/shard_map/finish/pallas_call | solution.py:220
  85.5 8.6 %all-to-all-done.2.load_ref = bf16[4,1072,128]{2,1,0:T(8,128)(2,1)S(1)} async-done(((bf16[4,1072,128]{2,1,0:T(8,128)(2,1)}), bf16[4,1072,128]{2,1,0:T(8,128)(2,1)S(1)}, u32[]{:S(2)}, u32[]{:S(2)}) %all-to-all-start.2) | async-done | bytes 1097760 | tf_op jit(solution)/shard_map/all_to_all | solution.py:395
  94.1 1.2 weigh.1
  95.5 5.3 %all-to-all-start.3 = ((bf16[64,8,128]{2,1,0:T(8,128)(2,1)}), bf16[64,8,128]{2,1,0:T(8,128)(2,1)S(1)}, u32[]{:S(2)}, u32[]{:S(2)}) async-start(bf16[64,8,128]{2,1,0:T(8,128)(2,1)} %bitcast.4), calls=%async_computation.3 | async-start | bytes 262144 | tf_op jit(solution)/shard_map/all_to_all | solution.py:395
  100.9 1.1 multiply_convert_fusion
  102.0 10.7 %all-to-all-done.3.parts_ref = bf16[64,8,128]{2,1,0:T(8,128)(2,1)S(1)} async-done(((bf16[64,8,128]{2,1,0:T(8,128)(2,1)}), bf16[64,8,128]{2,1,0:T(8,128)(2,1)S(1)}, u32[]{:S(2)}, u32[]{:S(2)}) %all-to-all-start.3) | async-done | bytes 131104 | tf_op jit(solution)/shard_map/all_to_all | solution.py:395
  112.8 0.7 join.1
  113.5 4.8 %all-to-all-start.4 = ((bf16[32,8,128]{2,1,0:T(8,128)(2,1)}), bf16[32,8,128]{2,1,0:T(8,128)(2,1)S(1)}, u32[]{:S(2)}, u32[]{:S(2)}) async-start(bf16[32,8,128]{2,1,0:T(8,128)(2,1)} %join.1), calls=%async_computation.4 | async-start | bytes 131072 | tf_op jit(solution)/shard_map/all_to_all | solution.py:395
  118.3 0.8 multiply_convert_fusion.1
  119.1 8.3 %all-to-all-done.4 = bf16[32,8,128]{2,1,0:T(8,128)(2,1)S(1)} async-done(((bf16[32,8,128]{2,1,0:T(8,128)(2,1)}), bf16[32,8,128]{2,1,0:T(8,128)(2,1)S(1)}, u32[]{:S(2)}, u32[]{:S(2)}) %all-to-all-start.4) | async-done | bytes 65568 | tf_op jit(solution)/shard_map/all_to_all | solution.py:395
  (24 shorter events, 1.8 us)
Async XLA Ops:
  0.6 12.1 %copy-start.4 = (s32[2]{0:T(128)S(1)}, s32[2]{0:T(128)}, u32[]{:S(2)}) copy-start(s32[2]{0:T(128)} %response_ref.7) | copy-start | bytes 28
  0.6 12.1 %copy-start.1 = (s32[1024]{0:T(1024)S(1)}, s32[1024]{0:T(1024)}, u32[]{:S(2)}) copy-start(s32[1024]{0:T(1024)} %lengths_ref.1) | copy-start | bytes 12292
  0.7 12.1 %copy-start = (bf16[2,128,512]{2,1,0:T(8,128)(2,1)S(1)}, bf16[2,128,512]{2,1,0:T(8,128)(2,1)}, u32[]{:S(2)}) copy-start(bf16[2,128,512]{2,1,0:T(8,128)(2,1)} %own_ref.3) | copy-start | bytes 786436
  2.4 27.8 %all-to-all-start = ((bf16[8,2,32,512]{3,2,1,0:T(8,128)(2,1)}), bf16[8,2,32,512]{3,2,1,0:T(8,128)(2,1)S(1)}, u32[]{:S(2)}, u32[]{:S(2)}) async-start(bf16[8,2,32,512]{3,2,1,0:T(8,128)(2,1)} %broadcast_in_dim.32), calls=%async_computation | async-start | bytes 1048576 | tf_op jit(solution)/shard_map/all_to_all | solution.py:395
  12.7 21.3 %copy-start.3 = (s32[512]{0:T(512)S(1)}, s32[512]{0:T(512)}, u32[]{:S(2)}) copy-start(s32[512]{0:T(512)} %pair_prompt_ref.5) | copy-start | bytes 6148
  17.2 0.9 copy-start.5
  30.2 3.8 %collective-permute-start = (bf16[8,2,32,512]{3,2,1,0:T(8,128)(2,1)S(1)}, bf16[8,2,32,512]{3,2,1,0:T(8,128)(2,1)S(1)}, u32[]{:S(2)}, u32[]{:S(2)}) collective-permute-start(bf16[8,2,32,512]{3,2,1,0:T(8,128)(2,1)S(1)} %all-to-all-done.near_ref), channel_id=1, source_target_pairs={{0,32},{32,0},{1,33},{33,1},{2,34},{34,2},{3,35},{35,3},{4,36},{36... | collective-permute-start | bytes 1572872 | tf_op jit(solution)/shard_map/ppermute | solution.py:409
  47.9 11.1 %collective-permute-start.1 = (bf16[4,528,128]{2,1,0:T(8,128)(2,1)S(1)}, bf16[4,528,128]{2,1,0:T(8,128)(2,1)S(1)}, u32[]{:S(2)}, u32[]{:S(2)}) collective-permute-start(bf16[4,528,128]{2,1,0:T(8,128)(2,1)S(1)} %get-tuple-element.33), channel_id=1, source_target_pairs={{0,32},{32,0},{1,33},{33,1},{2,34},{34,2},{3,35},{35,3},{4,36},{36... | collective-permute-start | bytes 1622024 | tf_op jit(solution)/shard_map/ppermute | solution.py:413
  49.9 23.1 %all-to-all-start.1 = ((f32[128,4,128]{2,1,0:T(4,128)}), f32[128,4,128]{2,1,0:T(4,128)S(1)}, u32[]{:S(2)}, u32[]{:S(2)}) async-start(f32[128,4,128]{2,1,0:T(4,128)} %get-tuple-element.30), calls=%async_computation.1 | async-start | bytes 524288 | tf_op jit(solution)/shard_map/all_to_all | solution.py:395
  73.9 20.2 %all-to-all-start.2 = ((bf16[4,1072,128]{2,1,0:T(8,128)(2,1)}), bf16[4,1072,128]{2,1,0:T(8,128)(2,1)S(1)}, u32[]{:S(2)}, u32[]{:S(2)}) async-start(bf16[4,1072,128]{2,1,0:T(8,128)(2,1)} %broadcast_dynamic-update-slice_fusion), calls=%async_computation.2 | async-start | bytes 2195456 | tf_op jit(solution)/shard_map/all_to_all | solution.py:395
  78.2 15.9 %copy-start.2 = (f32[512]{0:T(512)S(1)}, f32[512]{0:T(512)}, u32[]{:S(2)}) copy-start(f32[512]{0:T(512)} %param.15) | copy-start | bytes 6148
  85.5 15.4 %copy-start.6 = (bf16[2,128,1792]{2,1,0:T(8,128)(2,1)S(1)}, bf16[2,128,1792]{2,1,0:T(8,128)(2,1)}, u32[]{:S(2)}) copy-start(bf16[2,128,1792]{2,1,0:T(8,128)(2,1)} %get-tuple-element.39) | copy-start | bytes 2752516
  95.5 17.2 %all-to-all-start.3 = ((bf16[64,8,128]{2,1,0:T(8,128)(2,1)}), bf16[64,8,128]{2,1,0:T(8,128)(2,1)S(1)}, u32[]{:S(2)}, u32[]{:S(2)}) async-start(bf16[64,8,128]{2,1,0:T(8,128)(2,1)} %bitcast.4), calls=%async_computation.3 | async-start | bytes 262144 | tf_op jit(solution)/shard_map/all_to_all | solution.py:395
  113.5 13.9 %all-to-all-start.4 = ((bf16[32,8,128]{2,1,0:T(8,128)(2,1)}), bf16[32,8,128]{2,1,0:T(8,128)(2,1)S(1)}, u32[]{:S(2)}, u32[]{:S(2)}) async-start(bf16[32,8,128]{2,1,0:T(8,128)(2,1)} %join.1), calls=%async_computation.4 | async-start | bytes 131072 | tf_op jit(solution)/shard_map/all_to_all | solution.py:395

commit v7 on v4

--- a/solution.py
+++ b/solution.py
@@ -332,8 +332,8 @@
                 at = source * 2 + slot
                 for p in range(2):
                     sums[p] = sums[p] + factor_s[p, at : at + 1, :] * piece
-        both = jnp.concatenate([s.reshape(8, 1, 4, HEAD) for s in sums], axis=1)
-        out_ref[z] = both.reshape(8, 8, HEAD).astype(bf16)
+        for p in range(2):
+            out_ref[z, p * 4 : p * 4 + 4] = sums[p].reshape(4, 8, HEAD).astype(bf16)
         return 0
 
     lax.fori_loop(0, 8, step, 0)
@@ -408,8 +408,8 @@
     grad_q = (own * dq.astype(f32)).astype(bf16)
     grad_own = (own * down.astype(f32)).astype(bf16)
     total = join(to_all(parts.reshape(64, 8, HEAD), APART))
-    total = to_all(total, RESP).reshape(8, 4, 2, 4, HEAD)
-    grad_prompt = jnp.transpose(total, (2, 0, 3, 1, 4)).reshape(2, 32, 512)
+    total = to_all(total, RESP).reshape(2, 4, 4, 8, HEAD)
+    grad_prompt = jnp.transpose(total, (0, 1, 3, 2, 4)).reshape(2, 32, 512)
     return margins.reshape(-1), grad_q, grad_own, grad_prompt
 
 

time: 119 us -> 119 us (level)
  no operation moved by 1% of the time
where the time goes in v7:
time: 119 us; the launch traced here: 118 us
  waiting for transfers between devices  46 us (39%)
  starting transfers between devices  37.7 us (32%)
  Pallas kernels  27.5 us (23%)
  local copies, waits for them, and re-layouts  4.22 us (4%)
  other arithmetic  2.34 us (2%)
    all_to_all x5, waiting for transfers between devices, to_all(): return lax.all_to_all(pieces, axes, 0, 0, tiled=True)  44.1 us
    all_to_all x5, starting transfers between devices, to_all(): return lax.all_to_all(pieces, axes, 0, 0, tiled=True)  35.8 us
    pallas_call x4, Pallas kernels, per_group(): pl.pallas_call(kernel, out_shape=out_shape, grid_spec=pltpu.PrefetchScala...  25.5 us
  transfers between devices with their start and end apart: 6, of which 6 were waited for; matrix products, arithmetic and copies ran while one was open for 2% of the time, Pallas kernels for 16%

profile of v7, /device:TPU:8, one launch (start us, length us, event | category | flops | bytes accessed | tf_op | source)
XLA Modules:
  0.0 118.4 jit_solution(12893594272013665863)
XLA Ops:
  0.7 1.7 %broadcast_in_dim.17 = bf16[8,2,32,512]{3,2,1,0:T(8,128)(2,1)} broadcast(bf16[2,32,512]{2,1,0:T(8,128)(2,1)} %param.8), dimensions={1,2,3} | broadcast | bytes 589824 | tf_op jit(solution)/shard_map/broadcast_in_dim | solution.py:384
  2.4 10.3 %all-to-all-start = ((bf16[8,2,32,512]{3,2,1,0:T(8,128)(2,1)}), bf16[8,2,32,512]{3,2,1,0:T(8,128)(2,1)S(1)}, u32[]{:S(2)}, u32[]{:S(2)}) async-start(bf16[8,2,32,512]{3,2,1,0:T(8,128)(2,1)} %broadcast_in_dim.17), calls=%async_computation | async-start | bytes 1048576 | tf_op jit(solution)/shard_map/all_to_all | solution.py:379
  12.8 4.5 %prepare.1 = (bf16[4,896,128]{2,1,0:T(8,128)(2,1)S(1)}, bf16[4,896,128]{2,1,0:T(8,128)(2,1)}, f32[4,8,896]{2,1,0:T(8,128)S(1)}) custom-call(s32[2]{0:T(128)S(1)} %copy-done.4, s32[1024]{0:T(1024)S(1)} %copy-done.1, bf16[2,128,1792]{2,1,0:T(8,128)(2,1)} %q_ref.1, bf16[2,128,1792]{2,1,0:T(8,128)(2,1)} %r_ref.1, bf16[2,128,512]{2,1,0:T(8,128)(2,1)S(1)} %copy-done), custom_call_target="tpu_custom_call" | custom-call | flops 240000000 | bytes 4000000 | tf_op jit(solution)/shard_map/prepare/pallas_call | solution.py:208
  17.2 0.9 copy-done.5
  18.2 12.1 %all-to-all-done.near_ref = bf16[8,2,32,512]{3,2,1,0:T(8,128)(2,1)S(1)} async-done(((bf16[8,2,32,512]{3,2,1,0:T(8,128)(2,1)}), bf16[8,2,32,512]{3,2,1,0:T(8,128)(2,1)S(1)}, u32[]{:S(2)}, u32[]{:S(2)}) %all-to-all-start) | async-done | bytes 524320 | tf_op jit(solution)/shard_map/all_to_all | solution.py:379
  30.2 1.9 %collective-permute-start = (bf16[8,2,32,512]{3,2,1,0:T(8,128)(2,1)S(1)}, bf16[8,2,32,512]{3,2,1,0:T(8,128)(2,1)S(1)}, u32[]{:S(2)}, u32[]{:S(2)}) collective-permute-start(bf16[8,2,32,512]{3,2,1,0:T(8,128)(2,1)S(1)} %all-to-all-done.near_ref), channel_id=1, source_target_pairs={{0,32},{32,0},{1,33},{33,1},{2,34},{34,2},{3,35},{35,3},{4,36},{36... | collective-permute-start | bytes 1572872 | tf_op jit(solution)/shard_map/ppermute | solution.py:394
  32.2 1.8 %collective-permute-done.far_ref = bf16[8,2,32,512]{3,2,1,0:T(8,128)(2,1)S(1)} collective-permute-done((bf16[8,2,32,512]{3,2,1,0:T(8,128)(2,1)S(1)}, bf16[8,2,32,512]{3,2,1,0:T(8,128)(2,1)S(1)}, u32[]{:S(2)}, u32[]{:S(2)}) %collective-permute-start) | collective-permute-done | bytes 524320 | tf_op jit(solution)/shard_map/ppermute | solution.py:394
  34.0 6.2 %forward.1 = (f32[4,8,896]{2,1,0:T(8,128)S(1)}, f32[64,4,128]{2,1,0:T(4,128)}) custom-call(s32[2]{0:T(128)S(1)} %copy-done.4, s32[512]{0:T(512)S(1)} %copy-done.3, bf16[4,896,128]{2,1,0:T(8,128)(2,1)} %copy-done.5, bf16[4,896,128]{2,1,0:T(8,128)(2,1)} %get-tuple-element.23.r_ref, f32[4,8,896]{2,1,0:T(8,128)S(1)} %get-tuple-element.24.part_ref, ...), custom_call_target="tpu_custom_call" | custom-call | flops 940000000 | bytes 4000000 | tf_op jit(solution)/shard_map/forward/pallas_call | solution.py:208
  40.3 8.1 %all-to-all-start.1 = ((f32[64,4,128]{2,1,0:T(4,128)}), f32[64,4,128]{2,1,0:T(4,128)S(1)}, u32[]{:S(2)}, u32[]{:S(2)}) async-start(f32[64,4,128]{2,1,0:T(4,128)} %get-tuple-element.27), calls=%async_computation.1 | async-start | bytes 262144 | tf_op jit(solution)/shard_map/all_to_all | solution.py:379
  48.7 7.6 %backward.1 = bf16[8,528,128]{2,1,0:T(8,128)(2,1)} custom-call(s32[2]{0:T(128)S(1)} %copy-done.4, s32[512]{0:T(512)S(1)} %copy-done.3, s32[1]{0:T(128)} %bitcast.2.place_ref, bf16[4,896,128]{2,1,0:T(8,128)(2,1)} %copy-done.5, bf16[4,896,128]{2,1,0:T(8,128)(2,1)} %get-tuple-element.23.r_ref, f32[4,8,896]{2,1,0:T(8,128)S(1)} %get-tuple-element.26.stats_ref, ...), custom_call_target="tpu_custom_call" | custom-call | flops 1880000000 | bytes 4000000 | tf_op jit(solution)/shard_map/backward/pallas_call | solution.py:208
  56.2 4.3 %all-to-all-done.1 = f32[64,4,128]{2,1,0:T(4,128)S(1)} async-done(((f32[64,4,128]{2,1,0:T(4,128)}), f32[64,4,128]{2,1,0:T(4,128)S(1)}, u32[]{:S(2)}, u32[]{:S(2)}) %all-to-all-start.1) | async-done | bytes 131104 | tf_op jit(solution)/shard_map/all_to_all | solution.py:379
  60.7 0.6 broadcast_dynamic-update-slice_fusion
  61.3 4.3 %all-to-all-start.2 = ((bf16[8,528,128]{2,1,0:T(8,128)(2,1)}), bf16[8,528,128]{2,1,0:T(8,128)(2,1)S(1)}, u32[]{:S(2)}, u32[]{:S(2)}) async-start(bf16[8,528,128]{2,1,0:T(8,128)(2,1)} %broadcast_dynamic-update-slice_fusion), calls=%async_computation.2 | async-start | bytes 2162688 | tf_op jit(solution)/shard_map/all_to_all | solution.py:379
  65.6 7.2 %finish.1 = (bf16[2,128,1792]{2,1,0:T(8,128)(2,1)}, bf16[2,128,512]{2,1,0:T(8,128)(2,1)S(1)}, f32[8,128]{1,0:T(8,128)S(1)}) custom-call(s32[2]{0:T(128)S(1)} %copy-done.4, s32[512]{0:T(512)S(1)} %copy-done.3, bf16[4,896,128]{2,1,0:T(8,128)(2,1)} %copy-done.5, bf16[4,896,128]{2,1,0:T(8,128)(2,1)} %get-tuple-element.23.r_ref, ...), custom_call_target="tpu_custom_call" | custom-call | flops 2000000000 | bytes 4000000 | tf_op jit(solution)/shard_map/finish/pallas_call | solution.py:208
  72.9 8.4 %all-to-all-done.2.load_ref = bf16[8,528,128]{2,1,0:T(8,128)(2,1)S(1)} async-done(((bf16[8,528,128]{2,1,0:T(8,128)(2,1)}), bf16[8,528,128]{2,1,0:T(8,128)(2,1)S(1)}, u32[]{:S(2)}, u32[]{:S(2)}) %all-to-all-start.2) | async-done | bytes 1081376 | tf_op jit(solution)/shard_map/all_to_all | solution.py:379
  81.3 1.2 %weigh.1 = (f32[4,128]{1,0:T(4,128)}, f32[4,128]{1,0:T(4,128)S(1)}, bf16[8,8,8,128]{3,2,1,0:T(8,128)(2,1)}) custom-call(f32[4,128]{1,0:T(4,128)S(1)} %bitcast.15, s32[4,128]{1,0:T(4,128)S(1)} %bitcast.16, bf16[8,528,128]{2,1,0:T(8,128)(2,1)S(1)} %all-to-all-done.2.load_ref, f32[8,128]{1,0:T(8,128)S(1)} %get-tuple-element.28.done_ref), custom_call_target="tpu_custom_call" | custom-call | tf_op jit(solution)/shard_map/weigh/pallas_call | solution.py:344
  82.8 8.4 %all-to-all-start.3 = ((bf16[64,8,128]{2,1,0:T(8,128)(2,1)}), bf16[64,8,128]{2,1,0:T(8,128)(2,1)S(1)}, u32[]{:S(2)}, u32[]{:S(2)}) async-start(bf16[64,8,128]{2,1,0:T(8,128)(2,1)} %bitcast.7), calls=%async_computation.3 | async-start | bytes 262144 | tf_op jit(solution)/shard_map/all_to_all | solution.py:379
  91.2 1.1 multiply_convert_fusion
  92.3 11.0 %all-to-all-done.3.parts_ref = bf16[64,8,128]{2,1,0:T(8,128)(2,1)S(1)} async-done(((bf16[64,8,128]{2,1,0:T(8,128)(2,1)}), bf16[64,8,128]{2,1,0:T(8,128)(2,1)S(1)}, u32[]{:S(2)}, u32[]{:S(2)}) %all-to-all-start.3) | async-done | bytes 131104 | tf_op jit(solution)/shard_map/all_to_all | solution.py:379
  103.3 0.7 join.1
  104.0 4.7 %all-to-all-start.4 = ((bf16[32,8,128]{2,1,0:T(8,128)(2,1)}), bf16[32,8,128]{2,1,0:T(8,128)(2,1)S(1)}, u32[]{:S(2)}, u32[]{:S(2)}) async-start(bf16[32,8,128]{2,1,0:T(8,128)(2,1)} %join.1), calls=%async_computation.4 | async-start | bytes 131072 | tf_op jit(solution)/shard_map/all_to_all | solution.py:379
  108.7 0.8 multiply_convert_fusion.1
  109.5 8.3 %all-to-all-done.4 = bf16[32,8,128]{2,1,0:T(8,128)(2,1)S(1)} async-done(((bf16[32,8,128]{2,1,0:T(8,128)(2,1)}), bf16[32,8,128]{2,1,0:T(8,128)(2,1)S(1)}, u32[]{:S(2)}, u32[]{:S(2)}) %all-to-all-start.4) | async-done | bytes 65568 | tf_op jit(solution)/shard_map/all_to_all | solution.py:379
  117.8 0.6 copy.16
  (23 shorter events, 0.7 us)
Async XLA Ops:
  0.6 12.1 %copy-start.4 = (s32[2]{0:T(128)S(1)}, s32[2]{0:T(128)}, u32[]{:S(2)}) copy-start(s32[2]{0:T(128)} %response_ref.7) | copy-start | bytes 28
  0.6 12.1 %copy-start.1 = (s32[1024]{0:T(1024)S(1)}, s32[1024]{0:T(1024)}, u32[]{:S(2)}) copy-start(s32[1024]{0:T(1024)} %lengths_ref.1) | copy-start | bytes 12292
  0.7 12.1 %copy-start = (bf16[2,128,512]{2,1,0:T(8,128)(2,1)S(1)}, bf16[2,128,512]{2,1,0:T(8,128)(2,1)}, u32[]{:S(2)}) copy-start(bf16[2,128,512]{2,1,0:T(8,128)(2,1)} %own_ref.3) | copy-start | bytes 786436
  2.4 27.8 %all-to-all-start = ((bf16[8,2,32,512]{3,2,1,0:T(8,128)(2,1)}), bf16[8,2,32,512]{3,2,1,0:T(8,128)(2,1)S(1)}, u32[]{:S(2)}, u32[]{:S(2)}) async-start(bf16[8,2,32,512]{3,2,1,0:T(8,128)(2,1)} %broadcast_in_dim.17), calls=%async_computation | async-start | bytes 1048576 | tf_op jit(solution)/shard_map/all_to_all | solution.py:379
  12.7 21.3 %copy-start.3 = (s32[512]{0:T(512)S(1)}, s32[512]{0:T(512)}, u32[]{:S(2)}) copy-start(s32[512]{0:T(512)} %pair_prompt_ref.5) | copy-start | bytes 6148
  17.2 0.9 copy-start.5
  30.2 3.8 %collective-permute-start = (bf16[8,2,32,512]{3,2,1,0:T(8,128)(2,1)S(1)}, bf16[8,2,32,512]{3,2,1,0:T(8,128)(2,1)S(1)}, u32[]{:S(2)}, u32[]{:S(2)}) collective-permute-start(bf16[8,2,32,512]{3,2,1,0:T(8,128)(2,1)S(1)} %all-to-all-done.near_ref), channel_id=1, source_target_pairs={{0,32},{32,0},{1,33},{33,1},{2,34},{34,2},{3,35},{35,3},{4,36},{36... | collective-permute-start | bytes 1572872 | tf_op jit(solution)/shard_map/ppermute | solution.py:394
  40.3 20.3 %all-to-all-start.1 = ((f32[64,4,128]{2,1,0:T(4,128)}), f32[64,4,128]{2,1,0:T(4,128)S(1)}, u32[]{:S(2)}, u32[]{:S(2)}) async-start(f32[64,4,128]{2,1,0:T(4,128)} %get-tuple-element.27), calls=%async_computation.1 | async-start | bytes 262144 | tf_op jit(solution)/shard_map/all_to_all | solution.py:379
  61.3 20.0 %all-to-all-start.2 = ((bf16[8,528,128]{2,1,0:T(8,128)(2,1)}), bf16[8,528,128]{2,1,0:T(8,128)(2,1)S(1)}, u32[]{:S(2)}, u32[]{:S(2)}) async-start(bf16[8,528,128]{2,1,0:T(8,128)(2,1)} %broadcast_dynamic-update-slice_fusion), calls=%async_computation.2 | async-start | bytes 2162688 | tf_op jit(solution)/shard_map/all_to_all | solution.py:379
  65.6 15.7 %copy-start.2 = (f32[512]{0:T(512)S(1)}, f32[512]{0:T(512)}, u32[]{:S(2)}) copy-start(f32[512]{0:T(512)} %param.15) | copy-start | bytes 6148
  72.9 18.3 %copy-start.6 = (bf16[2,128,1792]{2,1,0:T(8,128)(2,1)S(1)}, bf16[2,128,1792]{2,1,0:T(8,128)(2,1)}, u32[]{:S(2)}) copy-start(bf16[2,128,1792]{2,1,0:T(8,128)(2,1)} %get-tuple-element.31) | copy-start | bytes 2752516
  82.8 20.6 %all-to-all-start.3 = ((bf16[64,8,128]{2,1,0:T(8,128)(2,1)}), bf16[64,8,128]{2,1,0:T(8,128)(2,1)S(1)}, u32[]{:S(2)}, u32[]{:S(2)}) async-start(bf16[64,8,128]{2,1,0:T(8,128)(2,1)} %bitcast.7), calls=%async_computation.3 | async-start | bytes 262144 | tf_op jit(solution)/shard_map/all_to_all | solution.py:379
  104.0 13.8 %all-to-all-start.4 = ((bf16[32,8,128]{2,1,0:T(8,128)(2,1)}), bf16[32,8,128]{2,1,0:T(8,128)(2,1)S(1)}, u32[]{:S(2)}, u32[]{:S(2)}) async-start(bf16[32,8,128]{2,1,0:T(8,128)(2,1)} %join.1), calls=%async_computation.4 | async-start | bytes 131072 | tf_op jit(solution)/shard_map/all_to_all | solution.py:379

commit v8 on v5

--- a/solution.py
+++ b/solution.py
@@ -392,13 +392,13 @@
 
 def copies_to_all(shard, axes):
     size = lax.axis_size(axes)
-    hbm = pl.BlockSpec(memory_space=pltpu.HBM)
     repeated = pl.pallas_call(
         repeat_kernel,
         out_shape=jax.ShapeDtypeStruct((size, *shard.shape), shard.dtype),
-        in_specs=[hbm],
-        out_specs=hbm,
+        in_specs=[pl.BlockSpec(memory_space=pltpu.VMEM)],
+        out_specs=pl.BlockSpec(memory_space=pltpu.HBM),
         scratch_shapes=[pltpu.SemaphoreType.DMA((size,))],
+        compiler_params=pltpu.CompilerParams(vmem_limit_bytes=58 << 20),
         name="repeat",
     )(shard)
     return to_all(repeated, axes)

time: 134 us -> 119 us (0.89)
  Pallas kernels: 44.5 us -> 29.2 us
    pallas_call x1, Pallas kernels: 17.1 us -> 1.76 us  [copies_to_all(): pl.pallas_call(repeat_kernel, out_shape=jax.ShapeDtypeStruct((size, *shar...]
  transfers between devices with their start and end apart: 6 -> 6, of which waited for: 6 -> 6; matrix products, arithmetic and copies ran while one was open for 2% -> 2% of each run, Pallas kernels for 14% -> 16%
where the time goes in v8:
time: 119 us; the launch traced here: 118 us
  waiting for transfers between devices  46 us (39%)
  starting transfers between devices  37.7 us (32%)
  Pallas kernels  29.2 us (25%)
  local copies, waits for them, and re-layouts  2.48 us (2%)
  other arithmetic  2.34 us (2%)
    all_to_all x5, waiting for transfers between devices, to_all(): return lax.all_to_all(pieces, axes, 0, 0, tiled=True)  44.1 us
    all_to_all x5, starting transfers between devices, to_all(): return lax.all_to_all(pieces, axes, 0, 0, tiled=True)  35.8 us
    pallas_call x4, Pallas kernels, per_group(): pl.pallas_call(kernel, out_shape=out_shape, grid_spec=pltpu.PrefetchScala...  25.5 us
  transfers between devices with their start and end apart: 6, of which 6 were waited for; matrix products, arithmetic and copies ran while one was open for 2% of the time, Pallas kernels for 16%

profile of v8, /device:TPU:8, one launch (start us, length us, event | category | flops | bytes accessed | tf_op | source)
XLA Modules:
  0.0 118.5 jit_solution(834734283358303835)
XLA Ops:
  0.7 1.8 %repeat.1 = bf16[8,2,32,512]{3,2,1,0:T(8,128)(2,1)} custom-call(bf16[2,32,512]{2,1,0:T(8,128)(2,1)} %shard_ref.1), custom_call_target="tpu_custom_call" | custom-call | tf_op jit(solution)/shard_map/repeat/pallas_call | solution.py:395
  2.4 10.3 %all-to-all-start = ((bf16[8,2,32,512]{3,2,1,0:T(8,128)(2,1)}), bf16[8,2,32,512]{3,2,1,0:T(8,128)(2,1)S(1)}, u32[]{:S(2)}, u32[]{:S(2)}) async-start(bf16[8,2,32,512]{3,2,1,0:T(8,128)(2,1)} %repeat.1), calls=%async_computation | async-start | bytes 1048576 | tf_op jit(solution)/shard_map/all_to_all | solution.py:379
  12.8 4.5 %prepare.1 = (bf16[4,896,128]{2,1,0:T(8,128)(2,1)S(1)}, bf16[4,896,128]{2,1,0:T(8,128)(2,1)}, f32[4,8,896]{2,1,0:T(8,128)S(1)}) custom-call(s32[2]{0:T(128)S(1)} %copy-done.4, s32[1024]{0:T(1024)S(1)} %copy-done.1, bf16[2,128,1792]{2,1,0:T(8,128)(2,1)} %q_ref.1, bf16[2,128,1792]{2,1,0:T(8,128)(2,1)} %r_ref.1, bf16[2,128,512]{2,1,0:T(8,128)(2,1)S(1)} %copy-done), custom_call_target="tpu_custom_call" | custom-call | flops 240000000 | bytes 4000000 | tf_op jit(solution)/shard_map/prepare/pallas_call | solution.py:208
  17.3 0.9 copy-done.5
  18.2 12.1 %all-to-all-done.near_ref = bf16[8,2,32,512]{3,2,1,0:T(8,128)(2,1)S(1)} async-done(((bf16[8,2,32,512]{3,2,1,0:T(8,128)(2,1)}), bf16[8,2,32,512]{3,2,1,0:T(8,128)(2,1)S(1)}, u32[]{:S(2)}, u32[]{:S(2)}) %all-to-all-start) | async-done | bytes 524320 | tf_op jit(solution)/shard_map/all_to_all | solution.py:379
  30.3 1.9 %collective-permute-start = (bf16[8,2,32,512]{3,2,1,0:T(8,128)(2,1)S(1)}, bf16[8,2,32,512]{3,2,1,0:T(8,128)(2,1)S(1)}, u32[]{:S(2)}, u32[]{:S(2)}) collective-permute-start(bf16[8,2,32,512]{3,2,1,0:T(8,128)(2,1)S(1)} %all-to-all-done.near_ref), channel_id=1, source_target_pairs={{0,32},{32,0},{1,33},{33,1},{2,34},{34,2},{3,35},{35,3},{4,36},{36... | collective-permute-start | bytes 1572872 | tf_op jit(solution)/shard_map/ppermute | solution.py:414
  32.2 1.8 %collective-permute-done.far_ref = bf16[8,2,32,512]{3,2,1,0:T(8,128)(2,1)S(1)} collective-permute-done((bf16[8,2,32,512]{3,2,1,0:T(8,128)(2,1)S(1)}, bf16[8,2,32,512]{3,2,1,0:T(8,128)(2,1)S(1)}, u32[]{:S(2)}, u32[]{:S(2)}) %collective-permute-start) | collective-permute-done | bytes 524320 | tf_op jit(solution)/shard_map/ppermute | solution.py:414
  34.0 6.2 %forward.1 = (f32[4,8,896]{2,1,0:T(8,128)S(1)}, f32[64,4,128]{2,1,0:T(4,128)}) custom-call(s32[2]{0:T(128)S(1)} %copy-done.4, s32[512]{0:T(512)S(1)} %copy-done.3, bf16[4,896,128]{2,1,0:T(8,128)(2,1)} %copy-done.5, bf16[4,896,128]{2,1,0:T(8,128)(2,1)} %get-tuple-element.23.r_ref, f32[4,8,896]{2,1,0:T(8,128)S(1)} %get-tuple-element.24.part_ref, ...), custom_call_target="tpu_custom_call" | custom-call | flops 940000000 | bytes 4000000 | tf_op jit(solution)/shard_map/forward/pallas_call | solution.py:208
  40.3 8.1 %all-to-all-start.1 = ((f32[64,4,128]{2,1,0:T(4,128)}), f32[64,4,128]{2,1,0:T(4,128)S(1)}, u32[]{:S(2)}, u32[]{:S(2)}) async-start(f32[64,4,128]{2,1,0:T(4,128)} %get-tuple-element.27), calls=%async_computation.1 | async-start | bytes 262144 | tf_op jit(solution)/shard_map/all_to_all | solution.py:379
  48.7 7.6 %backward.1 = bf16[8,528,128]{2,1,0:T(8,128)(2,1)} custom-call(s32[2]{0:T(128)S(1)} %copy-done.4, s32[512]{0:T(512)S(1)} %copy-done.3, s32[1]{0:T(128)} %bitcast.2.place_ref, bf16[4,896,128]{2,1,0:T(8,128)(2,1)} %copy-done.5, bf16[4,896,128]{2,1,0:T(8,128)(2,1)} %get-tuple-element.23.r_ref, f32[4,8,896]{2,1,0:T(8,128)S(1)} %get-tuple-element.26.stats_ref, ...), custom_call_target="tpu_custom_call" | custom-call | flops 1880000000 | bytes 4000000 | tf_op jit(solution)/shard_map/backward/pallas_call | solution.py:208
  56.3 4.3 %all-to-all-done.1 = f32[64,4,128]{2,1,0:T(4,128)S(1)} async-done(((f32[64,4,128]{2,1,0:T(4,128)}), f32[64,4,128]{2,1,0:T(4,128)S(1)}, u32[]{:S(2)}, u32[]{:S(2)}) %all-to-all-start.1) | async-done | bytes 131104 | tf_op jit(solution)/shard_map/all_to_all | solution.py:379
  60.8 0.6 broadcast_dynamic-update-slice_fusion
  61.4 4.3 %all-to-all-start.2 = ((bf16[8,528,128]{2,1,0:T(8,128)(2,1)}), bf16[8,528,128]{2,1,0:T(8,128)(2,1)S(1)}, u32[]{:S(2)}, u32[]{:S(2)}) async-start(bf16[8,528,128]{2,1,0:T(8,128)(2,1)} %broadcast_dynamic-update-slice_fusion), calls=%async_computation.2 | async-start | bytes 2162688 | tf_op jit(solution)/shard_map/all_to_all | solution.py:379
  65.7 7.2 %finish.1 = (bf16[2,128,1792]{2,1,0:T(8,128)(2,1)}, bf16[2,128,512]{2,1,0:T(8,128)(2,1)S(1)}, f32[8,128]{1,0:T(8,128)S(1)}) custom-call(s32[2]{0:T(128)S(1)} %copy-done.4, s32[512]{0:T(512)S(1)} %copy-done.3, bf16[4,896,128]{2,1,0:T(8,128)(2,1)} %copy-done.5, bf16[4,896,128]{2,1,0:T(8,128)(2,1)} %get-tuple-element.23.r_ref, ...), custom_call_target="tpu_custom_call" | custom-call | flops 2000000000 | bytes 4000000 | tf_op jit(solution)/shard_map/finish/pallas_call | solution.py:208
  72.9 8.4 %all-to-all-done.2.load_ref = bf16[8,528,128]{2,1,0:T(8,128)(2,1)S(1)} async-done(((bf16[8,528,128]{2,1,0:T(8,128)(2,1)}), bf16[8,528,128]{2,1,0:T(8,128)(2,1)S(1)}, u32[]{:S(2)}, u32[]{:S(2)}) %all-to-all-start.2) | async-done | bytes 1081376 | tf_op jit(solution)/shard_map/all_to_all | solution.py:379
  81.4 1.2 %weigh.1 = (f32[4,128]{1,0:T(4,128)}, f32[4,128]{1,0:T(4,128)S(1)}, bf16[8,8,8,128]{3,2,1,0:T(8,128)(2,1)}) custom-call(f32[4,128]{1,0:T(4,128)S(1)} %bitcast.15, s32[4,128]{1,0:T(4,128)S(1)} %bitcast.16, bf16[8,528,128]{2,1,0:T(8,128)(2,1)S(1)} %all-to-all-done.2.load_ref, f32[8,128]{1,0:T(8,128)S(1)} %get-tuple-element.28.done_ref), custom_call_target="tpu_custom_call" | custom-call | tf_op jit(solution)/shard_map/weigh/pallas_call | solution.py:344
  82.8 8.4 %all-to-all-start.3 = ((bf16[64,8,128]{2,1,0:T(8,128)(2,1)}), bf16[64,8,128]{2,1,0:T(8,128)(2,1)S(1)}, u32[]{:S(2)}, u32[]{:S(2)}) async-start(bf16[64,8,128]{2,1,0:T(8,128)(2,1)} %bitcast.7), calls=%async_computation.3 | async-start | bytes 262144 | tf_op jit(solution)/shard_map/all_to_all | solution.py:379
  91.2 1.1 multiply_convert_fusion
  92.3 11.0 %all-to-all-done.3.parts_ref = bf16[64,8,128]{2,1,0:T(8,128)(2,1)S(1)} async-done(((bf16[64,8,128]{2,1,0:T(8,128)(2,1)}), bf16[64,8,128]{2,1,0:T(8,128)(2,1)S(1)}, u32[]{:S(2)}, u32[]{:S(2)}) %all-to-all-start.3) | async-done | bytes 131104 | tf_op jit(solution)/shard_map/all_to_all | solution.py:379
  103.4 0.7 join.1
  104.1 4.7 %all-to-all-start.4 = ((bf16[32,8,128]{2,1,0:T(8,128)(2,1)}), bf16[32,8,128]{2,1,0:T(8,128)(2,1)S(1)}, u32[]{:S(2)}, u32[]{:S(2)}) async-start(bf16[32,8,128]{2,1,0:T(8,128)(2,1)} %join.1), calls=%async_computation.4 | async-start | bytes 131072 | tf_op jit(solution)/shard_map/all_to_all | solution.py:379
  108.8 0.8 multiply_convert_fusion.1
  109.6 8.3 %all-to-all-done.4 = bf16[32,8,128]{2,1,0:T(8,128)(2,1)S(1)} async-done(((bf16[32,8,128]{2,1,0:T(8,128)(2,1)}), bf16[32,8,128]{2,1,0:T(8,128)(2,1)S(1)}, u32[]{:S(2)}, u32[]{:S(2)}) %all-to-all-start.4) | async-done | bytes 65568 | tf_op jit(solution)/shard_map/all_to_all | solution.py:379
  117.8 0.6 copy.16
  (23 shorter events, 0.7 us)
Async XLA Ops:
  0.6 12.1 %copy-start.4 = (s32[2]{0:T(128)S(1)}, s32[2]{0:T(128)}, u32[]{:S(2)}) copy-start(s32[2]{0:T(128)} %response_ref.7) | copy-start | bytes 28
  0.6 12.1 %copy-start.1 = (s32[1024]{0:T(1024)S(1)}, s32[1024]{0:T(1024)}, u32[]{:S(2)}) copy-start(s32[1024]{0:T(1024)} %lengths_ref.1) | copy-start | bytes 12292
  0.7 12.1 %copy-start = (bf16[2,128,512]{2,1,0:T(8,128)(2,1)S(1)}, bf16[2,128,512]{2,1,0:T(8,128)(2,1)}, u32[]{:S(2)}) copy-start(bf16[2,128,512]{2,1,0:T(8,128)(2,1)} %own_ref.3) | copy-start | bytes 786436
  2.4 27.8 %all-to-all-start = ((bf16[8,2,32,512]{3,2,1,0:T(8,128)(2,1)}), bf16[8,2,32,512]{3,2,1,0:T(8,128)(2,1)S(1)}, u32[]{:S(2)}, u32[]{:S(2)}) async-start(bf16[8,2,32,512]{3,2,1,0:T(8,128)(2,1)} %repeat.1), calls=%async_computation | async-start | bytes 1048576 | tf_op jit(solution)/shard_map/all_to_all | solution.py:379
  12.8 21.3 %copy-start.3 = (s32[512]{0:T(512)S(1)}, s32[512]{0:T(512)}, u32[]{:S(2)}) copy-start(s32[512]{0:T(512)} %pair_prompt_ref.5) | copy-start | bytes 6148
  17.3 0.9 copy-start.5
  30.3 3.8 %collective-permute-start = (bf16[8,2,32,512]{3,2,1,0:T(8,128)(2,1)S(1)}, bf16[8,2,32,512]{3,2,1,0:T(8,128)(2,1)S(1)}, u32[]{:S(2)}, u32[]{:S(2)}) collective-permute-start(bf16[8,2,32,512]{3,2,1,0:T(8,128)(2,1)S(1)} %all-to-all-done.near_ref), channel_id=1, source_target_pairs={{0,32},{32,0},{1,33},{33,1},{2,34},{34,2},{3,35},{35,3},{4,36},{36... | collective-permute-start | bytes 1572872 | tf_op jit(solution)/shard_map/ppermute | solution.py:414
  40.3 20.3 %all-to-all-start.1 = ((f32[64,4,128]{2,1,0:T(4,128)}), f32[64,4,128]{2,1,0:T(4,128)S(1)}, u32[]{:S(2)}, u32[]{:S(2)}) async-start(f32[64,4,128]{2,1,0:T(4,128)} %get-tuple-element.27), calls=%async_computation.1 | async-start | bytes 262144 | tf_op jit(solution)/shard_map/all_to_all | solution.py:379
  61.4 20.0 %all-to-all-start.2 = ((bf16[8,528,128]{2,1,0:T(8,128)(2,1)}), bf16[8,528,128]{2,1,0:T(8,128)(2,1)S(1)}, u32[]{:S(2)}, u32[]{:S(2)}) async-start(bf16[8,528,128]{2,1,0:T(8,128)(2,1)} %broadcast_dynamic-update-slice_fusion), calls=%async_computation.2 | async-start | bytes 2162688 | tf_op jit(solution)/shard_map/all_to_all | solution.py:379
  65.7 15.7 %copy-start.2 = (f32[512]{0:T(512)S(1)}, f32[512]{0:T(512)}, u32[]{:S(2)}) copy-start(f32[512]{0:T(512)} %param.15) | copy-start | bytes 6148
  72.9 18.3 %copy-start.6 = (bf16[2,128,1792]{2,1,0:T(8,128)(2,1)S(1)}, bf16[2,128,1792]{2,1,0:T(8,128)(2,1)}, u32[]{:S(2)}) copy-start(bf16[2,128,1792]{2,1,0:T(8,128)(2,1)} %get-tuple-element.31) | copy-start | bytes 2752516
  82.8 20.6 %all-to-all-start.3 = ((bf16[64,8,128]{2,1,0:T(8,128)(2,1)}), bf16[64,8,128]{2,1,0:T(8,128)(2,1)S(1)}, u32[]{:S(2)}, u32[]{:S(2)}) async-start(bf16[64,8,128]{2,1,0:T(8,128)(2,1)} %bitcast.7), calls=%async_computation.3 | async-start | bytes 262144 | tf_op jit(solution)/shard_map/all_to_all | solution.py:379
  104.1 13.8 %all-to-all-start.4 = ((bf16[32,8,128]{2,1,0:T(8,128)(2,1)}), bf16[32,8,128]{2,1,0:T(8,128)(2,1)S(1)}, u32[]{:S(2)}, u32[]{:S(2)}) async-start(bf16[32,8,128]{2,1,0:T(8,128)(2,1)} %join.1), calls=%async_computation.4 | async-start | bytes 131072 | tf_op jit(solution)/shard_map/all_to_all | solution.py:379
